TPU v7x, 32 devices: a whole 2x2x4 slice. The times are simulated.
32 devices in a mesh: grp: 4 (over x, core), leaf: 8 (over z, y).
Axes of the slice: x: 2, y: 2, z: 4, core: 2. Of those that a mesh axis runs over, the one named last changes fastest.
Arguments:
- matrix: bfloat16 [8192, 8192], P('grp', 'leaf'), may hold values from -0.09375 to 0.09375
- probes: bfloat16 [8192, 512], P('leaf'), may hold values from -6 to 6
- leaf_skeleton: int32 [32, 128], P(('grp', 'leaf')), may hold values from 0 to 255, as said below
- node_skeleton: int32 [31, 128], replicated, may hold values from 0 to 255, as said below
Outputs:
- leaf_basis: float32 [8192, 128], P(('grp', 'leaf'))
- transfer: float32 [32, 256, 128], P(('grp', 'leaf'))
Inputs may be any that keep to these rules, and one draw needn't show every extreme that they name: `leaf_skeleton`: each row holds 128 distinct increasing row numbers within one leaf. `node_skeleton`: each row holds 128 distinct increasing numbers into the node's stacked rows, the first child's 128 rows first.
All inputs are finite; a program needn't handle non-finite values.
Results may differ from a plain program's by a relative error of at most 0.0003.
Values sent between devices are 32-bit elements; how exact they have to be, the bound alone decides.
No kernel may reach another device: no remote copies, remote signals or barrier semaphores. Data moves between devices by JAX's collectives and lax.ppermute only.
A program may use at most 128 MiB of HBM per device.

v0:
```python
import jax
import jax.numpy as jnp
from jax import lax
from jax.sharding import PartitionSpec as P


def from_partner(value, axis, stride):
    mask = 2**stride
    pairs = [(source, source ^ mask) for source in range(lax.axis_size(axis))]
    return lax.ppermute(value, axis, pairs)


def node_bases(stacked, picked):
    rows = jnp.take_along_axis(stacked, picked[:, :, None], axis=1)
    gram = jnp.einsum("nks,nls->nkl", rows, rows, precision=lax.Precision.HIGHEST)
    cross = jnp.einsum("nks,nis->nki", rows, stacked, precision=lax.Precision.HIGHEST)
    factor = jnp.linalg.cholesky(gram)
    first = lax.linalg.triangular_solve(factor, cross, left_side=True, lower=True)
    solved = lax.linalg.triangular_solve(
        factor, first, left_side=True, lower=True, transpose_a=True
    )
    return (jnp.swapaxes(solved, 1, 2), rows)


def on_device(matrix, probes, leaf_skeleton, node_skeleton):
    n_grp = lax.axis_size("grp")
    n_leaf = lax.axis_size("leaf")
    grp_pos = lax.axis_index("grp")
    leaf_pos = lax.axis_index("leaf")
    device = grp_pos * n_leaf + leaf_pos
    row_count, col_count = matrix.shape
    leaf_rows = row_count // n_leaf
    rank = leaf_skeleton.shape[1]
    all_leaves = n_grp * n_leaf
    leaf_bits = n_leaf.bit_length() - 1
    grp_bits = n_grp.bit_length() - 1
    levels = leaf_bits + grp_bits
    row_base = grp_pos * row_count
    col_leaf = (leaf_pos * col_count + jnp.arange(col_count, dtype=jnp.int32)) // leaf_rows
    row_index = jnp.arange(leaf_rows * lax.axis_size("leaf"), dtype=jnp.int32)
    block = jnp.take(matrix, row_index, axis=0)
    keep = ((row_base + row_index) // leaf_rows)[:, None] != col_leaf[None, :]
    block = jnp.where(keep, block, jnp.zeros((), matrix.dtype))
    samples_mine = lax.psum_scatter(
        jnp.dot(block, probes, preferred_element_type=jnp.float32),
        "leaf",
        scatter_dimension=0,
        tiled=True,
    )
    leaf_basis, carried = node_bases(samples_mine[None], leaf_skeleton)
    current = carried[0]
    result = jnp.zeros((2 * rank, rank), jnp.float32)

    def level_offset(level):
        total = 0
        for inner in range(1, level):
            total = total + (all_leaves >> inner)
        return total

    def keep_mine(result, level, basis):
        select = (device % (1 << level) == 1 << level - 1) | (device == 0) & (level == levels)
        return jnp.where(select, basis, result)

    def climb(current, partner, bit_value, level):
        lower = jnp.where(bit_value == 1, partner, current)
        upper = jnp.where(bit_value == 1, current, partner)
        stacked = jnp.concatenate([lower, upper], axis=0)[None]
        node = level_offset(level) + (device >> level)
        picked = lax.dynamic_slice_in_dim(node_skeleton, node, 1, 0)
        basis, rows = node_bases(stacked, picked)
        return (basis[0], rows[0])

    for bit in range(leaf_bits):
        partner = from_partner(current, "leaf", bit)
        basis, current = climb(current, partner, leaf_pos >> bit & 1, bit + 1)
        result = keep_mine(result, bit + 1, basis)
    for bit in range(grp_bits):
        partner = from_partner(current, "grp", bit)
        basis, current = climb(current, partner, grp_pos >> bit & 1, leaf_bits + bit + 1)
        result = keep_mine(result, leaf_bits + bit + 1, basis)
    return (leaf_basis[0], result[None])


def solution(mesh):
    return jax.shard_map(
        on_device,
        mesh=mesh,
        in_specs=(P("grp", "leaf"), P("leaf", None), P(("grp", "leaf"), None), P()),
        out_specs=(P(("grp", "leaf"), None), P(("grp", "leaf"), None, None)),
        check_vma=False,
    )
```

profile of v0, /device:TPU:0, one launch (start us, length us, event | category | flops | bytes accessed | tf_op | source)
XLA Modules:
  0.0 288.1 jit_solution(1435291202613817929)
XLA Ops:
  7.3 13.8 %gather_fusion = bf16[2048,1024]{1,0:T(8,128)(2,1)} fusion(bf16[2048,1024]{1,0:T(8,128)(2,1)} %param.11, s32[2048]{0:T(1024)S(1)} %iota_clamp_fusion), kind=kCustom, calls=%fused_computation.6 | custom fusion | bytes 8396800 | tf_op jit(solution)/shard_map/jit(_take)/gather | solution.py:41
  21.1 5.7 %fusion = f32[2048,512]{1,0:T(8,128)} fusion(bf16[1024,512]{1,0:T(8,128)(2,1)S(1)} %copy-done, bf16[2048,1024]{1,0:T(8,128)(2,1)} %gather_fusion, s32[1024]{0:T(1024)S(1)} %add_select_fusion.1, s32[2048]{0:T(1024)S(1)} %add_select_fusion, pred[2048]{0:T(1024)(128)(4,1)S(1)} %iota_compare_fusion.2), kind=kOutput, calls=%fused_computation.8 | convolution fusion | flops 2153775104 | bytes 9451520 | tf_op jit(solution)/shard_map/dot_general | solution.py:45
  26.9 0.8 fusion.76
  27.7 0.8 and_bitcast_fusion
  28.6 89.4 %reduce-scatter.2.cloned.1.call-done = f32[256,512]{1,0:T(8,128)} async-done(((f32[2048,512]{1,0:T(8,128)}), f32[256,512]{1,0:T(8,128)}) %reduce-scatter.2.cloned.1.call-update) | async-done | bytes 524304 | tf_op jit(solution)/shard_map/reduce_scatter | solution.py:44
  118.0 2.0 gather_fusion.1
  120.4 1.5 collective-permute-start
  122.1 11.7 %custom-call.24 = f32[1,128,128]{2,1,0:T(8,128)S(1)} custom-call(f32[1,128,128]{2,1,0:T(8,128)S(1)} %fusion.37), custom_call_target="Cholesky" | custom-call | tf_op jit(solution)/shard_map/jit(cholesky)/cholesky | solution.py:17
  135.1 9.8 %custom-call.26 = f32[1,1,128,128]{2,3,1,0:T(8,128)S(1)} custom-call(f32[1,1,128,128]{3,2,1,0:T(8,128)S(1)} %fusion.26), custom_call_target="InvertDiagBlocksLowerTriangular" | custom-call | tf_op jit(solution)/shard_map/triangular_solve/custom-call.2 | solution.py:19
  146.2 0.8 copy.18
  147.1 0.8 gather_fusion.2
  148.0 0.7 fusion.80
  149.0 1.8 collective-permute-start.1
  150.9 11.9 %custom-call.39 = f32[1,128,128]{2,1,0:T(8,128)S(1)} custom-call(f32[1,128,128]{2,1,0:T(8,128)S(1)} %fusion.32), custom_call_target="Cholesky" | custom-call | tf_op jit(solution)/shard_map/jit(cholesky)/cholesky | solution.py:17
  164.2 9.8 %custom-call.41 = f32[1,1,128,128]{2,3,1,0:T(8,128)S(1)} custom-call(f32[1,1,128,128]{3,2,1,0:T(8,128)S(1)} %fusion.31), custom_call_target="InvertDiagBlocksLowerTriangular" | custom-call | tf_op jit(solution)/shard_map/triangular_solve/custom-call.2 | solution.py:19
  174.7 0.8 gather_fusion.3
  176.7 1.0 collective-permute-start.2
  177.7 11.7 %custom-call.36 = f32[1,128,128]{2,1,0:T(8,128)S(1)} custom-call(f32[1,128,128]{2,1,0:T(8,128)S(1)} %fusion.33), custom_call_target="Cholesky" | custom-call | tf_op jit(solution)/shard_map/jit(cholesky)/cholesky | solution.py:17
  190.8 9.8 %custom-call.38 = f32[1,1,128,128]{2,3,1,0:T(8,128)S(1)} custom-call(f32[1,1,128,128]{3,2,1,0:T(8,128)S(1)} %fusion.30), custom_call_target="InvertDiagBlocksLowerTriangular" | custom-call | tf_op jit(solution)/shard_map/triangular_solve/custom-call.2 | solution.py:19
  201.4 0.8 gather_fusion.4
  202.2 1.1 fusion.78
  203.9 11.7 %custom-call.33 = f32[1,128,128]{2,1,0:T(8,128)S(1)} custom-call(f32[1,128,128]{2,1,0:T(8,128)S(1)} %fusion.34), custom_call_target="Cholesky" | custom-call | tf_op jit(solution)/shard_map/jit(cholesky)/cholesky | solution.py:17
  216.9 9.8 %custom-call.35 = f32[1,1,128,128]{2,3,1,0:T(8,128)S(1)} custom-call(f32[1,1,128,128]{3,2,1,0:T(8,128)S(1)} %fusion.29), custom_call_target="InvertDiagBlocksLowerTriangular" | custom-call | tf_op jit(solution)/shard_map/triangular_solve/custom-call.2 | solution.py:19
  227.5 0.8 gather_fusion.5
  228.3 0.7 fusion.77
  229.4 1.5 collective-permute-start.4
  231.0 11.9 %custom-call.30 = f32[1,128,128]{2,1,0:T(8,128)S(1)} custom-call(f32[1,128,128]{2,1,0:T(8,128)S(1)} %fusion.35), custom_call_target="Cholesky" | custom-call | tf_op jit(solution)/shard_map/jit(cholesky)/cholesky | solution.py:17
  244.2 9.8 %custom-call.32 = f32[1,1,128,128]{2,3,1,0:T(8,128)S(1)} custom-call(f32[1,1,128,128]{3,2,1,0:T(8,128)S(1)} %fusion.28), custom_call_target="InvertDiagBlocksLowerTriangular" | custom-call | tf_op jit(solution)/shard_map/triangular_solve/custom-call.2 | solution.py:19
  254.8 0.8 gather_fusion.6
  256.8 11.7 %custom-call.27 = f32[1,128,128]{2,1,0:T(8,128)S(1)} custom-call(f32[1,128,128]{2,1,0:T(8,128)S(1)} %fusion.36), custom_call_target="Cholesky" | custom-call | tf_op jit(solution)/shard_map/jit(cholesky)/cholesky | solution.py:17
  269.9 9.8 %custom-call.29 = f32[1,1,128,128]{2,3,1,0:T(8,128)S(1)} custom-call(f32[1,1,128,128]{3,2,1,0:T(8,128)S(1)} %fusion.27), custom_call_target="InvertDiagBlocksLowerTriangular" | custom-call | tf_op jit(solution)/shard_map/triangular_solve/custom-call.2 | solution.py:19
  280.3 0.8 copy.19
  (90 shorter events, 17.7 us)
Async XLA Ops:
  7.2 13.9 %copy-start = (bf16[1024,512]{1,0:T(8,128)(2,1)S(1)}, bf16[1024,512]{1,0:T(8,128)(2,1)}, u32[]{:S(2)}) copy-start(bf16[1024,512]{1,0:T(8,128)(2,1)} %param.12) | copy-start | bytes 3145732
  7.2 110.8 %reduce-scatter.2.cloned.1.call-start = ((), (), s32[]{:S(2)}) async-start(), calls=%async_computation.1 | async-start | bytes 4718592 | tf_op jit(solution)/shard_map/reduce_scatter | solution.py:44
  26.7 1.8 copy-start.2
  118.0 27.0 %copy-start.1 = (f32[256,512]{1,0:T(8,128)S(1)}, f32[256,512]{1,0:T(8,128)}, u32[]{:S(2)}) copy-start(f32[256,512]{1,0:T(8,128)} %reduce-scatter.2.cloned.1.call-done) | copy-start | bytes 1572868
  120.4 26.6 %collective-permute-start = (f32[128,512]{1,0:T(8,128)S(1)}, f32[128,512]{1,0:T(8,128)S(1)}, u32[]{:S(2)}, u32[]{:S(2)}) collective-permute-start(f32[128,512]{1,0:T(8,128)S(1)} %fusion.21), channel_id=1, source_target_pairs={{0,1},{1,0},{2,3},{3,2},{4,5},{5,4},{6,7},{7,6},{8,9},{9,8},{10,11... | collective-permute-start | bytes 786440 | tf_op jit(solution)/shard_map/ppermute | solution.py:10
  149.0 25.5 %collective-permute-start.1 = (f32[128,512]{1,0:T(8,128)S(1)}, f32[128,512]{1,0:T(8,128)S(1)}, u32[]{:S(2)}, u32[]{:S(2)}) collective-permute-start(f32[128,512]{1,0:T(8,128)S(1)} %fusion.20), channel_id=1, source_target_pairs={{0,2},{1,3},{2,0},{3,1},{4,6},{5,7},{6,4},{7,5},{8,10},{9,11},{10,... | collective-permute-start | bytes 786440 | tf_op jit(solution)/shard_map/ppermute | solution.py:10
  176.7 24.5 %collective-permute-start.2 = (f32[128,512]{1,0:T(8,128)S(1)}, f32[128,512]{1,0:T(8,128)S(1)}, u32[]{:S(2)}, u32[]{:S(2)}) collective-permute-start(f32[128,512]{1,0:T(8,128)S(1)} %fusion.19), channel_id=1, source_target_pairs={{0,4},{1,5},{2,6},{3,7},{4,0},{5,1},{6,2},{7,3},{8,12},{9,13},{10,... | collective-permute-start | bytes 786440 | tf_op jit(solution)/shard_map/ppermute | solution.py:10
  203.7 23.7 %collective-permute-start.3 = (f32[128,512]{1,0:T(8,128)S(1)}, f32[128,512]{1,0:T(8,128)S(1)}, u32[]{:S(2)}, u32[]{:S(2)}) collective-permute-start(f32[128,512]{1,0:T(8,128)S(1)} %fusion.18), channel_id=1, source_target_pairs={{0,8},{8,0},{16,24},{24,16},{1,9},{9,1},{17,25},{25,17},{2,10},{10... | collective-permute-start | bytes 786440 | tf_op jit(solution)/shard_map/ppermute | solution.py:10
  229.4 25.3 %collective-permute-start.4 = (f32[128,512]{1,0:T(8,128)S(1)}, f32[128,512]{1,0:T(8,128)S(1)}, u32[]{:S(2)}, u32[]{:S(2)}) collective-permute-start(f32[128,512]{1,0:T(8,128)S(1)} %fusion.17), channel_id=1, source_target_pairs={{0,16},{8,24},{16,0},{24,8},{1,17},{9,25},{17,1},{25,9},{2,18},{10... | collective-permute-start | bytes 786440 | tf_op jit(solution)/shard_map/ppermute | solution.py:10
Sparse Core Ops, SparseCore 0:
  26.9 91.0 reduce-scatter.1
where the time goes:
time: 291 us; the launch traced here: 288 us
  other arithmetic  140 us (48%)
  waiting for transfers between devices  89.4 us (31%)
  local copies, waits for them, and re-layouts  21.6 us (7%)
  matrix products  15.8 us (5%)
  between operations  15 us (5%)
  starting transfers between devices  5.93 us (2%)
    reduce_scatter x1, waiting for transfers between devices, on_device(): lax.psum_scatter(jnp.dot(block, probes, preferred_element_type=jnp.float3...  89.4 us
    another operation x18, other arithmetic, node_bases(): factor = jnp.linalg.cholesky(gram)  74.7 us
    another operation x12, other arithmetic, node_bases(): lax.linalg.triangular_solve(factor, first, left_side=True, lower=True, tr...  62.8 us
    gather x1, local copies, waits for them, and re-layouts, on_device(): block = jnp.take(matrix, row_index, axis=0)  13.8 us
    ppermute x5, starting transfers between devices, from_partner(): return lax.ppermute(value, axis, pairs)  5.89 us
  transfers between devices with their start and end apart: 6, of which 1 were waited for; matrix products, arithmetic and copies ran while one was open for 42% of the time, Pallas kernels for 0%

commit v1 on v0

v1 whole, which is shorter than its diff:
```python
import jax
import jax.numpy as jnp
from jax import lax
from jax.experimental import pallas as pl
from jax.experimental.pallas import tpu as pltpu
from jax.sharding import PartitionSpec as P

HIGHEST = lax.Precision.HIGHEST


def bits_of(count):
    return count.bit_length() - 1


def spd_inverse(a):
    n = a.shape[0]
    rows = lax.broadcasted_iota(jnp.int32, (n, n), 0)
    cols = lax.broadcasted_iota(jnp.int32, (n, n), 1)
    lane = cols[:1]
    for k in range(0, n, 2):
        r0 = a[k : k + 1, :]
        r1 = a[k + 1 : k + 2, :]
        c0 = jnp.broadcast_to(a[:, k : k + 1], (n, n))
        c1 = jnp.broadcast_to(a[:, k + 1 : k + 2], (n, n))
        p = jnp.broadcast_to(a[k : k + 1, k : k + 1], (1, n))
        q = jnp.broadcast_to(a[k : k + 1, k + 1 : k + 2], (1, n))
        s = jnp.broadcast_to(a[k + 1 : k + 2, k + 1 : k + 2], (1, n))
        inv = 1.0 / (p * s - q * q)
        ip, iq, js = s * inv, -q * inv, p * inv
        w0 = ip * r0 + iq * r1
        w1 = iq * r0 + js * r1
        upd = a - c0 * jnp.broadcast_to(w0, (n, n)) - c1 * jnp.broadcast_to(w1, (n, n))
        k0 = -(c0 * ip + c1 * iq)
        k1 = -(c0 * iq + c1 * js)
        upd = jnp.where(cols == k, k0, jnp.where(cols == k + 1, k1, upd))
        x0 = jnp.where(lane == k, ip, jnp.where(lane == k + 1, iq, w0))
        x1 = jnp.where(lane == k, iq, jnp.where(lane == k + 1, js, w1))
        upd = jnp.where(rows == k + 1, jnp.broadcast_to(x1, (n, n)), upd)
        a = jnp.where(rows == k, jnp.broadcast_to(x0, (n, n)), upd)
    return a


def basis_kernel(own_ref, received_ref, picked_ref, basis_ref):
    cross = own_ref[...] + received_ref[...]
    index = lax.broadcasted_iota(jnp.int32, cross.shape, 0)
    choice = (index == picked_ref[...]).astype(jnp.float32)
    gram = lax.dot_general(
        choice,
        cross,
        (((0,), (0,)), ((), ())),
        precision=HIGHEST,
        preferred_element_type=jnp.float32,
    )
    basis_ref[...] = jnp.dot(
        cross, spd_inverse(gram), precision=HIGHEST, preferred_element_type=jnp.float32
    )


def basis_of(own, received, picked):
    return pl.pallas_call(
        basis_kernel,
        out_shape=jax.ShapeDtypeStruct(own.shape, jnp.float32),
        name="basis",
    )(own, received, picked[None])


def product_kernel(n_leaf, n_grp, place_ref, matrix_ref, probes_ref, send_ref, keep_ref):
    step = pl.program_id(0)
    leaf = place_ref[1] * n_leaf + 2 * place_ref[0] + step
    hit = leaf - place_ref[2] * n_grp
    side = place_ref[2] & 1
    rows = matrix_ref.shape[0]
    half = send_ref.shape[1]
    pieces = []
    for c in range(n_grp):
        piece = matrix_ref[:, c * rows : (c + 1) * rows]
        pieces.append(jnp.where(hit == c, jnp.zeros_like(piece), piece))
    block = jnp.concatenate(pieces, axis=1)
    away = pl.multiple_of((1 - side) * half, half)
    home = pl.multiple_of(side * half, half)
    send_ref[...] = jnp.dot(
        block, probes_ref[:, pl.ds(away, half)], preferred_element_type=jnp.float32
    )
    keep_ref[...] = jnp.dot(
        block, probes_ref[:, pl.ds(home, half)], preferred_element_type=jnp.float32
    )


def on_device(matrix, probes, leaf_skeleton, node_skeleton):
    n_grp = lax.axis_size("grp")
    n_leaf = lax.axis_size("leaf")
    grp_pos = lax.axis_index("grp")
    leaf_pos = lax.axis_index("leaf")
    device = grp_pos * n_leaf + leaf_pos
    side = leaf_pos & 1
    spot = leaf_pos >> 1
    spots = n_leaf // 2
    row_count, col_count = matrix.shape
    leaf_rows = row_count // n_leaf
    half = probes.shape[1] // 2
    rank = leaf_skeleton.shape[1]
    all_leaves = n_grp * n_leaf
    leaf_bits, grp_bits = bits_of(n_leaf), bits_of(n_grp)
    levels = leaf_bits + grp_bits

    def across(value, where=range(spots)):
        pairs = [(2 * z + s, 2 * z + 1 - s) for z in where for s in range(2)]
        return lax.ppermute(value, "leaf", pairs)

    def along(value, hops):
        pairs = [(2 * a + s, 2 * b + s) for a, b in hops for s in range(2)]
        return lax.ppermute(value, "leaf", pairs)

    def product(target):
        place = jnp.stack([target, grp_pos, leaf_pos]).astype(jnp.int32)
        out = jax.ShapeDtypeStruct((2 * leaf_rows, half), jnp.float32)
        return pl.pallas_call(
            lambda *refs: product_kernel(n_leaf, n_grp, *refs),
            out_shape=(out, out),
            grid_spec=pltpu.PrefetchScalarGridSpec(
                num_scalar_prefetch=1,
                grid=(2,),
                in_specs=[
                    pl.BlockSpec((leaf_rows, col_count), lambda i, at: (2 * at[0] + i, 0)),
                    pl.BlockSpec(probes.shape, lambda i, at: (0, 0)),
                ],
                out_specs=[
                    pl.BlockSpec((leaf_rows, half), lambda i, at: (i, 0)),
                    pl.BlockSpec((leaf_rows, half), lambda i, at: (i, 0)),
                ],
            ),
            name="product",
        )(place, matrix, probes)

    other_leaf = across(leaf_skeleton)

    def summed(target, where):
        send, keep = product(jnp.clip(target, 0, spots - 1))
        return keep + across(send, where)

    up = down = None
    for step in range(1, spots):
        ups = range(0, step)
        downs = range(spots - step, spots)
        up_target = spots - step + spot
        down_target = step - spots + spot
        if step <= spots // 2:
            mine = summed(
                jnp.where(spot < step, up_target, down_target), sorted({*ups, *downs})
            )
            mine_up = mine_down = mine
        else:
            mine_up = summed(up_target, ups)
            mine_down = summed(down_target, downs)
        if up is not None:
            mine_up = mine_up + up
            mine_down = mine_down + down
        up = along(mine_up, [(z, z + 1) for z in ups])
        down = along(mine_down, [(z, z - 1) for z in downs])
    samples = summed(spot, range(spots))
    if up is not None:
        samples = samples + up + down

    def cross_of(stacked, rows):
        return lax.dot_general(
            stacked, rows, (((1,), (1,)), ((), ())), precision=HIGHEST
        )

    first = jnp.where(side == 0, leaf_skeleton[0], other_leaf[0])
    second = jnp.where(side == 0, other_leaf[0], leaf_skeleton[0])
    stacks = (samples[:leaf_rows], samples[leaf_rows:])
    rows = tuple(jnp.take(z, j, axis=0) for z, j in zip(stacks, (first, second)))
    crosses = tuple(cross_of(z, r) for z, r in zip(stacks, rows))
    own = jnp.where(side == 0, crosses[0], crosses[1])
    received = across(jnp.where(side == 0, crosses[1], crosses[0]))
    leaf_basis = basis_of(own, received, leaf_skeleton[0])

    def level_offset(level):
        return sum(all_leaves >> inner for inner in range(1, level))

    def picked_of(level):
        node = level_offset(level) + (device >> level)
        return lax.dynamic_slice_in_dim(node_skeleton, node, 1, 0)[0]

    low_stack = jnp.concatenate(rows, axis=0)
    low_picked = picked_of(1)
    current = low_rows = jnp.take(low_stack, low_picked, axis=0)
    low_cross = cross_of(low_stack, low_rows)
    high_stack, high_picked, high_rows = low_stack, low_picked, low_rows
    even = device - side
    for level in range(2, levels + 1):
        if level <= leaf_bits:
            bit = level - 2
            hops = [(z, z ^ 1 << bit) for z in range(0, spots, 1 << bit)]
            partner = along(current, hops)
            upper = spot >> bit & 1
        else:
            bit = level - leaf_bits - 1
            pairs = [
                (g * n_leaf + s, (g ^ 1 << bit) * n_leaf + s)
                for g in range(0, n_grp, 1 << bit)
                for s in range(2)
            ]
            partner = lax.ppermute(current, ("grp", "leaf"), pairs)
            upper = grp_pos >> bit & 1
        stacked = jnp.concatenate(
            [
                jnp.where(upper == 1, partner, current),
                jnp.where(upper == 1, current, partner),
            ],
            axis=0,
        )
        picked = picked_of(level)
        current = jnp.take(stacked, picked, axis=0)
        select = even % (1 << level) == 1 << level - 1
        if level == levels:
            select = select | (even == 0)
        high_stack = jnp.where(select, stacked, high_stack)
        high_rows = jnp.where(select, current, high_rows)
        high_picked = jnp.where(select, picked, high_picked)
    high_cross = cross_of(high_stack, high_rows)
    own = jnp.where(side == 1, low_cross, high_cross)
    received = across(jnp.where(side == 1, high_cross, low_cross))
    node_picked = jnp.where(side == 1, low_picked, high_picked)
    transfer = basis_of(own, received, node_picked)
    return (leaf_basis, transfer[None])


def solution(mesh):
    return jax.shard_map(
        on_device,
        mesh=mesh,
        in_specs=(P("grp", "leaf"), P("leaf", None), P(("grp", "leaf"), None), P()),
        out_specs=(P(("grp", "leaf"), None), P(("grp", "leaf"), None, None)),
        check_vma=False,
    )
```

time: 291 us -> 133 us (0.46)
  other arithmetic: 140 us -> 10.1 us
  waiting for transfers between devices: 89.4 us -> 30.9 us
  Pallas kernels: 0 us -> 38.5 us
  starting transfers between devices: 5.93 us -> 41.7 us
  local copies, waits for them, and re-layouts: 21.6 us -> 6.68 us
  between operations: 15 us -> 1.15 us
  matrix products: 15.8 us -> 2.91 us
    another operation x31 -> x3, other arithmetic: 138 us -> 1.9 us  [product(): place = jnp.stack([target, grp_pos, leaf_pos]).astype(jnp.int32)]
    reduce_scatter x1 -> x0, waiting for transfers between devices: 89.4 us -> none  [on_device(): lax.psum_scatter(jnp.dot(block, probes, preferred_element_type=jnp.float3...]
    pallas_call x0 -> x7, Pallas kernels: none -> 38.5 us  [the longest x2 19.5 us: basis_of(): pl.pallas_call(basis_kernel, out_shape=jax.ShapeDtypeStruct(own.shape, jn...]
    ppermute x5 -> x18, starting transfers between devices: 5.89 us -> 41.7 us  [the longest x8 21.5 us: along(): return lax.ppermute(value, 'leaf', pairs)]
    ppermute x5 -> x18, waiting for transfers between devices: 0.01 us -> 30.9 us  [the longest x8 18.1 us: along(): return lax.ppermute(value, 'leaf', pairs)]
    gather x7, local copies, waits for them, and re-layouts: 19.5 us -> 5.28 us  [the longest x4 3.02 us: on_device(): current = jnp.take(stacked, picked, axis=0)]
    dot_general x13 -> x4, matrix products: 12.4 us -> 2.91 us  [cross_of(): lax.dot_general(stacked, rows, (((1,), (1,)), ((), ())), precision=HIGHEST)]
    add x0 -> x5, other arithmetic: none -> 4.37 us  [the longest x2 2.87 us: on_device(): mine_up = mine_up + up]
  transfers between devices with their start and end apart: 6 -> 18, of which waited for: 1 -> 8; matrix products, arithmetic and copies ran while one was open for 42% -> 10% of each run, Pallas kernels for 0% -> 19%
where the time goes in v1:
time: 133 us; the launch traced here: 132 us
  starting transfers between devices  41.7 us (31%)
  Pallas kernels  38.5 us (29%)
  waiting for transfers between devices  30.9 us (23%)
  other arithmetic  10.1 us (8%)
  local copies, waits for them, and re-layouts  6.68 us (5%)
  matrix products  2.91 us (2%)
    ppermute x8, starting transfers between devices, along(): return lax.ppermute(value, 'leaf', pairs)  21.5 us
    pallas_call x2, Pallas kernels, basis_of(): pl.pallas_call(basis_kernel, out_shape=jax.ShapeDtypeStruct(own.shape, jn...  19.5 us
    pallas_call x5, Pallas kernels, product(): pl.pallas_call(lambda *refs: product_kernel(n_leaf, n_grp, *refs), out_sh...  19.1 us
    ppermute x8, waiting for transfers between devices, along(): return lax.ppermute(value, 'leaf', pairs)  18.1 us
    ppermute x8, starting transfers between devices, across(): return lax.ppermute(value, 'leaf', pairs)  14.7 us
    ppermute x8, waiting for transfers between devices, across(): return lax.ppermute(value, 'leaf', pairs)  9.82 us
    ppermute x2, starting transfers between devices, on_device(): partner = lax.ppermute(current, ('grp', 'leaf'), pairs)  5.48 us
    gather x4, local copies, waits for them, and re-layouts, on_device(): current = jnp.take(stacked, picked, axis=0)  3.02 us
  transfers between devices with their start and end apart: 18, of which 8 were waited for; matrix products, arithmetic and copies ran while one was open for 10% of the time, Pallas kernels for 19%

profile of v1, /device:TPU:0, one launch (start us, length us, event | category | flops | bytes accessed | tf_op | source)
XLA Modules:
  0.0 131.9 jit_solution(15361964800658302893)
XLA Ops:
  1.3 3.8 %product.8 = (f32[512,256]{1,0:T(8,128)}, f32[512,256]{1,0:T(8,128)}) custom-call(s32[3]{0:T(128)} %get-tuple-element.66.refs_0_, bf16[2048,1024]{1,0:T(8,128)(2,1)} %refs_1_.9, bf16[1024,512]{1,0:T(8,128)(2,1)} %refs_2_.9), custom_call_target="tpu_custom_call" | custom-call | tf_op jit(solution)/shard_map/product/pallas_call | solution.py:117
  5.1 5.0 %collective-permute-start.3 = (f32[512,256]{1,0:T(8,128)}, f32[512,256]{1,0:T(8,128)S(1)}, u32[]{:S(2)}, u32[]{:S(2)}) collective-permute-start(f32[512,256]{1,0:T(8,128)} %get-tuple-element.20), channel_id=1, source_target_pairs={{0,1},{1,0},{6,7},{7,6},{8,9},{9,8},{14,15},{15,14},{16,17},{17,16... | collective-permute-start | bytes 1572872 | tf_op jit(solution)/shard_map/ppermute | solution.py:108
  10.1 3.8 %product.7 = (f32[512,256]{1,0:T(8,128)}, f32[512,256]{1,0:T(8,128)}) custom-call(s32[3]{0:T(128)} %get-tuple-element.65.refs_0_, bf16[2048,1024]{1,0:T(8,128)(2,1)} %refs_1_.9, bf16[1024,512]{1,0:T(8,128)(2,1)} %refs_2_.9), custom_call_target="tpu_custom_call" | custom-call | tf_op jit(solution)/shard_map/product/pallas_call | solution.py:117
  13.9 9.2 %collective-permute-done.3 = f32[512,256]{1,0:T(8,128)S(1)} collective-permute-done((f32[512,256]{1,0:T(8,128)}, f32[512,256]{1,0:T(8,128)S(1)}, u32[]{:S(2)}, u32[]{:S(2)}) %collective-permute-start.3) | collective-permute-done | bytes 524320 | tf_op jit(solution)/shard_map/ppermute | solution.py:108
  23.2 1.3 %collective-permute-start.4 = (f32[512,256]{1,0:T(8,128)S(1)}, f32[512,256]{1,0:T(8,128)S(1)}, u32[]{:S(2)}, u32[]{:S(2)}) collective-permute-start(f32[512,256]{1,0:T(8,128)S(1)} %add.96), channel_id=1, source_target_pairs={{0,2},{1,3},{8,10},{9,11},{16,18},{17,19},{24,26},{25,27}} | collective-permute-start | bytes 1572872 | tf_op jit(solution)/shard_map/ppermute | solution.py:112
  25.9 3.8 %product.6 = (f32[512,256]{1,0:T(8,128)}, f32[512,256]{1,0:T(8,128)}) custom-call(s32[3]{0:T(128)} %get-tuple-element.64.refs_0_, bf16[2048,1024]{1,0:T(8,128)(2,1)} %refs_1_.9, bf16[1024,512]{1,0:T(8,128)(2,1)} %refs_2_.9), custom_call_target="tpu_custom_call" | custom-call | tf_op jit(solution)/shard_map/product/pallas_call | solution.py:117
  29.7 3.9 %collective-permute-start.1 = (f32[512,256]{1,0:T(8,128)}, f32[512,256]{1,0:T(8,128)S(1)}, u32[]{:S(2)}, u32[]{:S(2)}) collective-permute-start(f32[512,256]{1,0:T(8,128)} %get-tuple-element.16), channel_id=1, source_target_pairs={{0,1},{1,0},{2,3},{3,2},{4,5},{5,4},{8,9},{9,8},{10,11},{11,10},{1... | collective-permute-start | bytes 1572872 | tf_op jit(solution)/shard_map/ppermute | solution.py:108
  35.4 5.2 %collective-permute-start.5 = (f32[512,256]{1,0:T(8,128)}, f32[512,256]{1,0:T(8,128)}, u32[]{:S(2)}, u32[]{:S(2)}) collective-permute-start(f32[512,256]{1,0:T(8,128)} %get-tuple-element.37), channel_id=1, source_target_pairs={{0,2},{1,3},{2,4},{3,5},{8,10},{9,11},{10,12},{11,13},{16,18},{17,... | collective-permute-start | bytes 1572872 | tf_op jit(solution)/shard_map/ppermute | solution.py:112
  41.2 3.9 %product.9 = (f32[512,256]{1,0:T(8,128)}, f32[512,256]{1,0:T(8,128)}) custom-call(s32[3]{0:T(128)} %add_add_fusion.9.refs_0_, bf16[2048,1024]{1,0:T(8,128)(2,1)} %refs_1_.9, bf16[1024,512]{1,0:T(8,128)(2,1)} %refs_2_.9), custom_call_target="tpu_custom_call" | custom-call | tf_op jit(solution)/shard_map/product/pallas_call | solution.py:117
  45.1 1.6 %collective-permute-start.7 = (f32[512,256]{1,0:T(8,128)}, f32[512,256]{1,0:T(8,128)}, u32[]{:S(2)}, u32[]{:S(2)}) collective-permute-start(f32[512,256]{1,0:T(8,128)} %get-tuple-element.22), channel_id=1, source_target_pairs={{2,3},{3,2},{4,5},{5,4},{6,7},{7,6},{10,11},{11,10},{12,13},{13,12... | collective-permute-start | bytes 1572872 | tf_op jit(solution)/shard_map/ppermute | solution.py:108
  46.7 1.5 %collective-permute-start.9 = (f32[512,256]{1,0:T(8,128)S(1)}, f32[512,256]{1,0:T(8,128)}, u32[]{:S(2)}, u32[]{:S(2)}) collective-permute-start(f32[512,256]{1,0:T(8,128)S(1)} %get-tuple-element.38), channel_id=1, source_target_pairs={{4,2},{5,3},{6,4},{7,5},{12,10},{13,11},{14,12},{15,13},{20,18},{2... | collective-permute-start | bytes 1572872 | tf_op jit(solution)/shard_map/ppermute | solution.py:112
  48.2 3.8 %product.5 = (f32[512,256]{1,0:T(8,128)}, f32[512,256]{1,0:T(8,128)}) custom-call(s32[3]{0:T(128)} %get-tuple-element.63.refs_0_, bf16[2048,1024]{1,0:T(8,128)(2,1)} %refs_1_.9, bf16[1024,512]{1,0:T(8,128)(2,1)} %refs_2_.9), custom_call_target="tpu_custom_call" | custom-call | tf_op jit(solution)/shard_map/product/pallas_call | solution.py:117
  52.0 1.5 %collective-permute-start = (f32[512,256]{1,0:T(8,128)}, f32[512,256]{1,0:T(8,128)S(1)}, u32[]{:S(2)}, u32[]{:S(2)}) collective-permute-start(f32[512,256]{1,0:T(8,128)} %get-tuple-element.14), channel_id=1, source_target_pairs={{0,1},{1,0},{2,3},{3,2},{4,5},{5,4},{6,7},{7,6},{8,9},{9,8},{10,11... | collective-permute-start | bytes 1572872 | tf_op jit(solution)/shard_map/ppermute | solution.py:108
  53.4 1.4 %compare_and_fusion = (pred[128]{0:T(512)(128)(4,1)}, s32[128]{0:T(128)}, pred[128]{0:T(512)(128)(4,1)S(1)}, s32[128]{0:T(128)S(1)}, pred[128]{0:T(512)(128)(4,1...) fusion(s32[31,128]{1,0:T(8,128)} %param.9, ...), kind=kLoop, calls=%fused_computation.68 | loop fusion | flops 3840 | bytes 5780 | tf_op jit(solution)/shard_map/jit(_take)/and | solution.py:214
  55.5 1.9 %add_add_fusion.2 = f32[512,256]{1,0:T(8,128)} fusion(f32[512,256]{1,0:T(8,128)} %collective-permute-done.5, f32[512,256]{1,0:T(8,128)S(1)} %copy-done.2, f32[512,256]{1,0:T(8,128)S(1)} %collective-permute-done.1), kind=kLoop, calls=%fused_computation.9 | loop fusion | flops 262144 | bytes 2097152 | tf_op jit(solution)/shard_map/add | solution.py:156
  57.5 6.3 %collective-permute-start.6 = (f32[512,256]{1,0:T(8,128)}, f32[512,256]{1,0:T(8,128)S(1)}, u32[]{:S(2)}, u32[]{:S(2)}) collective-permute-start(f32[512,256]{1,0:T(8,128)} %add_add_fusion.2), channel_id=1, source_target_pairs={{0,2},{1,3},{2,4},{3,5},{4,6},{5,7},{8,10},{9,11},{10,12},{11,13},... | collective-permute-start | bytes 1572872 | tf_op jit(solution)/shard_map/ppermute | solution.py:112
  63.8 1.3 add_add_fusion
  65.1 1.3 collective-permute-start.10
  66.5 5.0 %collective-permute-done.6 = f32[512,256]{1,0:T(8,128)S(1)} collective-permute-done((f32[512,256]{1,0:T(8,128)}, f32[512,256]{1,0:T(8,128)S(1)}, u32[]{:S(2)}, u32[]{:S(2)}) %collective-permute-start.6) | collective-permute-done | bytes 524320 | tf_op jit(solution)/shard_map/ppermute | solution.py:112
  71.5 5.8 %collective-permute-done.10 = f32[512,256]{1,0:T(8,128)S(1)} collective-permute-done((f32[512,256]{1,0:T(8,128)S(1)}, f32[512,256]{1,0:T(8,128)S(1)}, u32[]{:S(2)}, u32[]{:S(2)}) %collective-permute-start.10) | collective-permute-done | bytes 524320 | tf_op jit(solution)/shard_map/ppermute | solution.py:112
  80.1 1.8 %collective-permute-start.13 = (f32[128,256]{1,0:T(8,128)S(1)}, f32[128,256]{1,0:T(8,128)S(1)}, u32[]{:S(2)}, u32[]{:S(2)}) collective-permute-start(f32[128,256]{1,0:T(8,128)S(1)} %broadcast_select_fusion.3), channel_id=1, source_target_pairs={{0,2},{1,3},{2,0},{3,1},{4,6},{5,7},{6,4},{7,5},{8,10},{9,11},{10,... | collective-permute-start | bytes 393224 | tf_op jit(solution)/shard_map/ppermute | solution.py:112
  82.0 3.2 %collective-permute-done.13 = f32[128,256]{1,0:T(8,128)S(1)} collective-permute-done((f32[128,256]{1,0:T(8,128)S(1)}, f32[128,256]{1,0:T(8,128)S(1)}, u32[]{:S(2)}, u32[]{:S(2)}) %collective-permute-start.13) | collective-permute-done | bytes 131104 | tf_op jit(solution)/shard_map/ppermute | solution.py:112
  86.1 3.5 %collective-permute-start.14 = (f32[128,256]{1,0:T(8,128)S(1)}, f32[128,256]{1,0:T(8,128)S(1)}, u32[]{:S(2)}, u32[]{:S(2)}) collective-permute-start(f32[128,256]{1,0:T(8,128)S(1)} %broadcast_select_fusion.2), channel_id=1, source_target_pairs={{0,4},{1,5},{4,0},{5,1},{8,12},{9,13},{12,8},{13,9},{16,20},{17,21... | collective-permute-start | bytes 393224 | tf_op jit(solution)/shard_map/ppermute | solution.py:112
  90.0 3.9 %collective-permute-done.14 = f32[128,256]{1,0:T(8,128)S(1)} collective-permute-done((f32[128,256]{1,0:T(8,128)S(1)}, f32[128,256]{1,0:T(8,128)S(1)}, u32[]{:S(2)}, u32[]{:S(2)}) %collective-permute-start.14) | collective-permute-done | bytes 131104 | tf_op jit(solution)/shard_map/ppermute | solution.py:112
  94.8 1.9 %collective-permute-start.15 = (f32[128,256]{1,0:T(8,128)S(1)}, f32[128,256]{1,0:T(8,128)S(1)}, u32[]{:S(2)}, u32[]{:S(2)}) collective-permute-start(f32[128,256]{1,0:T(8,128)S(1)} %broadcast_select_fusion.1), channel_id=1, source_target_pairs={{0,8},{1,9},{8,0},{9,1},{16,24},{17,25},{24,16},{25,17}} | collective-permute-start | bytes 393224 | tf_op jit(solution)/shard_map/ppermute | solution.py:204
  99.3 3.6 %collective-permute-start.16 = (f32[128,256]{1,0:T(8,128)S(1)}, f32[128,256]{1,0:T(8,128)S(1)}, u32[]{:S(2)}, u32[]{:S(2)}) collective-permute-start(f32[128,256]{1,0:T(8,128)S(1)} %broadcast_select_fusion), channel_id=1, source_target_pairs={{0,16},{1,17},{16,0},{17,1}} | collective-permute-start | bytes 393224 | tf_op jit(solution)/shard_map/ppermute | solution.py:204
  103.2 2.9 %collective-permute-done.16 = f32[128,256]{1,0:T(8,128)S(1)} collective-permute-done((f32[128,256]{1,0:T(8,128)S(1)}, f32[128,256]{1,0:T(8,128)S(1)}, u32[]{:S(2)}, u32[]{:S(2)}) %collective-permute-start.16) | collective-permute-done | bytes 131104 | tf_op jit(solution)/shard_map/ppermute | solution.py:204
  107.0 1.1 broadcast_select_fusion.14
  108.1 1.5 %collective-permute-start.17 = (f32[256,128]{1,0:T(8,128)S(1)}, f32[256,128]{1,0:T(8,128)S(1)}, u32[]{:S(2)}, u32[]{:S(2)}) collective-permute-start(f32[256,128]{1,0:T(8,128)S(1)} %get-tuple-element.41), channel_id=1, source_target_pairs={{0,1},{1,0},{2,3},{3,2},{4,5},{5,4},{6,7},{7,6},{8,9},{9,8},{10,11... | collective-permute-start | bytes 393224 | tf_op jit(solution)/shard_map/ppermute | solution.py:108
  109.7 1.4 %broadcast_select_fusion.22.picked_ref = s32[1,128]{1,0:T(1,128)} fusion(pred[]{:T(512)S(6)} %eq.48, pred[]{:T(512)S(6)} %or.3, pred[]{:T(512)S(6)} %eq.55, pred[]{:T(512)S(6)} %eq.56, pred[]{:T(512)S(6)} %eq.57, s32[31,128]{1,0:T(8,128)} %param.9, s32[]{:T(128)S(6)} %select_n.225, s32[]{:T(128)S(6)} %select_n.234, s32[]{:T(128)S(6)} %select_n.237, ...), kind=kLoop, calls=%fused_computation.84 | loop fusion | flops 640 | bytes 3097 | tf_op jit(solution)/shard_map/jit(_where)/select_n | solution.py:224
  111.7 9.7 %basis.2 = f32[256,128]{1,0:T(8,128)} custom-call(f32[256,128]{1,0:T(8,128)} %get-tuple-element.52.own_ref, f32[256,128]{1,0:T(8,128)} %copy-done.5, s32[1,128]{1,0:T(1,128)} %picked_ref.1), custom_call_target="tpu_custom_call" | custom-call | tf_op jit(solution)/shard_map/basis/pallas_call | solution.py:60
  122.1 9.7 %basis.3 = f32[256,128]{1,0:T(8,128)} custom-call(f32[256,128]{1,0:T(8,128)} %get-tuple-element.42.own_ref, f32[256,128]{1,0:T(8,128)} %copy-done.6, s32[1,128]{1,0:T(1,128)} %broadcast_select_fusion.22.picked_ref), custom_call_target="tpu_custom_call" | custom-call | tf_op jit(solution)/shard_map/basis/pallas_call | solution.py:60
  (79 shorter events, 15.3 us)
Async XLA Ops:
  5.1 18.0 %copy-start.1 = (f32[512,256]{1,0:T(8,128)S(1)}, f32[512,256]{1,0:T(8,128)}, u32[]{:S(2)}) copy-start(f32[512,256]{1,0:T(8,128)} %get-tuple-element.19) | copy-start | bytes 1572868
  5.1 18.0 %collective-permute-start.3 = (f32[512,256]{1,0:T(8,128)}, f32[512,256]{1,0:T(8,128)S(1)}, u32[]{:S(2)}, u32[]{:S(2)}) collective-permute-start(f32[512,256]{1,0:T(8,128)} %get-tuple-element.20), channel_id=1, source_target_pairs={{0,1},{1,0},{6,7},{7,6},{8,9},{9,8},{14,15},{15,14},{16,17},{17,16... | collective-permute-start | bytes 1572872 | tf_op jit(solution)/shard_map/ppermute | solution.py:108
  13.9 20.6 %copy-start.4 = (f32[512,256]{1,0:T(8,128)S(1)}, f32[512,256]{1,0:T(8,128)}, u32[]{:S(2)}) copy-start(f32[512,256]{1,0:T(8,128)} %get-tuple-element.17) | copy-start | bytes 1572868
  13.9 20.3 %collective-permute-start.2 = (f32[512,256]{1,0:T(8,128)}, f32[512,256]{1,0:T(8,128)S(1)}, u32[]{:S(2)}, u32[]{:S(2)}) collective-permute-start(f32[512,256]{1,0:T(8,128)} %get-tuple-element.18), channel_id=1, source_target_pairs={{0,1},{1,0},{2,3},{3,2},{4,5},{5,4},{6,7},{7,6},{8,9},{9,8},{10,11... | collective-permute-start | bytes 1572872 | tf_op jit(solution)/shard_map/ppermute | solution.py:108
  23.2 11.3 %collective-permute-start.4 = (f32[512,256]{1,0:T(8,128)S(1)}, f32[512,256]{1,0:T(8,128)S(1)}, u32[]{:S(2)}, u32[]{:S(2)}) collective-permute-start(f32[512,256]{1,0:T(8,128)S(1)} %add.96), channel_id=1, source_target_pairs={{0,2},{1,3},{8,10},{9,11},{16,18},{17,19},{24,26},{25,27}} | collective-permute-start | bytes 1572872 | tf_op jit(solution)/shard_map/ppermute | solution.py:112
  24.5 10.0 %collective-permute-start.8 = (f32[512,256]{1,0:T(8,128)S(1)}, f32[512,256]{1,0:T(8,128)S(1)}, u32[]{:S(2)}, u32[]{:S(2)}) collective-permute-start(f32[512,256]{1,0:T(8,128)S(1)} %add.96), channel_id=1, source_target_pairs={{6,4},{7,5},{14,12},{15,13},{22,20},{23,21},{30,28},{31,29}} | collective-permute-start | bytes 1572872 | tf_op jit(solution)/shard_map/ppermute | solution.py:112
  29.7 25.2 %collective-permute-start.1 = (f32[512,256]{1,0:T(8,128)}, f32[512,256]{1,0:T(8,128)S(1)}, u32[]{:S(2)}, u32[]{:S(2)}) collective-permute-start(f32[512,256]{1,0:T(8,128)} %get-tuple-element.16), channel_id=1, source_target_pairs={{0,1},{1,0},{2,3},{3,2},{4,5},{5,4},{8,9},{9,8},{10,11},{11,10},{1... | collective-permute-start | bytes 1572872 | tf_op jit(solution)/shard_map/ppermute | solution.py:108
  35.4 20.1 %collective-permute-start.5 = (f32[512,256]{1,0:T(8,128)}, f32[512,256]{1,0:T(8,128)}, u32[]{:S(2)}, u32[]{:S(2)}) collective-permute-start(f32[512,256]{1,0:T(8,128)} %get-tuple-element.37), channel_id=1, source_target_pairs={{0,2},{1,3},{2,4},{3,5},{8,10},{9,11},{10,12},{11,13},{16,18},{17,... | collective-permute-start | bytes 1572872 | tf_op jit(solution)/shard_map/ppermute | solution.py:112
  41.2 13.7 %copy-start.8 = (s32[1,128]{1,0:T(1,128)S(1)}, s32[1,128]{1,0:T(1,128)}, u32[]{:S(2)}) copy-start(s32[1,128]{1,0:T(1,128)} %picked_ref.1) | copy-start | bytes 1540
  41.2 14.3 %copy-start.2 = (f32[512,256]{1,0:T(8,128)S(1)}, f32[512,256]{1,0:T(8,128)}, u32[]{:S(2)}) copy-start(f32[512,256]{1,0:T(8,128)} %get-tuple-element.15) | copy-start | bytes 1572868
  45.1 18.6 %copy-start.3 = (f32[512,256]{1,0:T(8,128)S(1)}, f32[512,256]{1,0:T(8,128)}, u32[]{:S(2)}) copy-start(f32[512,256]{1,0:T(8,128)} %get-tuple-element.21) | copy-start | bytes 1572868
  45.1 18.6 %collective-permute-start.7 = (f32[512,256]{1,0:T(8,128)}, f32[512,256]{1,0:T(8,128)}, u32[]{:S(2)}, u32[]{:S(2)}) collective-permute-start(f32[512,256]{1,0:T(8,128)} %get-tuple-element.22), channel_id=1, source_target_pairs={{2,3},{3,2},{4,5},{5,4},{6,7},{7,6},{10,11},{11,10},{12,13},{13,12... | collective-permute-start | bytes 1572872 | tf_op jit(solution)/shard_map/ppermute | solution.py:108
  46.7 17.0 %collective-permute-start.9 = (f32[512,256]{1,0:T(8,128)S(1)}, f32[512,256]{1,0:T(8,128)}, u32[]{:S(2)}, u32[]{:S(2)}) collective-permute-start(f32[512,256]{1,0:T(8,128)S(1)} %get-tuple-element.38), channel_id=1, source_target_pairs={{4,2},{5,3},{6,4},{7,5},{12,10},{13,11},{14,12},{15,13},{20,18},{2... | collective-permute-start | bytes 1572872 | tf_op jit(solution)/shard_map/ppermute | solution.py:112
  52.0 25.3 %copy-start = (f32[512,256]{1,0:T(8,128)S(1)}, f32[512,256]{1,0:T(8,128)}, u32[]{:S(2)}) copy-start(f32[512,256]{1,0:T(8,128)} %get-tuple-element.13) | copy-start | bytes 1572868
  52.0 14.5 %collective-permute-start = (f32[512,256]{1,0:T(8,128)}, f32[512,256]{1,0:T(8,128)S(1)}, u32[]{:S(2)}, u32[]{:S(2)}) collective-permute-start(f32[512,256]{1,0:T(8,128)} %get-tuple-element.14), channel_id=1, source_target_pairs={{0,1},{1,0},{2,3},{3,2},{4,5},{5,4},{6,7},{7,6},{8,9},{9,8},{10,11... | collective-permute-start | bytes 1572872 | tf_op jit(solution)/shard_map/ppermute | solution.py:108
  54.9 11.5 %collective-permute-start.11 = (s32[1,128]{1,0:T(1,128)S(1)}, s32[1,128]{1,0:T(1,128)S(1)}, u32[]{:S(2)}, u32[]{:S(2)}) collective-permute-start(s32[1,128]{1,0:T(1,128)S(1)} %copy-done.8), channel_id=1, source_target_pairs={{0,1},{1,0},{2,3},{3,2},{4,5},{5,4},{6,7},{7,6},{8,9},{9,8},{10,11... | collective-permute-start | bytes 1544 | tf_op jit(solution)/shard_map/ppermute | solution.py:108
  57.5 14.0 %collective-permute-start.6 = (f32[512,256]{1,0:T(8,128)}, f32[512,256]{1,0:T(8,128)S(1)}, u32[]{:S(2)}, u32[]{:S(2)}) collective-permute-start(f32[512,256]{1,0:T(8,128)} %add_add_fusion.2), channel_id=1, source_target_pairs={{0,2},{1,3},{2,4},{3,5},{4,6},{5,7},{8,10},{9,11},{10,12},{11,13},... | collective-permute-start | bytes 1572872 | tf_op jit(solution)/shard_map/ppermute | solution.py:112
  65.1 14.9 %copy-start.7 = (pred[128]{0:T(512)(128)(4,1)S(1)}, pred[128]{0:T(512)(128)(4,1)}, u32[]{:S(2)}) copy-start(pred[128]{0:T(512)(128)(4,1)} %get-tuple-element.57) | copy-start | bytes 388
  65.1 12.2 %collective-permute-start.10 = (f32[512,256]{1,0:T(8,128)S(1)}, f32[512,256]{1,0:T(8,128)S(1)}, u32[]{:S(2)}, u32[]{:S(2)}) collective-permute-start(f32[512,256]{1,0:T(8,128)S(1)} %add_add_fusion), channel_id=1, source_target_pairs={{2,0},{3,1},{4,2},{5,3},{6,4},{7,5},{10,8},{11,9},{12,10},{13,11},... | collective-permute-start | bytes 1572872 | tf_op jit(solution)/shard_map/ppermute | solution.py:112
  77.3 4.6 %copy-start.11 = (s32[128]{0:T(128)S(1)}, s32[128]{0:T(128)}, u32[]{:S(2)}) copy-start(s32[128]{0:T(128)} %get-tuple-element.60) | copy-start | bytes 1540
  77.3 4.7 %copy-start.10 = (s32[128]{0:T(128)S(1)}, s32[128]{0:T(128)}, u32[]{:S(2)}) copy-start(s32[128]{0:T(128)} %get-tuple-element.24) | copy-start | bytes 1540
  80.1 5.1 %collective-permute-start.13 = (f32[128,256]{1,0:T(8,128)S(1)}, f32[128,256]{1,0:T(8,128)S(1)}, u32[]{:S(2)}, u32[]{:S(2)}) collective-permute-start(f32[128,256]{1,0:T(8,128)S(1)} %broadcast_select_fusion.3), channel_id=1, source_target_pairs={{0,2},{1,3},{2,0},{3,1},{4,6},{5,7},{6,4},{7,5},{8,10},{9,11},{10,... | collective-permute-start | bytes 393224 | tf_op jit(solution)/shard_map/ppermute | solution.py:112
  86.1 7.8 %collective-permute-start.14 = (f32[128,256]{1,0:T(8,128)S(1)}, f32[128,256]{1,0:T(8,128)S(1)}, u32[]{:S(2)}, u32[]{:S(2)}) collective-permute-start(f32[128,256]{1,0:T(8,128)S(1)} %broadcast_select_fusion.2), channel_id=1, source_target_pairs={{0,4},{1,5},{4,0},{5,1},{8,12},{9,13},{12,8},{13,9},{16,20},{17,21... | collective-permute-start | bytes 393224 | tf_op jit(solution)/shard_map/ppermute | solution.py:112
  90.0 17.0 %copy-start.9 = (pred[128]{0:T(512)(128)(4,1)S(1)}, pred[128]{0:T(512)(128)(4,1)}, u32[]{:S(2)}) copy-start(pred[128]{0:T(512)(128)(4,1)} %get-tuple-element.23) | copy-start | bytes 388
  94.8 3.5 %collective-permute-start.15 = (f32[128,256]{1,0:T(8,128)S(1)}, f32[128,256]{1,0:T(8,128)S(1)}, u32[]{:S(2)}, u32[]{:S(2)}) collective-permute-start(f32[128,256]{1,0:T(8,128)S(1)} %broadcast_select_fusion.1), channel_id=1, source_target_pairs={{0,8},{1,9},{8,0},{9,1},{16,24},{17,25},{24,16},{25,17}} | collective-permute-start | bytes 393224 | tf_op jit(solution)/shard_map/ppermute | solution.py:204
  97.8 13.3 %collective-permute-start.12 = (f32[256,128]{1,0:T(8,128)S(1)}, f32[256,128]{1,0:T(8,128)S(1)}, u32[]{:S(2)}, u32[]{:S(2)}) collective-permute-start(f32[256,128]{1,0:T(8,128)S(1)} %get-tuple-element.51), channel_id=1, source_target_pairs={{0,1},{1,0},{2,3},{3,2},{4,5},{5,4},{6,7},{7,6},{8,9},{9,8},{10,11... | collective-permute-start | bytes 393224 | tf_op jit(solution)/shard_map/ppermute | solution.py:108
  99.3 6.9 %collective-permute-start.16 = (f32[128,256]{1,0:T(8,128)S(1)}, f32[128,256]{1,0:T(8,128)S(1)}, u32[]{:S(2)}, u32[]{:S(2)}) collective-permute-start(f32[128,256]{1,0:T(8,128)S(1)} %broadcast_select_fusion), channel_id=1, source_target_pairs={{0,16},{1,17},{16,0},{17,1}} | collective-permute-start | bytes 393224 | tf_op jit(solution)/shard_map/ppermute | solution.py:204
  108.1 13.3 %collective-permute-start.17 = (f32[256,128]{1,0:T(8,128)S(1)}, f32[256,128]{1,0:T(8,128)S(1)}, u32[]{:S(2)}, u32[]{:S(2)}) collective-permute-start(f32[256,128]{1,0:T(8,128)S(1)} %get-tuple-element.41), channel_id=1, source_target_pairs={{0,1},{1,0},{2,3},{3,2},{4,5},{5,4},{6,7},{7,6},{8,9},{9,8},{10,11... | collective-permute-start | bytes 393224 | tf_op jit(solution)/shard_map/ppermute | solution.py:108
  111.1 0.7 copy-start.5
  121.5 0.7 copy-start.6

commit v2 on v1

v2 whole, which is shorter than its diff:
```python
import jax
import jax.numpy as jnp
from jax import lax
from jax.experimental import pallas as pl
from jax.experimental.pallas import tpu as pltpu
from jax.sharding import PartitionSpec as P


HIGHEST = lax.Precision.HIGHEST
GROUP = 1


def bits_of(count):
    return count.bit_length() - 1


def spd_inverse(a):
    n = a.shape[0]
    tiles = [a[8 * r : 8 * r + 8, :] for r in range(n // 8)]
    lane = lax.broadcasted_iota(jnp.int32, (8, n), 1)
    sub = lax.broadcasted_iota(jnp.int32, (8, n), 0)
    for kb in range(n // 8):
        k = 8 * kb
        edge = [jnp.broadcast_to(tiles[kb][:, k + j : k + j + 1], (8, n)) for j in range(8)]
        d = {
            (i, j): jnp.broadcast_to(edge[j][i : i + 1, :], (8, n))
            for i in range(8)
            for j in range(i + 1)
        }
        inside = (lane >= k) & (lane < k + 8)
        base = jnp.where(inside, jnp.where(lane - k == sub, 1.0, 0.0), tiles[kb])
        p = [jnp.broadcast_to(base[j : j + 1, :], (8, n)) for j in range(8)]
        inv, low = [None] * 8, {}
        for j in range(8):
            inv[j] = 1.0 / d[j, j]
            for i in range(j + 1, 8):
                low[i, j] = d[i, j] * inv[j]
            for i in range(j + 1, 8):
                for m in range(j + 1, i + 1):
                    d[i, m] = d[i, m] - low[i, j] * d[m, j]
                p[i] = p[i] - low[i, j] * p[j]
        w = [p[j] * inv[j] for j in range(8)]
        for j in range(7, 0, -1):
            for i in range(j):
                w[i] = w[i] - low[j, i] * w[j]
        fresh = []
        for r, t in enumerate(tiles):
            if r == kb:
                x = w[0]
                for j in range(1, 8):
                    x = jnp.where(sub == j, w[j], x)
            else:
                x = jnp.where(inside, 0.0, t)
                col = [jnp.broadcast_to(t[:, k + j : k + j + 1], (8, n)) for j in range(8)]
                pairs = [col[j] * w[j] + col[j + 1] * w[j + 1] for j in range(0, 8, 2)]
                x = x - ((pairs[0] + pairs[1]) + (pairs[2] + pairs[3]))
            fresh.append(x)
        tiles = fresh
    return jnp.concatenate(tiles, axis=0)


def dot(a, b, dims=((1,), (0,)), precision=HIGHEST):
    return lax.dot_general(
        a, b, (dims, ((), ())), precision=precision, preferred_element_type=jnp.float32
    )


def choices(picked, count):
    rank = picked.shape[1]
    index = lax.broadcasted_iota(jnp.int32, (count, rank), 0)
    chosen = index == picked
    ahead = jnp.sum((picked < index).astype(jnp.float32), axis=1, keepdims=True)
    member = jnp.sum(chosen.astype(jnp.float32), axis=1, keepdims=True)
    place = index.astype(jnp.float32) - ahead
    slot = lax.broadcasted_iota(jnp.int32, (count, rank), 1).astype(jnp.float32)
    others = (slot == place) & (jnp.broadcast_to(member, place.shape) < 0.5)
    return chosen.astype(jnp.float32), others.astype(jnp.float32)


def inverse_kernel(own_ref, received_ref, out_ref):
    out_ref[...] = spd_inverse(own_ref[...] + received_ref[...])


def leaf_kernel(own_ref, received_ref, inverse_ref, picked_ref, basis_ref):
    chosen, others = choices(picked_ref[...], basis_ref.shape[0])
    solved = dot(own_ref[...] + received_ref[...], inverse_ref[...])
    basis_ref[...] = chosen + dot(others, solved)


def node_kernel(own_ref, received_ref, picked_ref, basis_ref):
    cross = own_ref[...] + received_ref[...]
    index = lax.broadcasted_iota(jnp.int32, cross.shape, 0)
    choice = (index == picked_ref[...]).astype(jnp.float32)
    gram = dot(choice, cross, ((0,), (0,)))
    basis_ref[...] = dot(cross, spd_inverse(gram))


def unit_rows(matrix_ref, hit, n_grp):
    rows = matrix_ref.shape[0]
    pieces = []
    for c in range(n_grp):
        piece = matrix_ref[:, c * rows : (c + 1) * rows]
        pieces.append(jnp.where(hit == c, jnp.zeros_like(piece), piece))
    return pieces


def sides(block, probes_ref, side, half):
    away = probes_ref[:, pl.ds(pl.multiple_of((1 - side) * half, half), half)]
    home = probes_ref[:, pl.ds(pl.multiple_of(side * half, half), half)]
    return dot(block, away, precision=None), dot(block, home, precision=None)


def plain_kernel(n_leaf, n_grp, mask, place_ref, matrix_ref, probes_ref, send_ref, keep_ref):
    spot = (place_ref[1] >> 1) ^ mask
    hit = place_ref[0] * n_leaf + 2 * spot + pl.program_id(0) - place_ref[1] * n_grp
    block = jnp.concatenate(unit_rows(matrix_ref, hit, n_grp), axis=1)
    send_ref[...], keep_ref[...] = sides(block, probes_ref, place_ref[1] & 1, send_ref.shape[1])


def ordered_kernel(n_leaf, n_grp, high, place_ref, matrix_ref, probes_ref, picked_ref, *outs):
    step = pl.program_id(0)
    spot = (place_ref[1] >> 1) ^ (high - step // 2)
    hit = place_ref[0] * n_leaf + 2 * spot + step % 2 - place_ref[1] * n_grp
    rank, half = picked_ref.shape[2], outs[0].shape[1]
    chosen, others = choices(picked_ref[0], matrix_ref.shape[0])
    order = jnp.concatenate([chosen, others], axis=1).astype(jnp.bfloat16)
    block = jnp.concatenate(
        [
            dot(order, piece, ((0,), (0,)), None).astype(jnp.bfloat16)
            for piece in unit_rows(matrix_ref, hit, n_grp)
        ],
        axis=1,
    )
    away, home = sides(block, probes_ref, place_ref[1] & 1, half)
    for j in range(len(outs) // 4):

        @pl.when(step // 2 == j)
        def _():
            at = pl.ds(pl.multiple_of(step % 2 * rank, rank), rank)
            outs[4 * j][at, :] = away[:rank]
            outs[4 * j + 1][at, :] = home[:rank]
            outs[4 * j + 2][at, :] = away[rank:]
            outs[4 * j + 3][at, :] = home[rank:]


def split_kernel(place_ref, keep_ref, received_ref, picked_ref, first_ref, second_ref):
    total = keep_ref[...] + received_ref[...]
    chosen, others = choices(picked_ref[0], total.shape[0])
    first_ref[...] = dot(chosen, total, ((0,), (0,)))
    second_ref[...] = dot(others, total, ((0,), (0,)))


def on_device(matrix, probes, leaf_skeleton, node_skeleton):
    n_grp = lax.axis_size("grp")
    n_leaf = lax.axis_size("leaf")
    grp_pos = lax.axis_index("grp")
    leaf_pos = lax.axis_index("leaf")
    device = grp_pos * n_leaf + leaf_pos
    side = leaf_pos & 1
    spot = leaf_pos >> 1
    spots = n_leaf // 2
    row_count, col_count = matrix.shape
    leaf_rows = row_count // n_leaf
    half = probes.shape[1] // 2
    rank = leaf_skeleton.shape[1]
    all_leaves = n_grp * n_leaf
    leaf_bits, grp_bits = bits_of(n_leaf), bits_of(n_grp)
    levels = leaf_bits + grp_bits

    def across(value):
        return lax.ppermute(value, "leaf", [(p, p ^ 1) for p in range(n_leaf)])

    def along(value, hops):
        pairs = [(2 * a + s, 2 * b + s) for a, b in hops for s in range(2)]
        return lax.ppermute(value, "leaf", pairs)

    place = jnp.stack([grp_pos, leaf_pos]).astype(jnp.int32)
    masks = list(range(spots - 1, -1, -1))
    top = masks[0]
    wide = jax.ShapeDtypeStruct((2 * leaf_rows, half), jnp.float32)
    slim = jax.ShapeDtypeStruct((2 * rank, half), jnp.float32)

    def leaf_row(high):
        return lambda i, at: 2 * ((at[1] >> 1) ^ (high - i // 2)) + i % 2

    def grid_spec(count, in_specs, out_specs):
        return pltpu.PrefetchScalarGridSpec(
            num_scalar_prefetch=1, grid=(count,), in_specs=in_specs, out_specs=out_specs
        )

    def matrix_specs(high):
        row = leaf_row(high)
        return [
            pl.BlockSpec((leaf_rows, col_count), lambda i, at: (row(i, at), 0)),
            pl.BlockSpec(probes.shape, lambda i, at: (0, 0)),
        ]

    def picked_spec(high):
        row = leaf_row(high)
        return pl.BlockSpec((1, 1, rank), lambda i, at: (row(i, at), 0, 0))

    send, keep = pl.pallas_call(
        lambda *refs: plain_kernel(n_leaf, n_grp, top, *refs),
        out_shape=(wide,) * 2,
        grid_spec=grid_spec(
            2, matrix_specs(top), [pl.BlockSpec((leaf_rows, half), lambda i, at: (i, 0))] * 2
        ),
        name="product",
    )(place, matrix, probes)

    skeletons = leaf_skeleton
    for bit in range(leaf_bits):
        partner = lax.ppermute(skeletons, "leaf", [(p, p ^ 1 << bit) for p in range(n_leaf)])
        if bit == 0:
            send, partner = lax.optimization_barrier((send, partner))
        skeletons = jnp.where(
            leaf_pos >> bit & 1 == 1,
            jnp.concatenate([partner, skeletons], axis=0),
            jnp.concatenate([skeletons, partner], axis=0),
        )
    top_received = across(send)
    tables = skeletons[:, None, :]

    def ordered(group):
        high, count = group[0], len(group)
        outs = pl.pallas_call(
            lambda *refs: ordered_kernel(n_leaf, n_grp, high, *refs),
            out_shape=(slim,) * (4 * count),
            grid_spec=grid_spec(
                2 * count,
                [*matrix_specs(high), picked_spec(high)],
                [pl.BlockSpec(slim.shape, lambda i, at: (0, 0))] * (4 * count),
            ),
            name="ordered",
        )
        outs = outs(place, matrix, probes, tables)
        return {mask: outs[4 * j : 4 * j + 4] for j, mask in enumerate(group)}

    pieces = {}
    for at in range(1, spots, GROUP):
        pieces.update(ordered(masks[at : at + GROUP]))

    piece = pl.BlockSpec((leaf_rows, half), lambda i, at: (i, 0))
    part = pl.BlockSpec((rank, half), lambda i, at: (i, 0))
    first, second = {}, {}
    first[top], second[top] = pl.pallas_call(
        split_kernel,
        out_shape=(slim,) * 2,
        grid_spec=grid_spec(2, [piece, piece, picked_spec(top)], [part] * 2),
        name="split",
    )(place, keep, top_received, tables)

    for mask in masks[1:]:
        received = across(pieces[mask][0])
        first[mask] = pieces[mask][1] + received
        if mask == min(1, top):
            gate = received
    for mask in masks[1:]:
        send, _ = lax.optimization_barrier((pieces[mask][2], gate))
        second[mask] = pieces[mask][3] + across(send)

    def gathered(values, gates=None):
        values = dict(values)
        for mask in masks[:-1]:
            bit = mask & -mask
            value = values[mask]
            if gates is not None:
                gate = gates[0] if mask == top else gates[1]
                value, _ = lax.optimization_barrier((value, gate))
            elif mask ^ bit == 0:
                early.append(value)
            arrived = along(value, [(z, z ^ bit) for z in range(spots)])
            if gates is not None and mask != top:
                arrived, _ = lax.optimization_barrier((arrived, gates[2]))
            values[mask ^ bit] = values[mask ^ bit] + arrived
        return values[0]

    early = []

    skeleton_rows = gathered(first)

    def cross_of(stacked, rows):
        return dot(stacked, rows, ((1,), (1,)))

    halves = (skeleton_rows[:rank], skeleton_rows[rank:])
    grams = [cross_of(r, r) for r in halves]
    own_gram = jnp.where(side == 0, grams[0], grams[1])
    received_gram = across(jnp.where(side == 0, grams[1], grams[0]))

    def level_offset(level):
        return sum(all_leaves >> inner for inner in range(1, level))

    def picked_of(level):
        node = level_offset(level) + (device >> level)
        return lax.dynamic_slice_in_dim(node_skeleton, node, 1, 0)[0]

    gates = []
    low_stack = skeleton_rows
    low_picked = picked_of(1)
    current = low_rows = jnp.take(low_stack, low_picked, axis=0)
    low_cross = cross_of(low_stack, low_rows)
    high_stack, high_picked, high_rows = low_stack, low_picked, low_rows
    even = device - side
    for level in range(2, levels + 1):
        if level <= leaf_bits:
            bit = level - 2
            hops = [(z, z ^ 1 << bit) for z in range(0, spots, 1 << bit)]
            partner = along(current, hops)
            upper = spot >> bit & 1
            gates.append(partner)
        else:
            bit = level - leaf_bits - 1
            pairs = [
                (g * n_leaf + s, (g ^ 1 << bit) * n_leaf + s)
                for g in range(0, n_grp, 1 << bit)
                for s in range(2)
            ]
            partner = lax.ppermute(current, ("grp", "leaf"), pairs)
            upper = grp_pos >> bit & 1
        stacked = jnp.concatenate(
            [
                jnp.where(upper == 1, partner, current),
                jnp.where(upper == 1, current, partner),
            ],
            axis=0,
        )
        picked = picked_of(level)
        current = jnp.take(stacked, picked, axis=0)
        select = even % (1 << level) == 1 << level - 1
        if level == levels:
            select = select | (even == 0)
        high_stack = jnp.where(select, stacked, high_stack)
        high_rows = jnp.where(select, current, high_rows)
        high_picked = jnp.where(select, picked, high_picked)
    high_cross = cross_of(high_stack, high_rows)
    own = jnp.where(side == 1, low_cross, high_cross)
    sent = jnp.where(side == 1, high_cross, low_cross)
    received = across(sent)
    own_gram, _ = lax.optimization_barrier((own_gram, sent))
    square = jax.ShapeDtypeStruct((rank, rank), jnp.float32)
    inverse = pl.pallas_call(inverse_kernel, out_shape=square, name="inverse")(own_gram, received_gram)
    node_picked = jnp.where(side == 1, low_picked, high_picked)
    other_rows = gathered(second, [early[0], gates[-1], inverse])
    crosses = [
        cross_of(z, r) for z, r in zip((other_rows[:rank], other_rows[rank:]), halves)
    ]
    own_leaf = jnp.where(side == 0, crosses[0], crosses[1])
    received_leaf = across(jnp.where(side == 0, crosses[1], crosses[0]))
    tall = jax.ShapeDtypeStruct((leaf_rows, rank), jnp.float32)
    leaf_basis = pl.pallas_call(leaf_kernel, out_shape=tall, name="leaf_basis")(
        own_leaf, received_leaf, inverse, leaf_skeleton
    )

    received, *_ = lax.optimization_barrier((received, *crosses))
    tall = jax.ShapeDtypeStruct((2 * rank, rank), jnp.float32)
    transfer = pl.pallas_call(node_kernel, out_shape=tall, name="node_basis")(
        own, received, node_picked[None]
    )
    return (leaf_basis, transfer[None])


def solution(mesh):
    return jax.shard_map(
        on_device,
        mesh=mesh,
        in_specs=(P("grp", "leaf"), P("leaf", None), P(("grp", "leaf"), None), P()),
        out_specs=(P(("grp", "leaf"), None), P(("grp", "leaf"), None, None)),
        check_vma=False,
    )
```

time: 133 us -> 110 us (0.83)
  waiting for transfers between devices: 30.9 us -> 18.4 us
  starting transfers between devices: 41.7 us -> 37.1 us
  other arithmetic: 10.1 us -> 6.16 us
    ppermute x8, waiting for transfers between devices: 18.1 us -> 9.22 us  [along(): return lax.ppermute(value, 'leaf', pairs)]
    ppermute x8, starting transfers between devices: 21.5 us -> 12.7 us  [along(): return lax.ppermute(value, 'leaf', pairs)]
    ppermute x8 -> x13, starting transfers between devices: 14.7 us -> 19 us  [the longest x10 10.8 us: across(): return lax.ppermute(value, 'leaf', [(p, p ^ 1) for p in range(n_leaf)])]
    ppermute x8 -> x13, waiting for transfers between devices: 9.82 us -> 6.62 us  [the longest x10 3.5 us: across(): return lax.ppermute(value, 'leaf', [(p, p ^ 1) for p in range(n_leaf)])]
    add x5 -> x6, other arithmetic: 4.37 us -> 1.98 us  [the longest x4 1.91 us: gathered(): values[mask ^ bit] = values[mask ^ bit] + arrived]
    gather x2 -> x0, local copies, waits for them, and re-layouts: 1.51 us -> none  [on_device(): jnp.take(z, j, axis=0)]
    pallas_call x7 -> x8, Pallas kernels: 38.5 us -> 37.4 us  [the longest x3 13.9 us: ordered(): outs = outs(place, matrix, probes, tables)]
    dot_general x4 -> x6, matrix products: 2.91 us -> 3.9 us  [dot(): lax.dot_general(a, b, (dims, ((), ())), precision=precision, preferred_el...]
  transfers between devices with their start and end apart: 18 -> 23, of which waited for: 8 -> 9; matrix products, arithmetic and copies ran while one was open for 10% -> 13% of each run, Pallas kernels for 19% -> 27%
where the time goes in v2:
time: 110 us
  Pallas kernels  37.4 us (34%)
  starting transfers between devices  37.1 us (34%)
  waiting for transfers between devices  18.4 us (17%)
  other arithmetic  6.16 us (6%)
  local copies, waits for them, and re-layouts  5.91 us (5%)
  matrix products  3.9 us (4%)
    pallas_call x3, Pallas kernels, ordered(): outs = outs(place, matrix, probes, tables)  13.9 us
    ppermute x8, starting transfers between devices, along(): return lax.ppermute(value, 'leaf', pairs)  12.7 us
    ppermute x10, starting transfers between devices, across(): return lax.ppermute(value, 'leaf', [(p, p ^ 1) for p in range(n_leaf)])  10.8 us
    ppermute x8, waiting for transfers between devices, along(): return lax.ppermute(value, 'leaf', pairs)  9.22 us
    ppermute x3, starting transfers between devices, on_device(): lax.ppermute(skeletons, 'leaf', [(p, p ^ 1 << bit) for p in range(n_leaf)])  8.22 us
    pallas_call x1, Pallas kernels, on_device(): pl.pallas_call(node_kernel, out_shape=tall, name='node_basis')  7.99 us
    pallas_call x1, Pallas kernels, on_device(): pl.pallas_call(inverse_kernel, out_shape=square, name='inverse')  6.02 us
    ppermute x2, starting transfers between devices, on_device(): partner = lax.ppermute(current, ('grp', 'leaf'), pairs)  5.36 us
  transfers between devices with their start and end apart: 23, of which 9 were waited for; matrix products, arithmetic and copies ran while one was open for 13% of the time, Pallas kernels for 27%

profile of v2, /device:TPU:0, one launch (start us, length us, event | category | flops | bytes accessed | tf_op | source)
XLA Modules:
  0.0 109.9 jit_solution(2535343225919516824)
XLA Ops:
  0.6 3.1 %collective-permute-start = (s32[1,128]{1,0:T(1,128)}, s32[1,128]{1,0:T(1,128)S(1)}, u32[]{:S(2)}, u32[]{:S(2)}) collective-permute-start(s32[1,128]{1,0:T(1,128)} %picked_ref.1), channel_id=1, source_target_pairs={{0,1},{1,0},{2,3},{3,2},{4,5},{5,4},{6,7},{7,6},{8,9},{9,8},{10,11... | collective-permute-start | bytes 1544 | tf_op jit(solution)/shard_map/ppermute | solution.py:213
  4.3 3.8 %product.1 = (f32[512,256]{1,0:T(8,128)}, f32[512,256]{1,0:T(8,128)}) custom-call(s32[2]{0:T(128)} %pad_add_fusion.refs_0_.place_ref, bf16[2048,1024]{1,0:T(8,128)(2,1)} %refs_1_.7, bf16[1024,512]{1,0:T(8,128)(2,1)} %refs_2_.7), custom_call_target="tpu_custom_call" | custom-call | tf_op jit(solution)/shard_map/product/pallas_call | solution.py:202
  8.2 2.1 %collective-permute-start.1 = (s32[2,128]{1,0:T(2,128)S(1)}, s32[2,128]{1,0:T(2,128)S(1)}, u32[]{:S(2)}, u32[]{:S(2)}) collective-permute-start(s32[2,128]{1,0:T(2,128)S(1)} %add_select_fusion.1), channel_id=1, source_target_pairs={{0,2},{1,3},{2,0},{3,1},{4,6},{5,7},{6,4},{7,5},{8,10},{9,11},{10,... | collective-permute-start | bytes 3080 | tf_op jit(solution)/shard_map/ppermute | solution.py:213
  10.3 1.6 %collective-permute-done.1 = s32[2,128]{1,0:T(2,128)S(1)} collective-permute-done((s32[2,128]{1,0:T(2,128)S(1)}, s32[2,128]{1,0:T(2,128)S(1)}, u32[]{:S(2)}, u32[]{:S(2)}) %collective-permute-start.1) | collective-permute-done | bytes 1056 | tf_op jit(solution)/shard_map/ppermute | solution.py:213
  11.8 3.0 %collective-permute-start.2 = (s32[4,128]{1,0:T(4,128)S(1)}, s32[4,128]{1,0:T(4,128)S(1)}, u32[]{:S(2)}, u32[]{:S(2)}) collective-permute-start(s32[4,128]{1,0:T(4,128)S(1)} %add_select_fusion), channel_id=1, source_target_pairs={{0,4},{1,5},{2,6},{3,7},{4,0},{5,1},{6,2},{7,3},{8,12},{9,13},{10,... | collective-permute-start | bytes 6152 | tf_op jit(solution)/shard_map/ppermute | solution.py:213
  14.9 1.6 %collective-permute-done.2 = s32[4,128]{1,0:T(4,128)S(1)} collective-permute-done((s32[4,128]{1,0:T(4,128)S(1)}, s32[4,128]{1,0:T(4,128)S(1)}, u32[]{:S(2)}, u32[]{:S(2)}) %collective-permute-start.2) | collective-permute-done | bytes 2080 | tf_op jit(solution)/shard_map/ppermute | solution.py:213
  17.0 4.6 %ordered.5 = (f32[256,256]{1,0:T(8,128)}, f32[256,256]{1,0:T(8,128)}, f32[256,256]{1,0:T(8,128)}, f32[256,256]{1,0:T(8,128)}) custom-call(s32[2]{0:T(128)} %pad_add_fusion.refs_0_.place_ref, bf16[2048,1024]{1,0:T(8,128)(2,1)} %refs_1_.7, bf16[1024,512]{1,0:T(8,128)(2,1)} %refs_2_.7, s32[8,1,128]{2,1,0:T(1,128)} %broadcast_select_fusion.18.refs_3_.picked_ref), custom_call_target="tpu_custom_call" | custom-call | tf_op jit(solution)/shard_map/ordered/pallas_call | solution.py:236
  21.6 4.7 %ordered.4 = (f32[256,256]{1,0:T(8,128)}, f32[256,256]{1,0:T(8,128)}, f32[256,256]{1,0:T(8,128)}, f32[256,256]{1,0:T(8,128)}) custom-call(s32[2]{0:T(128)} %pad_add_fusion.refs_0_.place_ref, bf16[2048,1024]{1,0:T(8,128)(2,1)} %refs_1_.7, bf16[1024,512]{1,0:T(8,128)(2,1)} %refs_2_.7, s32[8,1,128]{2,1,0:T(1,128)} %broadcast_select_fusion.18.refs_3_.picked_ref), custom_call_target="tpu_custom_call" | custom-call | tf_op jit(solution)/shard_map/ordered/pallas_call | solution.py:236
  26.3 1.9 %collective-permute-start.7 = (f32[256,256]{1,0:T(8,128)S(1)}, f32[256,256]{1,0:T(8,128)S(1)}, u32[]{:S(2)}, u32[]{:S(2)}) collective-permute-start(f32[256,256]{1,0:T(8,128)S(1)} %copy-done.10), channel_id=1, source_target_pairs={{0,1},{1,0},{2,3},{3,2},{4,5},{5,4},{6,7},{7,6},{8,9},{9,8},{10,11... | collective-permute-start | bytes 786440 | tf_op jit(solution)/shard_map/ppermute | solution.py:171
  29.2 3.5 %split.1 = (f32[256,256]{1,0:T(8,128)}, f32[256,256]{1,0:T(8,128)}) custom-call(s32[2]{0:T(128)} %pad_add_fusion.refs_0_.place_ref, f32[512,256]{1,0:T(8,128)} %get-tuple-element.40.keep_ref, f32[512,256]{1,0:T(8,128)} %copy-done, s32[8,1,128]{2,1,0:T(1,128)} %broadcast_select_fusion.18.refs_3_.picked_ref), custom_call_target="tpu_custom_call" | custom-call | tf_op jit(solution)/shard_map/split/pallas_call | solution.py:246
  32.8 1.9 %collective-permute-start.8 = (f32[256,256]{1,0:T(8,128)}, f32[256,256]{1,0:T(8,128)S(1)}, u32[]{:S(2)}, u32[]{:S(2)}) collective-permute-start(f32[256,256]{1,0:T(8,128)} %get-tuple-element.45), channel_id=1, source_target_pairs={{0,2},{1,3},{2,0},{3,1},{4,6},{5,7},{6,4},{7,5},{8,10},{9,11},{10,... | collective-permute-start | bytes 786440 | tf_op jit(solution)/shard_map/ppermute | solution.py:175
  35.5 4.7 %ordered.3 = (f32[256,256]{1,0:T(8,128)}, f32[256,256]{1,0:T(8,128)}, f32[256,256]{1,0:T(8,128)}, f32[256,256]{1,0:T(8,128)}) custom-call(s32[2]{0:T(128)} %pad_add_fusion.refs_0_.place_ref, bf16[2048,1024]{1,0:T(8,128)(2,1)} %refs_1_.7, bf16[1024,512]{1,0:T(8,128)(2,1)} %refs_2_.7, s32[8,1,128]{2,1,0:T(1,128)} %broadcast_select_fusion.18.refs_3_.picked_ref), custom_call_target="tpu_custom_call" | custom-call | tf_op jit(solution)/shard_map/ordered/pallas_call | solution.py:236
  40.2 1.5 %collective-permute-start.10 = (f32[256,256]{1,0:T(8,128)}, f32[256,256]{1,0:T(8,128)S(1)}, u32[]{:S(2)}, u32[]{:S(2)}) collective-permute-start(f32[256,256]{1,0:T(8,128)} %get-tuple-element.48), channel_id=1, source_target_pairs={{0,1},{1,0},{2,3},{3,2},{4,5},{5,4},{6,7},{7,6},{8,9},{9,8},{10,11... | collective-permute-start | bytes 786440 | tf_op jit(solution)/shard_map/ppermute | solution.py:171
  42.3 2.7 %collective-permute-start.11 = (f32[256,256]{1,0:T(8,128)S(1)}, f32[256,256]{1,0:T(8,128)S(1)}, u32[]{:S(2)}, u32[]{:S(2)}) collective-permute-start(f32[256,256]{1,0:T(8,128)S(1)} %add_add_fusion.2), channel_id=1, source_target_pairs={{0,4},{1,5},{2,6},{3,7},{4,0},{5,1},{6,2},{7,3},{8,12},{9,13},{10,... | collective-permute-start | bytes 786440 | tf_op jit(solution)/shard_map/ppermute | solution.py:175
  45.0 1.4 %collective-permute-start.19 = (f32[256,256]{1,0:T(8,128)S(1)}, f32[256,256]{1,0:T(8,128)S(1)}, u32[]{:S(2)}, u32[]{:S(2)}) collective-permute-start(f32[256,256]{1,0:T(8,128)S(1)} %copy-done.9), channel_id=1, source_target_pairs={{0,1},{1,0},{2,3},{3,2},{4,5},{5,4},{6,7},{7,6},{8,9},{9,8},{10,11... | collective-permute-start | bytes 786440 | tf_op jit(solution)/shard_map/ppermute | solution.py:171
  46.4 2.2 %collective-permute-done.10 = f32[256,256]{1,0:T(8,128)S(1)} collective-permute-done((f32[256,256]{1,0:T(8,128)}, f32[256,256]{1,0:T(8,128)S(1)}, u32[]{:S(2)}, u32[]{:S(2)}) %collective-permute-start.10) | collective-permute-done | bytes 262176 | tf_op jit(solution)/shard_map/ppermute | solution.py:171
  48.6 2.9 %collective-permute-done.12 = f32[256,256]{1,0:T(8,128)S(1)} collective-permute-done((f32[256,256]{1,0:T(8,128)S(1)}, f32[256,256]{1,0:T(8,128)S(1)}, u32[]{:S(2)}, u32[]{:S(2)}) %collective-permute-start.12) | collective-permute-done | bytes 262176 | tf_op jit(solution)/shard_map/ppermute | solution.py:175
  53.4 2.7 %collective-permute-start.13 = (f32[128,256]{1,0:T(8,128)S(1)}, f32[128,256]{1,0:T(8,128)S(1)}, u32[]{:S(2)}, u32[]{:S(2)}) collective-permute-start(f32[128,256]{1,0:T(8,128)S(1)} %broadcast_select_fusion.3), channel_id=1, source_target_pairs={{0,2},{1,3},{2,0},{3,1},{4,6},{5,7},{6,4},{7,5},{8,10},{9,11},{10,... | collective-permute-start | bytes 393224 | tf_op jit(solution)/shard_map/ppermute | solution.py:175
  56.1 1.6 %collective-permute-start.5 = (f32[256,256]{1,0:T(8,128)}, f32[256,256]{1,0:T(8,128)S(1)}, u32[]{:S(2)}, u32[]{:S(2)}) collective-permute-start(f32[256,256]{1,0:T(8,128)} %get-tuple-element.39), channel_id=1, source_target_pairs={{0,1},{1,0},{2,3},{3,2},{4,5},{5,4},{6,7},{7,6},{8,9},{9,8},{10,11... | collective-permute-start | bytes 786440 | tf_op jit(solution)/shard_map/ppermute | solution.py:171
  60.1 4.7 %collective-permute-start.14 = (f32[128,256]{1,0:T(8,128)S(1)}, f32[128,256]{1,0:T(8,128)S(1)}, u32[]{:S(2)}, u32[]{:S(2)}) collective-permute-start(f32[128,256]{1,0:T(8,128)S(1)} %broadcast_select_fusion.2), channel_id=1, source_target_pairs={{0,4},{1,5},{4,0},{5,1},{8,12},{9,13},{12,8},{13,9},{16,20},{17,21... | collective-permute-start | bytes 393224 | tf_op jit(solution)/shard_map/ppermute | solution.py:175
  65.2 5.5 %collective-permute-done.14 = f32[128,256]{1,0:T(8,128)S(1)} collective-permute-done((f32[128,256]{1,0:T(8,128)S(1)}, f32[128,256]{1,0:T(8,128)S(1)}, u32[]{:S(2)}, u32[]{:S(2)}) %collective-permute-start.14) | collective-permute-done | bytes 131104 | tf_op jit(solution)/shard_map/ppermute | solution.py:175
  71.7 1.9 %collective-permute-start.16 = (f32[128,256]{1,0:T(8,128)S(1)}, f32[128,256]{1,0:T(8,128)S(1)}, u32[]{:S(2)}, u32[]{:S(2)}) collective-permute-start(f32[128,256]{1,0:T(8,128)S(1)} %broadcast_select_fusion.1), channel_id=1, source_target_pairs={{0,8},{1,9},{8,0},{9,1},{16,24},{17,25},{24,16},{25,17}} | collective-permute-start | bytes 393224 | tf_op jit(solution)/shard_map/ppermute | solution.py:318
  74.5 1.7 %collective-permute-start.18 = (f32[128,128]{1,0:T(8,128)}, f32[128,128]{1,0:T(8,128)}, u32[]{:S(2)}, u32[]{:S(2)}) collective-permute-start(f32[128,128]{1,0:T(8,128)} %get-tuple-element.81), channel_id=1, source_target_pairs={{0,1},{1,0},{2,3},{3,2},{4,5},{5,4},{6,7},{7,6},{8,9},{9,8},{10,11... | collective-permute-start | bytes 196616 | tf_op jit(solution)/shard_map/ppermute | solution.py:171
  77.2 3.4 %collective-permute-start.17 = (f32[128,256]{1,0:T(8,128)S(1)}, f32[128,256]{1,0:T(8,128)S(1)}, u32[]{:S(2)}, u32[]{:S(2)}) collective-permute-start(f32[128,256]{1,0:T(8,128)S(1)} %broadcast_select_fusion), channel_id=1, source_target_pairs={{0,16},{1,17},{16,0},{17,1}} | collective-permute-start | bytes 393224 | tf_op jit(solution)/shard_map/ppermute | solution.py:318
  81.5 2.6 %collective-permute-done.17 = f32[128,256]{1,0:T(8,128)S(1)} collective-permute-done((f32[128,256]{1,0:T(8,128)S(1)}, f32[128,256]{1,0:T(8,128)S(1)}, u32[]{:S(2)}, u32[]{:S(2)}) %collective-permute-start.17) | collective-permute-done | bytes 131104 | tf_op jit(solution)/shard_map/ppermute | solution.py:318
  85.4 1.0 broadcast_select_fusion.10
  86.9 6.0 %inverse.1.inverse_ref = f32[128,128]{1,0:T(8,128)} custom-call(f32[128,128]{1,0:T(8,128)} %get-tuple-element.51.own_ref, f32[128,128]{1,0:T(8,128)} %collective-permute-done.18.received_ref), custom_call_target="tpu_custom_call" | custom-call | tf_op jit(solution)/shard_map/inverse/pallas_call | solution.py:341
  94.2 1.6 %collective-permute-start.21 = (f32[128,128]{1,0:T(8,128)S(1)}, f32[128,128]{1,0:T(8,128)S(1)}, u32[]{:S(2)}, u32[]{:S(2)}) collective-permute-start(f32[128,128]{1,0:T(8,128)S(1)} %get-tuple-element.79), channel_id=1, source_target_pairs={{0,1},{1,0},{2,3},{3,2},{4,5},{5,4},{6,7},{7,6},{8,9},{9,8},{10,11... | collective-permute-start | bytes 196616 | tf_op jit(solution)/shard_map/ppermute | solution.py:171
  95.8 1.4 %broadcast_select_fusion.23.picked_ref = s32[1,128]{1,0:T(1,128)} fusion(pred[]{:T(512)S(6)} %eq.61, pred[]{:T(512)S(6)} %or.3, pred[]{:T(512)S(6)} %eq.67, pred[]{:T(512)S(6)} %eq.68, pred[]{:T(512)S(6)} %eq.69, s32[31,128]{1,0:T(8,128)} %param.9, s32[]{:T(128)S(6)} %select_n.250, s32[]{:T(128)S(6)} %select_n.253, s32[]{:T(128)S(6)} %select_n.263, ...), kind=kLoop, calls=%fused_computation.87 | loop fusion | flops 640 | bytes 3097 | tf_op jit(solution)/shard_map/jit(_where)/select_n | solution.py:342
  97.2 1.3 %collective-permute-done.21.received_ref = f32[128,128]{1,0:T(8,128)S(1)} collective-permute-done((f32[128,128]{1,0:T(8,128)S(1)}, f32[128,128]{1,0:T(8,128)S(1)}, u32[]{:S(2)}, u32[]{:S(2)}) %collective-permute-start.21) | collective-permute-done | bytes 65568 | tf_op jit(solution)/shard_map/ppermute | solution.py:171
  99.1 2.1 %leaf_basis.1 = f32[256,128]{1,0:T(8,128)} custom-call(f32[128,128]{1,0:T(8,128)} %get-tuple-element.80.own_ref, f32[128,128]{1,0:T(8,128)} %copy-done.7, f32[128,128]{1,0:T(8,128)} %inverse.1.inverse_ref, s32[1,128]{1,0:T(1,128)} %picked_ref.1), custom_call_target="tpu_custom_call" | custom-call | tf_op jit(solution)/shard_map/leaf_basis/pallas_call | solution.py:350
  101.9 8.0 %node_basis.1 = f32[256,128]{1,0:T(8,128)} custom-call(f32[256,128]{1,0:T(8,128)} %get-tuple-element.69.own_ref, f32[256,128]{1,0:T(8,128)} %copy-done.6, s32[1,128]{1,0:T(1,128)} %broadcast_select_fusion.23.picked_ref), custom_call_target="tpu_custom_call" | custom-call | tf_op jit(solution)/shard_map/node_basis/pallas_call | solution.py:356
  (84 shorter events, 16.1 us)
Async XLA Ops:
  0.6 7.5 %copy-start.8 = (s32[1,128]{1,0:T(1,128)S(1)}, s32[1,128]{1,0:T(1,128)}, u32[]{:S(2)}) copy-start(s32[1,128]{1,0:T(1,128)} %picked_ref.1) | copy-start | bytes 1540
  0.6 7.5 %collective-permute-start = (s32[1,128]{1,0:T(1,128)}, s32[1,128]{1,0:T(1,128)S(1)}, u32[]{:S(2)}, u32[]{:S(2)}) collective-permute-start(s32[1,128]{1,0:T(1,128)} %picked_ref.1), channel_id=1, source_target_pairs={{0,1},{1,0},{2,3},{3,2},{4,5},{5,4},{6,7},{7,6},{8,9},{9,8},{10,11... | collective-permute-start | bytes 1544 | tf_op jit(solution)/shard_map/ppermute | solution.py:213
  8.1 20.3 %collective-permute-start.6 = (f32[512,256]{1,0:T(8,128)}, f32[512,256]{1,0:T(8,128)S(1)}, u32[]{:S(2)}, u32[]{:S(2)}) collective-permute-start(f32[512,256]{1,0:T(8,128)} %get-tuple-element.41), channel_id=1, source_target_pairs={{0,1},{1,0},{2,3},{3,2},{4,5},{5,4},{6,7},{7,6},{8,9},{9,8},{10,11... | collective-permute-start | bytes 1572872 | tf_op jit(solution)/shard_map/ppermute | solution.py:171
  8.2 3.7 %collective-permute-start.1 = (s32[2,128]{1,0:T(2,128)S(1)}, s32[2,128]{1,0:T(2,128)S(1)}, u32[]{:S(2)}, u32[]{:S(2)}) collective-permute-start(s32[2,128]{1,0:T(2,128)S(1)} %add_select_fusion.1), channel_id=1, source_target_pairs={{0,2},{1,3},{2,0},{3,1},{4,6},{5,7},{6,4},{7,5},{8,10},{9,11},{10,... | collective-permute-start | bytes 3080 | tf_op jit(solution)/shard_map/ppermute | solution.py:213
  11.8 4.6 %collective-permute-start.2 = (s32[4,128]{1,0:T(4,128)S(1)}, s32[4,128]{1,0:T(4,128)S(1)}, u32[]{:S(2)}, u32[]{:S(2)}) collective-permute-start(s32[4,128]{1,0:T(4,128)S(1)} %add_select_fusion), channel_id=1, source_target_pairs={{0,4},{1,5},{2,6},{3,7},{4,0},{5,1},{6,2},{7,3},{8,12},{9,13},{10,... | collective-permute-start | bytes 6152 | tf_op jit(solution)/shard_map/ppermute | solution.py:213
  21.6 4.7 %copy-start.10 = (f32[256,256]{1,0:T(8,128)S(1)}, f32[256,256]{1,0:T(8,128)}, u32[]{:S(2)}) copy-start(f32[256,256]{1,0:T(8,128)} %get-tuple-element.44) | copy-start | bytes 786436
  26.3 15.4 %copy-start.3 = (f32[256,256]{1,0:T(8,128)S(1)}, f32[256,256]{1,0:T(8,128)}, u32[]{:S(2)}) copy-start(f32[256,256]{1,0:T(8,128)} %get-tuple-element.49) | copy-start | bytes 786436
  26.3 16.0 %copy-start.5 = (f32[256,256]{1,0:T(8,128)S(1)}, f32[256,256]{1,0:T(8,128)}, u32[]{:S(2)}) copy-start(f32[256,256]{1,0:T(8,128)} %get-tuple-element.43) | copy-start | bytes 786436
  26.3 18.7 %copy-start.9 = (f32[256,256]{1,0:T(8,128)S(1)}, f32[256,256]{1,0:T(8,128)}, u32[]{:S(2)}) copy-start(f32[256,256]{1,0:T(8,128)} %get-tuple-element.55) | copy-start | bytes 786436
  26.3 16.0 %collective-permute-start.7 = (f32[256,256]{1,0:T(8,128)S(1)}, f32[256,256]{1,0:T(8,128)S(1)}, u32[]{:S(2)}, u32[]{:S(2)}) collective-permute-start(f32[256,256]{1,0:T(8,128)S(1)} %copy-done.10), channel_id=1, source_target_pairs={{0,1},{1,0},{2,3},{3,2},{4,5},{5,4},{6,7},{7,6},{8,9},{9,8},{10,11... | collective-permute-start | bytes 786440 | tf_op jit(solution)/shard_map/ppermute | solution.py:171
  28.2 13.5 %collective-permute-start.3 = (f32[256,256]{1,0:T(8,128)}, f32[256,256]{1,0:T(8,128)S(1)}, u32[]{:S(2)}, u32[]{:S(2)}) collective-permute-start(f32[256,256]{1,0:T(8,128)} %get-tuple-element.35), channel_id=1, source_target_pairs={{0,1},{1,0},{2,3},{3,2},{4,5},{5,4},{6,7},{7,6},{8,9},{9,8},{10,11... | collective-permute-start | bytes 786440 | tf_op jit(solution)/shard_map/ppermute | solution.py:171
  28.4 0.8 copy-start
  32.8 9.5 %collective-permute-start.8 = (f32[256,256]{1,0:T(8,128)}, f32[256,256]{1,0:T(8,128)S(1)}, u32[]{:S(2)}, u32[]{:S(2)}) collective-permute-start(f32[256,256]{1,0:T(8,128)} %get-tuple-element.45), channel_id=1, source_target_pairs={{0,2},{1,3},{2,0},{3,1},{4,6},{5,7},{6,4},{7,5},{8,10},{9,11},{10,... | collective-permute-start | bytes 786440 | tf_op jit(solution)/shard_map/ppermute | solution.py:175
  35.5 22.7 %copy-start.2 = (f32[256,256]{1,0:T(8,128)S(1)}, f32[256,256]{1,0:T(8,128)}, u32[]{:S(2)}) copy-start(f32[256,256]{1,0:T(8,128)} %get-tuple-element.53) | copy-start | bytes 786436
  40.2 8.4 %collective-permute-start.10 = (f32[256,256]{1,0:T(8,128)}, f32[256,256]{1,0:T(8,128)S(1)}, u32[]{:S(2)}, u32[]{:S(2)}) collective-permute-start(f32[256,256]{1,0:T(8,128)} %get-tuple-element.48), channel_id=1, source_target_pairs={{0,1},{1,0},{2,3},{3,2},{4,5},{5,4},{6,7},{7,6},{8,9},{9,8},{10,11... | collective-permute-start | bytes 786440 | tf_op jit(solution)/shard_map/ppermute | solution.py:171
  41.8 9.7 %collective-permute-start.12 = (f32[256,256]{1,0:T(8,128)S(1)}, f32[256,256]{1,0:T(8,128)S(1)}, u32[]{:S(2)}, u32[]{:S(2)}) collective-permute-start(f32[256,256]{1,0:T(8,128)S(1)} %add.91), channel_id=1, source_target_pairs={{0,2},{1,3},{2,0},{3,1},{4,6},{5,7},{6,4},{7,5},{8,10},{9,11},{10,... | collective-permute-start | bytes 786440 | tf_op jit(solution)/shard_map/ppermute | solution.py:175
  42.3 9.2 %collective-permute-start.11 = (f32[256,256]{1,0:T(8,128)S(1)}, f32[256,256]{1,0:T(8,128)S(1)}, u32[]{:S(2)}, u32[]{:S(2)}) collective-permute-start(f32[256,256]{1,0:T(8,128)S(1)} %add_add_fusion.2), channel_id=1, source_target_pairs={{0,4},{1,5},{2,6},{3,7},{4,0},{5,1},{6,2},{7,3},{8,12},{9,13},{10,... | collective-permute-start | bytes 786440 | tf_op jit(solution)/shard_map/ppermute | solution.py:175
  45.0 13.2 %collective-permute-start.19 = (f32[256,256]{1,0:T(8,128)S(1)}, f32[256,256]{1,0:T(8,128)S(1)}, u32[]{:S(2)}, u32[]{:S(2)}) collective-permute-start(f32[256,256]{1,0:T(8,128)S(1)} %copy-done.9), channel_id=1, source_target_pairs={{0,1},{1,0},{2,3},{3,2},{4,5},{5,4},{6,7},{7,6},{8,9},{9,8},{10,11... | collective-permute-start | bytes 786440 | tf_op jit(solution)/shard_map/ppermute | solution.py:171
  53.4 5.8 %collective-permute-start.13 = (f32[128,256]{1,0:T(8,128)S(1)}, f32[128,256]{1,0:T(8,128)S(1)}, u32[]{:S(2)}, u32[]{:S(2)}) collective-permute-start(f32[128,256]{1,0:T(8,128)S(1)} %broadcast_select_fusion.3), channel_id=1, source_target_pairs={{0,2},{1,3},{2,0},{3,1},{4,6},{5,7},{6,4},{7,5},{8,10},{9,11},{10,... | collective-permute-start | bytes 393224 | tf_op jit(solution)/shard_map/ppermute | solution.py:175
  56.1 24.6 %collective-permute-start.5 = (f32[256,256]{1,0:T(8,128)}, f32[256,256]{1,0:T(8,128)S(1)}, u32[]{:S(2)}, u32[]{:S(2)}) collective-permute-start(f32[256,256]{1,0:T(8,128)} %get-tuple-element.39), channel_id=1, source_target_pairs={{0,1},{1,0},{2,3},{3,2},{4,5},{5,4},{6,7},{7,6},{8,9},{9,8},{10,11... | collective-permute-start | bytes 786440 | tf_op jit(solution)/shard_map/ppermute | solution.py:171
  57.7 35.2 %collective-permute-start.4 = (f32[256,256]{1,0:T(8,128)}, f32[256,256]{1,0:T(8,128)S(1)}, u32[]{:S(2)}, u32[]{:S(2)}) collective-permute-start(f32[256,256]{1,0:T(8,128)} %get-tuple-element.36), channel_id=1, source_target_pairs={{0,1},{1,0},{2,3},{3,2},{4,5},{5,4},{6,7},{7,6},{8,9},{9,8},{10,11... | collective-permute-start | bytes 786440 | tf_op jit(solution)/shard_map/ppermute | solution.py:171
  58.2 22.5 %copy-start.4 = (f32[256,256]{1,0:T(8,128)S(1)}, f32[256,256]{1,0:T(8,128)}, u32[]{:S(2)}) copy-start(f32[256,256]{1,0:T(8,128)} %get-tuple-element.37) | copy-start | bytes 786436
  58.3 22.4 %collective-permute-start.9 = (f32[256,256]{1,0:T(8,128)}, f32[256,256]{1,0:T(8,128)S(1)}, u32[]{:S(2)}, u32[]{:S(2)}) collective-permute-start(f32[256,256]{1,0:T(8,128)} %get-tuple-element.46), channel_id=1, source_target_pairs={{0,2},{1,3},{2,0},{3,1},{4,6},{5,7},{6,4},{7,5},{8,10},{9,11},{10,... | collective-permute-start | bytes 786440 | tf_op jit(solution)/shard_map/ppermute | solution.py:175
  60.1 10.6 %collective-permute-start.14 = (f32[128,256]{1,0:T(8,128)S(1)}, f32[128,256]{1,0:T(8,128)S(1)}, u32[]{:S(2)}, u32[]{:S(2)}) collective-permute-start(f32[128,256]{1,0:T(8,128)S(1)} %broadcast_select_fusion.2), channel_id=1, source_target_pairs={{0,4},{1,5},{4,0},{5,1},{8,12},{9,13},{12,8},{13,9},{16,20},{17,21... | collective-permute-start | bytes 393224 | tf_op jit(solution)/shard_map/ppermute | solution.py:175
  71.7 4.6 %collective-permute-start.16 = (f32[128,256]{1,0:T(8,128)S(1)}, f32[128,256]{1,0:T(8,128)S(1)}, u32[]{:S(2)}, u32[]{:S(2)}) collective-permute-start(f32[128,256]{1,0:T(8,128)S(1)} %broadcast_select_fusion.1), channel_id=1, source_target_pairs={{0,8},{1,9},{8,0},{9,1},{16,24},{17,25},{24,16},{25,17}} | collective-permute-start | bytes 393224 | tf_op jit(solution)/shard_map/ppermute | solution.py:318
  74.5 12.3 %collective-permute-start.18 = (f32[128,128]{1,0:T(8,128)}, f32[128,128]{1,0:T(8,128)}, u32[]{:S(2)}, u32[]{:S(2)}) collective-permute-start(f32[128,128]{1,0:T(8,128)} %get-tuple-element.81), channel_id=1, source_target_pairs={{0,1},{1,0},{2,3},{3,2},{4,5},{5,4},{6,7},{7,6},{8,9},{9,8},{10,11... | collective-permute-start | bytes 196616 | tf_op jit(solution)/shard_map/ppermute | solution.py:171
  76.3 16.6 %copy-start.1 = (f32[256,256]{1,0:T(8,128)S(1)}, f32[256,256]{1,0:T(8,128)}, u32[]{:S(2)}) copy-start(f32[256,256]{1,0:T(8,128)} %get-tuple-element.33) | copy-start | bytes 786436
  77.2 6.9 %collective-permute-start.17 = (f32[128,256]{1,0:T(8,128)S(1)}, f32[128,256]{1,0:T(8,128)S(1)}, u32[]{:S(2)}, u32[]{:S(2)}) collective-permute-start(f32[128,256]{1,0:T(8,128)S(1)} %broadcast_select_fusion), channel_id=1, source_target_pairs={{0,16},{1,17},{16,0},{17,1}} | collective-permute-start | bytes 393224 | tf_op jit(solution)/shard_map/ppermute | solution.py:318
  81.5 11.4 %collective-permute-start.15 = (f32[256,256]{1,0:T(8,128)}, f32[256,256]{1,0:T(8,128)S(1)}, u32[]{:S(2)}, u32[]{:S(2)}) collective-permute-start(f32[256,256]{1,0:T(8,128)} %add_add_fusion.3), channel_id=1, source_target_pairs={{0,4},{1,5},{2,6},{3,7},{4,0},{5,1},{6,2},{7,3},{8,12},{9,13},{10,... | collective-permute-start | bytes 786440 | tf_op jit(solution)/shard_map/ppermute | solution.py:175
  81.5 11.5 %collective-permute-start.20 = (f32[256,256]{1,0:T(8,128)S(1)}, f32[256,256]{1,0:T(8,128)S(1)}, u32[]{:S(2)}, u32[]{:S(2)}) collective-permute-start(f32[256,256]{1,0:T(8,128)S(1)} %add.105), channel_id=1, source_target_pairs={{0,2},{1,3},{2,0},{3,1},{4,6},{5,7},{6,4},{7,5},{8,10},{9,11},{10,... | collective-permute-start | bytes 786440 | tf_op jit(solution)/shard_map/ppermute | solution.py:175
  86.5 14.7 %collective-permute-start.22 = (f32[256,128]{1,0:T(8,128)S(1)}, f32[256,128]{1,0:T(8,128)S(1)}, u32[]{:S(2)}, u32[]{:S(2)}) collective-permute-start(f32[256,128]{1,0:T(8,128)S(1)} %get-tuple-element.70), channel_id=1, source_target_pairs={{0,1},{1,0},{2,3},{3,2},{4,5},{5,4},{6,7},{7,6},{8,9},{9,8},{10,11... | collective-permute-start | bytes 393224 | tf_op jit(solution)/shard_map/ppermute | solution.py:171
  94.2 4.3 %collective-permute-start.21 = (f32[128,128]{1,0:T(8,128)S(1)}, f32[128,128]{1,0:T(8,128)S(1)}, u32[]{:S(2)}, u32[]{:S(2)}) collective-permute-start(f32[128,128]{1,0:T(8,128)S(1)} %get-tuple-element.79), channel_id=1, source_target_pairs={{0,1},{1,0},{2,3},{3,2},{4,5},{5,4},{6,7},{7,6},{8,9},{9,8},{10,11... | collective-permute-start | bytes 196616 | tf_op jit(solution)/shard_map/ppermute | solution.py:171
  (2 other events, 1.3 us)

commit v3 on v2

--- a/solution.py
+++ b/solution.py
@@ -81,18 +81,18 @@
     out_ref[...] = spd_inverse(own_ref[...] + received_ref[...])
 
 
-def leaf_kernel(own_ref, received_ref, inverse_ref, picked_ref, basis_ref):
-    chosen, others = choices(picked_ref[...], basis_ref.shape[0])
-    solved = dot(own_ref[...] + received_ref[...], inverse_ref[...])
-    basis_ref[...] = chosen + dot(others, solved)
-
-
-def node_kernel(own_ref, received_ref, picked_ref, basis_ref):
-    cross = own_ref[...] + received_ref[...]
+def finish_kernel(
+    node_at, own_ref, received_ref, inverse_ref, picked_ref, table_ref, leaf_ref, node_ref
+):
+    total = own_ref[...] + received_ref[...]
+    rank = total.shape[1]
+    cross = total[rank:]
     index = lax.broadcasted_iota(jnp.int32, cross.shape, 0)
-    choice = (index == picked_ref[...]).astype(jnp.float32)
+    choice = (index == table_ref[pl.ds(node_at[0], 1), :]).astype(jnp.float32)
     gram = dot(choice, cross, ((0,), (0,)))
-    basis_ref[...] = dot(cross, spd_inverse(gram))
+    chosen, others = choices(picked_ref[...], leaf_ref.shape[0])
+    leaf_ref[...] = chosen + dot(others, dot(total[:rank], inverse_ref[...]))
+    node_ref[...] = dot(cross, spd_inverse(gram))
 
 
 def unit_rows(matrix_ref, hit, n_grp):
@@ -243,12 +243,13 @@
     piece = pl.BlockSpec((leaf_rows, half), lambda i, at: (i, 0))
     part = pl.BlockSpec((rank, half), lambda i, at: (i, 0))
     first, second = {}, {}
-    first[top], second[top] = pl.pallas_call(
+    split = pl.pallas_call(
         split_kernel,
         out_shape=(slim,) * 2,
         grid_spec=grid_spec(2, [piece, piece, picked_spec(top)], [part] * 2),
         name="split",
-    )(place, keep, top_received, tables)
+    )
+    first[top], second[top] = split(place, keep, top_received, tables)
 
     for mask in masks[1:]:
         received = across(pieces[mask][0])
@@ -269,7 +270,9 @@
                 value, _ = lax.optimization_barrier((value, gate))
             elif mask ^ bit == 0:
                 early.append(value)
-            arrived = along(value, [(z, z ^ bit) for z in range(spots)])
+            arrived = along(
+                value, [(z, z ^ bit) for z in range(spots)]
+            )
             if gates is not None and mask != top:
                 arrived, _ = lax.optimization_barrier((arrived, gates[2]))
             values[mask ^ bit] = values[mask ^ bit] + arrived
@@ -297,9 +300,9 @@
     gates = []
     low_stack = skeleton_rows
     low_picked = picked_of(1)
-    current = low_rows = jnp.take(low_stack, low_picked, axis=0)
-    low_cross = cross_of(low_stack, low_rows)
-    high_stack, high_picked, high_rows = low_stack, low_picked, low_rows
+    node_own = device >> 1
+    current = jnp.take(low_stack, low_picked, axis=0)
+    low_cross = high_cross = cross_of(low_stack, current)
     even = device - side
     for level in range(2, levels + 1):
         if level <= leaf_bits:
@@ -315,7 +318,8 @@
                 for g in range(0, n_grp, 1 << bit)
                 for s in range(2)
             ]
-            partner = lax.ppermute(current, ("grp", "leaf"), pairs)
+            send = lambda value: lax.ppermute(value, ("grp", "leaf"), pairs)
+            partner = send(current)
             upper = grp_pos >> bit & 1
         stacked = jnp.concatenate(
             [
@@ -329,33 +333,39 @@
         select = even % (1 << level) == 1 << level - 1
         if level == levels:
             select = select | (even == 0)
-        high_stack = jnp.where(select, stacked, high_stack)
-        high_rows = jnp.where(select, current, high_rows)
-        high_picked = jnp.where(select, picked, high_picked)
-    high_cross = cross_of(high_stack, high_rows)
-    own = jnp.where(side == 1, low_cross, high_cross)
-    sent = jnp.where(side == 1, high_cross, low_cross)
-    received = across(sent)
-    own_gram, _ = lax.optimization_barrier((own_gram, sent))
-    square = jax.ShapeDtypeStruct((rank, rank), jnp.float32)
-    inverse = pl.pallas_call(inverse_kernel, out_shape=square, name="inverse")(own_gram, received_gram)
-    node_picked = jnp.where(side == 1, low_picked, high_picked)
-    other_rows = gathered(second, [early[0], gates[-1], inverse])
+        high_cross = jnp.where(select, cross_of(stacked, current), high_cross)
+        node = level_offset(level) + (device >> level)
+        node_own = jnp.where(select & (side == 0), node, node_own)
+
+    other_rows = gathered(second, [early[0], gates[0], current])
     crosses = [
         cross_of(z, r) for z, r in zip((other_rows[:rank], other_rows[rank:]), halves)
     ]
-    own_leaf = jnp.where(side == 0, crosses[0], crosses[1])
-    received_leaf = across(jnp.where(side == 0, crosses[1], crosses[0]))
-    tall = jax.ShapeDtypeStruct((leaf_rows, rank), jnp.float32)
-    leaf_basis = pl.pallas_call(leaf_kernel, out_shape=tall, name="leaf_basis")(
-        own_leaf, received_leaf, inverse, leaf_skeleton
-    )
-
-    received, *_ = lax.optimization_barrier((received, *crosses))
-    tall = jax.ShapeDtypeStruct((2 * rank, rank), jnp.float32)
-    transfer = pl.pallas_call(node_kernel, out_shape=tall, name="node_basis")(
-        own, received, node_picked[None]
-    )
+    own = jnp.concatenate(
+        [
+            jnp.where(side == 0, crosses[0], crosses[1]),
+            jnp.where(side == 1, low_cross, high_cross),
+        ],
+        axis=0,
+    )
+    sent = jnp.concatenate(
+        [
+            jnp.where(side == 0, crosses[1], crosses[0]),
+            jnp.where(side == 1, high_cross, low_cross),
+        ],
+        axis=0,
+    )
+    received = across(sent)
+    square = jax.ShapeDtypeStruct((rank, rank), jnp.float32)
+    inverse = pl.pallas_call(inverse_kernel, out_shape=square, name="inverse")(own_gram, received_gram)
+    tall = [jax.ShapeDtypeStruct((rows, rank), jnp.float32) for rows in (leaf_rows, 2 * rank)]
+    whole = pl.BlockSpec(memory_space=pltpu.VMEM)
+    leaf_basis, transfer = pl.pallas_call(
+        finish_kernel,
+        out_shape=tall,
+        in_specs=[pl.BlockSpec(memory_space=pltpu.SMEM)] + [whole] * 5,
+        name="finish",
+    )(node_own[None], own, received, inverse, leaf_skeleton, node_skeleton)
     return (leaf_basis, transfer[None])
 
 

time: 110 us -> 116 us (1.055)
  waiting for transfers between devices: 18.4 us -> 30.3 us
  Pallas kernels: 37.4 us -> 34.3 us
  starting transfers between devices: 37.1 us -> 35.3 us
  other arithmetic: 6.16 us -> 4.88 us
    ppermute x10 -> x9, waiting for transfers between devices: 3.5 us -> 11.5 us  [across(): return lax.ppermute(value, 'leaf', [(p, p ^ 1) for p in range(n_leaf)])]
    pallas_call x3 -> x2, Pallas kernels: 13.6 us -> 10.8 us  [the longest x1 7.3 us: on_device(): pl.pallas_call(finish_kernel, out_shape=tall, in_specs=[pl.BlockSpec(memo...]
    ppermute x8, waiting for transfers between devices: 9.22 us -> 12 us  [along(): return lax.ppermute(value, 'leaf', pairs)]
    ppermute x10 -> x9, starting transfers between devices: 10.8 us -> 9.33 us  [across(): return lax.ppermute(value, 'leaf', [(p, p ^ 1) for p in range(n_leaf)])]
    select_n x2 -> x1, other arithmetic: 1.47 us -> 0.08 us  [on_device(): current = jnp.take(low_stack, low_picked, axis=0)]
    dot_general x6 -> x9, matrix products: 3.9 us -> 3.63 us  [dot(): lax.dot_general(a, b, (dims, ((), ())), precision=precision, preferred_el...]
  transfers between devices with their start and end apart: 23 -> 22, of which waited for: 9 -> 9; matrix products, arithmetic and copies ran while one was open for 13% -> 10% of each run, Pallas kernels for 27% -> 23%
where the time goes in v3:
time: 116 us; the launch traced here: 115 us
  starting transfers between devices  35.3 us (30%)
  Pallas kernels  34.3 us (30%)
  waiting for transfers between devices  30.3 us (26%)
  local copies, waits for them, and re-layouts  5.95 us (5%)
  other arithmetic  4.88 us (4%)
  matrix products  3.63 us (3%)
    pallas_call x3, Pallas kernels, ordered(): outs = outs(place, matrix, probes, tables)  13.6 us
    ppermute x8, starting transfers between devices, along(): return lax.ppermute(value, 'leaf', pairs)  12.2 us
    ppermute x8, waiting for transfers between devices, along(): return lax.ppermute(value, 'leaf', pairs)  12 us
    ppermute x9, waiting for transfers between devices, across(): return lax.ppermute(value, 'leaf', [(p, p ^ 1) for p in range(n_leaf)])  11.5 us
    ppermute x9, starting transfers between devices, across(): return lax.ppermute(value, 'leaf', [(p, p ^ 1) for p in range(n_leaf)])  9.33 us
    ppermute x3, starting transfers between devices, on_device(): lax.ppermute(skeletons, 'leaf', [(p, p ^ 1 << bit) for p in range(n_leaf)])  8.22 us
    pallas_call x1, Pallas kernels, on_device(): pl.pallas_call(finish_kernel, out_shape=tall, in_specs=[pl.BlockSpec(memo...  7.3 us
    pallas_call x1, Pallas kernels, on_device(): pl.pallas_call(inverse_kernel, out_shape=square, name='inverse')  6.02 us
  transfers between devices with their start and end apart: 22, of which 9 were waited for; matrix products, arithmetic and copies ran while one was open for 10% of the time, Pallas kernels for 23%

profile of v3, /device:TPU:0, one launch (start us, length us, event | category | flops | bytes accessed | tf_op | source)
XLA Modules:
  0.0 115.4 jit_solution(16872862599892830319)
XLA Ops:
  0.6 3.1 %collective-permute-start = (s32[1,128]{1,0:T(1,128)}, s32[1,128]{1,0:T(1,128)S(1)}, u32[]{:S(2)}, u32[]{:S(2)}) collective-permute-start(s32[1,128]{1,0:T(1,128)} %picked_ref.1), channel_id=1, source_target_pairs={{0,1},{1,0},{2,3},{3,2},{4,5},{5,4},{6,7},{7,6},{8,9},{9,8},{10,11... | collective-permute-start | bytes 1544 | tf_op jit(solution)/shard_map/ppermute | solution.py:213
  4.3 3.8 %product.1 = (f32[512,256]{1,0:T(8,128)}, f32[512,256]{1,0:T(8,128)}) custom-call(s32[2]{0:T(128)} %pad_add_fusion.refs_0_.place_ref, bf16[2048,1024]{1,0:T(8,128)(2,1)} %refs_1_.7, bf16[1024,512]{1,0:T(8,128)(2,1)} %refs_2_.7), custom_call_target="tpu_custom_call" | custom-call | tf_op jit(solution)/shard_map/product/pallas_call | solution.py:202
  8.2 2.1 %collective-permute-start.1 = (s32[2,128]{1,0:T(2,128)S(1)}, s32[2,128]{1,0:T(2,128)S(1)}, u32[]{:S(2)}, u32[]{:S(2)}) collective-permute-start(s32[2,128]{1,0:T(2,128)S(1)} %add_select_fusion.1), channel_id=1, source_target_pairs={{0,2},{1,3},{2,0},{3,1},{4,6},{5,7},{6,4},{7,5},{8,10},{9,11},{10,... | collective-permute-start | bytes 3080 | tf_op jit(solution)/shard_map/ppermute | solution.py:213
  10.3 1.6 %collective-permute-done.1 = s32[2,128]{1,0:T(2,128)S(1)} collective-permute-done((s32[2,128]{1,0:T(2,128)S(1)}, s32[2,128]{1,0:T(2,128)S(1)}, u32[]{:S(2)}, u32[]{:S(2)}) %collective-permute-start.1) | collective-permute-done | bytes 1056 | tf_op jit(solution)/shard_map/ppermute | solution.py:213
  11.8 3.0 %collective-permute-start.2 = (s32[4,128]{1,0:T(4,128)S(1)}, s32[4,128]{1,0:T(4,128)S(1)}, u32[]{:S(2)}, u32[]{:S(2)}) collective-permute-start(s32[4,128]{1,0:T(4,128)S(1)} %add_select_fusion), channel_id=1, source_target_pairs={{0,4},{1,5},{2,6},{3,7},{4,0},{5,1},{6,2},{7,3},{8,12},{9,13},{10,... | collective-permute-start | bytes 6152 | tf_op jit(solution)/shard_map/ppermute | solution.py:213
  14.9 1.6 %collective-permute-done.2 = s32[4,128]{1,0:T(4,128)S(1)} collective-permute-done((s32[4,128]{1,0:T(4,128)S(1)}, s32[4,128]{1,0:T(4,128)S(1)}, u32[]{:S(2)}, u32[]{:S(2)}) %collective-permute-start.2) | collective-permute-done | bytes 2080 | tf_op jit(solution)/shard_map/ppermute | solution.py:213
  17.0 4.5 %ordered.5 = (f32[256,256]{1,0:T(8,128)}, f32[256,256]{1,0:T(8,128)}, f32[256,256]{1,0:T(8,128)}, f32[256,256]{1,0:T(8,128)}) custom-call(s32[2]{0:T(128)} %pad_add_fusion.refs_0_.place_ref, bf16[2048,1024]{1,0:T(8,128)(2,1)} %refs_1_.7, bf16[1024,512]{1,0:T(8,128)(2,1)} %refs_2_.7, s32[8,1,128]{2,1,0:T(1,128)} %broadcast_select_fusion.19.refs_3_.picked_ref), custom_call_target="tpu_custom_call" | custom-call | tf_op jit(solution)/shard_map/ordered/pallas_call | solution.py:236
  21.6 4.6 %ordered.4 = (f32[256,256]{1,0:T(8,128)}, f32[256,256]{1,0:T(8,128)}, f32[256,256]{1,0:T(8,128)}, f32[256,256]{1,0:T(8,128)}) custom-call(s32[2]{0:T(128)} %pad_add_fusion.refs_0_.place_ref, bf16[2048,1024]{1,0:T(8,128)(2,1)} %refs_1_.7, bf16[1024,512]{1,0:T(8,128)(2,1)} %refs_2_.7, s32[8,1,128]{2,1,0:T(1,128)} %broadcast_select_fusion.19.refs_3_.picked_ref), custom_call_target="tpu_custom_call" | custom-call | tf_op jit(solution)/shard_map/ordered/pallas_call | solution.py:236
  26.1 1.9 %collective-permute-start.7 = (f32[256,256]{1,0:T(8,128)}, f32[256,256]{1,0:T(8,128)S(1)}, u32[]{:S(2)}, u32[]{:S(2)}) collective-permute-start(f32[256,256]{1,0:T(8,128)} %get-tuple-element.44), channel_id=1, source_target_pairs={{0,1},{1,0},{2,3},{3,2},{4,5},{5,4},{6,7},{7,6},{8,9},{9,8},{10,11... | collective-permute-start | bytes 786440 | tf_op jit(solution)/shard_map/ppermute | solution.py:171
  29.1 3.5 %split.1 = (f32[256,256]{1,0:T(8,128)}, f32[256,256]{1,0:T(8,128)}) custom-call(s32[2]{0:T(128)} %pad_add_fusion.refs_0_.place_ref, f32[512,256]{1,0:T(8,128)} %get-tuple-element.40.keep_ref, f32[512,256]{1,0:T(8,128)} %copy-done, s32[8,1,128]{2,1,0:T(1,128)} %broadcast_select_fusion.19.refs_3_.picked_ref), custom_call_target="tpu_custom_call" | custom-call | tf_op jit(solution)/shard_map/split/pallas_call | solution.py:252
  32.6 1.9 %collective-permute-start.8 = (f32[256,256]{1,0:T(8,128)}, f32[256,256]{1,0:T(8,128)S(1)}, u32[]{:S(2)}, u32[]{:S(2)}) collective-permute-start(f32[256,256]{1,0:T(8,128)} %get-tuple-element.45), channel_id=1, source_target_pairs={{0,2},{1,3},{2,0},{3,1},{4,6},{5,7},{6,4},{7,5},{8,10},{9,11},{10,... | collective-permute-start | bytes 786440 | tf_op jit(solution)/shard_map/ppermute | solution.py:175
  35.4 4.6 %ordered.3 = (f32[256,256]{1,0:T(8,128)}, f32[256,256]{1,0:T(8,128)}, f32[256,256]{1,0:T(8,128)}, f32[256,256]{1,0:T(8,128)}) custom-call(s32[2]{0:T(128)} %pad_add_fusion.refs_0_.place_ref, bf16[2048,1024]{1,0:T(8,128)(2,1)} %refs_1_.7, bf16[1024,512]{1,0:T(8,128)(2,1)} %refs_2_.7, s32[8,1,128]{2,1,0:T(1,128)} %broadcast_select_fusion.19.refs_3_.picked_ref), custom_call_target="tpu_custom_call" | custom-call | tf_op jit(solution)/shard_map/ordered/pallas_call | solution.py:236
  39.9 1.5 %collective-permute-start.10 = (f32[256,256]{1,0:T(8,128)}, f32[256,256]{1,0:T(8,128)S(1)}, u32[]{:S(2)}, u32[]{:S(2)}) collective-permute-start(f32[256,256]{1,0:T(8,128)} %get-tuple-element.48), channel_id=1, source_target_pairs={{0,1},{1,0},{2,3},{3,2},{4,5},{5,4},{6,7},{7,6},{8,9},{9,8},{10,11... | collective-permute-start | bytes 786440 | tf_op jit(solution)/shard_map/ppermute | solution.py:171
  42.2 3.0 %collective-permute-start.11 = (f32[256,256]{1,0:T(8,128)S(1)}, f32[256,256]{1,0:T(8,128)S(1)}, u32[]{:S(2)}, u32[]{:S(2)}) collective-permute-start(f32[256,256]{1,0:T(8,128)S(1)} %add_add_fusion.2), channel_id=1, source_target_pairs={{0,4},{1,5},{2,6},{3,7},{4,0},{5,1},{6,2},{7,3},{8,12},{9,13},{10,... | collective-permute-start | bytes 786440 | tf_op jit(solution)/shard_map/ppermute | solution.py:175
  45.3 1.6 %collective-permute-start.5 = (f32[256,256]{1,0:T(8,128)S(1)}, f32[256,256]{1,0:T(8,128)S(1)}, u32[]{:S(2)}, u32[]{:S(2)}) collective-permute-start(f32[256,256]{1,0:T(8,128)S(1)} %copy-done.9), channel_id=1, source_target_pairs={{0,1},{1,0},{2,3},{3,2},{4,5},{5,4},{6,7},{7,6},{8,9},{9,8},{10,11... | collective-permute-start | bytes 786440 | tf_op jit(solution)/shard_map/ppermute | solution.py:171
  46.9 8.1 %collective-permute-done.18 = f32[256,256]{1,0:T(8,128)S(1)} collective-permute-done((f32[256,256]{1,0:T(8,128)}, f32[256,256]{1,0:T(8,128)S(1)}, u32[]{:S(2)}, u32[]{:S(2)}) %collective-permute-start.18) | collective-permute-done | bytes 262176 | tf_op jit(solution)/shard_map/ppermute | solution.py:171
  54.9 1.5 %collective-permute-start.4 = (f32[256,256]{1,0:T(8,128)}, f32[256,256]{1,0:T(8,128)S(1)}, u32[]{:S(2)}, u32[]{:S(2)}) collective-permute-start(f32[256,256]{1,0:T(8,128)} %get-tuple-element.36), channel_id=1, source_target_pairs={{0,1},{1,0},{2,3},{3,2},{4,5},{5,4},{6,7},{7,6},{8,9},{9,8},{10,11... | collective-permute-start | bytes 786440 | tf_op jit(solution)/shard_map/ppermute | solution.py:171
  57.0 1.0 add_add_fusion.1
  58.9 1.7 %collective-permute-start.13 = (f32[128,256]{1,0:T(8,128)S(1)}, f32[128,256]{1,0:T(8,128)S(1)}, u32[]{:S(2)}, u32[]{:S(2)}) collective-permute-start(f32[128,256]{1,0:T(8,128)S(1)} %broadcast_select_fusion.4), channel_id=1, source_target_pairs={{0,2},{1,3},{2,0},{3,1},{4,6},{5,7},{6,4},{7,5},{8,10},{9,11},{10,... | collective-permute-start | bytes 393224 | tf_op jit(solution)/shard_map/ppermute | solution.py:175
  61.0 3.4 %collective-permute-done.9 = f32[256,256]{1,0:T(8,128)S(1)} collective-permute-done((f32[256,256]{1,0:T(8,128)S(1)}, f32[256,256]{1,0:T(8,128)S(1)}, u32[]{:S(2)}, u32[]{:S(2)}) %collective-permute-start.9) | collective-permute-done | bytes 262176 | tf_op jit(solution)/shard_map/ppermute | solution.py:175
  64.7 5.4 %collective-permute-done.13 = f32[128,256]{1,0:T(8,128)S(1)} collective-permute-done((f32[128,256]{1,0:T(8,128)S(1)}, f32[128,256]{1,0:T(8,128)S(1)}, u32[]{:S(2)}, u32[]{:S(2)}) %collective-permute-start.13) | collective-permute-done | bytes 131104 | tf_op jit(solution)/shard_map/ppermute | solution.py:175
  71.1 2.6 %collective-permute-start.15 = (f32[128,256]{1,0:T(8,128)S(1)}, f32[128,256]{1,0:T(8,128)S(1)}, u32[]{:S(2)}, u32[]{:S(2)}) collective-permute-start(f32[128,256]{1,0:T(8,128)S(1)} %broadcast_select_fusion.3), channel_id=1, source_target_pairs={{0,4},{1,5},{4,0},{5,1},{8,12},{9,13},{12,8},{13,9},{16,20},{17,21... | collective-permute-start | bytes 393224 | tf_op jit(solution)/shard_map/ppermute | solution.py:175
  73.7 2.3 %collective-permute-start.14 = (f32[256,256]{1,0:T(8,128)S(1)}, f32[256,256]{1,0:T(8,128)S(1)}, u32[]{:S(2)}, u32[]{:S(2)}) collective-permute-start(f32[256,256]{1,0:T(8,128)S(1)} %add_add_fusion.3), channel_id=1, source_target_pairs={{0,4},{1,5},{2,6},{3,7},{4,0},{5,1},{6,2},{7,3},{8,12},{9,13},{10,... | collective-permute-start | bytes 786440 | tf_op jit(solution)/shard_map/ppermute | solution.py:175
  76.4 3.1 %collective-permute-done.15 = f32[128,256]{1,0:T(8,128)S(1)} collective-permute-done((f32[128,256]{1,0:T(8,128)S(1)}, f32[128,256]{1,0:T(8,128)S(1)}, u32[]{:S(2)}, u32[]{:S(2)}) %collective-permute-start.15) | collective-permute-done | bytes 131104 | tf_op jit(solution)/shard_map/ppermute | solution.py:175
  80.5 1.9 %collective-permute-start.16 = (f32[128,256]{1,0:T(8,128)S(1)}, f32[128,256]{1,0:T(8,128)S(1)}, u32[]{:S(2)}, u32[]{:S(2)}) collective-permute-start(f32[128,256]{1,0:T(8,128)S(1)} %broadcast_select_fusion.2), channel_id=1, source_target_pairs={{0,8},{1,9},{8,0},{9,1},{16,24},{17,25},{24,16},{25,17}} | collective-permute-start | bytes 393224 | tf_op jit(solution)/shard_map/ppermute | solution.py:321
  82.8 0.9 collective-permute-done.16
  84.7 3.6 %collective-permute-start.17 = (f32[128,256]{1,0:T(8,128)S(1)}, f32[128,256]{1,0:T(8,128)S(1)}, u32[]{:S(2)}, u32[]{:S(2)}) collective-permute-start(f32[128,256]{1,0:T(8,128)S(1)} %broadcast_select_fusion.1), channel_id=1, source_target_pairs={{0,16},{1,17},{16,0},{17,1}} | collective-permute-start | bytes 393224 | tf_op jit(solution)/shard_map/ppermute | solution.py:321
  88.7 2.8 %collective-permute-done.17 = f32[128,256]{1,0:T(8,128)S(1)} collective-permute-done((f32[128,256]{1,0:T(8,128)S(1)}, f32[128,256]{1,0:T(8,128)S(1)}, u32[]{:S(2)}, u32[]{:S(2)}) %collective-permute-start.17) | collective-permute-done | bytes 131104 | tf_op jit(solution)/shard_map/ppermute | solution.py:321
  94.6 2.0 %collective-permute-start.21 = (f32[128,128]{1,0:T(8,128)S(1)}, f32[128,128]{1,0:T(8,128)S(1)}, u32[]{:S(2)}, u32[]{:S(2)}) collective-permute-start(f32[128,128]{1,0:T(8,128)S(1)} %get-tuple-element.79), channel_id=1, source_target_pairs={{0,1},{1,0},{2,3},{3,2},{4,5},{5,4},{6,7},{7,6},{8,9},{9,8},{10,11... | collective-permute-start | bytes 196616 | tf_op jit(solution)/shard_map/ppermute | solution.py:171
  96.6 3.4 %collective-permute-done.21.received_ref = f32[128,128]{1,0:T(8,128)S(1)} collective-permute-done((f32[128,128]{1,0:T(8,128)S(1)}, f32[128,128]{1,0:T(8,128)S(1)}, u32[]{:S(2)}, u32[]{:S(2)}) %collective-permute-start.21) | collective-permute-done | bytes 65568 | tf_op jit(solution)/shard_map/ppermute | solution.py:171
  100.7 6.0 %inverse.1.inverse_ref = f32[128,128]{1,0:T(8,128)} custom-call(f32[128,128]{1,0:T(8,128)} %get-tuple-element.80.own_ref, f32[128,128]{1,0:T(8,128)} %copy-done.7), custom_call_target="tpu_custom_call" | custom-call | tf_op jit(solution)/shard_map/inverse/pallas_call | solution.py:360
  108.1 7.3 %finish.1 = (f32[256,128]{1,0:T(8,128)}, f32[256,128]{1,0:T(8,128)}) custom-call(s32[1]{0:T(128)} %bitcast.node_at, f32[384,128]{1,0:T(8,128)} %pad_maximum_fusion.4.own_ref, f32[384,128]{1,0:T(8,128)} %copy-done.6, f32[128,128]{1,0:T(8,128)} %inverse.1.inverse_ref, s32[1,128]{1,0:T(1,128)} %picked_ref.1, s32[31,128]{1,0:T(8,128)} %table_ref.1), custom_call_target="tpu_custom_call" | custom-call | tf_op jit(solution)/shard_map/finish/pallas_call | solution.py:363
  (86 shorter events, 14.9 us)
Async XLA Ops:
  0.6 7.5 %copy-start.8 = (s32[1,128]{1,0:T(1,128)S(1)}, s32[1,128]{1,0:T(1,128)}, u32[]{:S(2)}) copy-start(s32[1,128]{1,0:T(1,128)} %picked_ref.1) | copy-start | bytes 1540
  0.6 7.5 %collective-permute-start = (s32[1,128]{1,0:T(1,128)}, s32[1,128]{1,0:T(1,128)S(1)}, u32[]{:S(2)}, u32[]{:S(2)}) collective-permute-start(s32[1,128]{1,0:T(1,128)} %picked_ref.1), channel_id=1, source_target_pairs={{0,1},{1,0},{2,3},{3,2},{4,5},{5,4},{6,7},{7,6},{8,9},{9,8},{10,11... | collective-permute-start | bytes 1544 | tf_op jit(solution)/shard_map/ppermute | solution.py:213
  8.1 20.1 %collective-permute-start.6 = (f32[512,256]{1,0:T(8,128)}, f32[512,256]{1,0:T(8,128)S(1)}, u32[]{:S(2)}, u32[]{:S(2)}) collective-permute-start(f32[512,256]{1,0:T(8,128)} %get-tuple-element.41), channel_id=1, source_target_pairs={{0,1},{1,0},{2,3},{3,2},{4,5},{5,4},{6,7},{7,6},{8,9},{9,8},{10,11... | collective-permute-start | bytes 1572872 | tf_op jit(solution)/shard_map/ppermute | solution.py:171
  8.2 3.7 %collective-permute-start.1 = (s32[2,128]{1,0:T(2,128)S(1)}, s32[2,128]{1,0:T(2,128)S(1)}, u32[]{:S(2)}, u32[]{:S(2)}) collective-permute-start(s32[2,128]{1,0:T(2,128)S(1)} %add_select_fusion.1), channel_id=1, source_target_pairs={{0,2},{1,3},{2,0},{3,1},{4,6},{5,7},{6,4},{7,5},{8,10},{9,11},{10,... | collective-permute-start | bytes 3080 | tf_op jit(solution)/shard_map/ppermute | solution.py:213
  11.8 4.6 %collective-permute-start.2 = (s32[4,128]{1,0:T(4,128)S(1)}, s32[4,128]{1,0:T(4,128)S(1)}, u32[]{:S(2)}, u32[]{:S(2)}) collective-permute-start(s32[4,128]{1,0:T(4,128)S(1)} %add_select_fusion), channel_id=1, source_target_pairs={{0,4},{1,5},{2,6},{3,7},{4,0},{5,1},{6,2},{7,3},{8,12},{9,13},{10,... | collective-permute-start | bytes 6152 | tf_op jit(solution)/shard_map/ppermute | solution.py:213
  26.1 15.8 %copy-start.3 = (f32[256,256]{1,0:T(8,128)S(1)}, f32[256,256]{1,0:T(8,128)}, u32[]{:S(2)}) copy-start(f32[256,256]{1,0:T(8,128)} %get-tuple-element.49) | copy-start | bytes 786436
  26.1 16.1 %copy-start.5 = (f32[256,256]{1,0:T(8,128)S(1)}, f32[256,256]{1,0:T(8,128)}, u32[]{:S(2)}) copy-start(f32[256,256]{1,0:T(8,128)} %get-tuple-element.43) | copy-start | bytes 786436
  26.1 19.1 %copy-start.9 = (f32[256,256]{1,0:T(8,128)S(1)}, f32[256,256]{1,0:T(8,128)}, u32[]{:S(2)}) copy-start(f32[256,256]{1,0:T(8,128)} %get-tuple-element.39) | copy-start | bytes 786436
  26.1 30.3 %copy-start.2 = (f32[256,256]{1,0:T(8,128)S(1)}, f32[256,256]{1,0:T(8,128)}, u32[]{:S(2)}) copy-start(f32[256,256]{1,0:T(8,128)} %get-tuple-element.52) | copy-start | bytes 786436
  26.1 16.0 %collective-permute-start.7 = (f32[256,256]{1,0:T(8,128)}, f32[256,256]{1,0:T(8,128)S(1)}, u32[]{:S(2)}, u32[]{:S(2)}) collective-permute-start(f32[256,256]{1,0:T(8,128)} %get-tuple-element.44), channel_id=1, source_target_pairs={{0,1},{1,0},{2,3},{3,2},{4,5},{5,4},{6,7},{7,6},{8,9},{9,8},{10,11... | collective-permute-start | bytes 786440 | tf_op jit(solution)/shard_map/ppermute | solution.py:171
  28.1 13.4 %collective-permute-start.3 = (f32[256,256]{1,0:T(8,128)}, f32[256,256]{1,0:T(8,128)S(1)}, u32[]{:S(2)}, u32[]{:S(2)}) collective-permute-start(f32[256,256]{1,0:T(8,128)} %get-tuple-element.35), channel_id=1, source_target_pairs={{0,1},{1,0},{2,3},{3,2},{4,5},{5,4},{6,7},{7,6},{8,9},{9,8},{10,11... | collective-permute-start | bytes 786440 | tf_op jit(solution)/shard_map/ppermute | solution.py:171
  28.2 0.8 copy-start
  32.6 23.9 %copy-start.10 = (f32[256,256]{1,0:T(8,128)S(1)}, f32[256,256]{1,0:T(8,128)}, u32[]{:S(2)}) copy-start(f32[256,256]{1,0:T(8,128)} %get-tuple-element.46) | copy-start | bytes 786436
  32.6 9.6 %collective-permute-start.8 = (f32[256,256]{1,0:T(8,128)}, f32[256,256]{1,0:T(8,128)S(1)}, u32[]{:S(2)}, u32[]{:S(2)}) collective-permute-start(f32[256,256]{1,0:T(8,128)} %get-tuple-element.45), channel_id=1, source_target_pairs={{0,2},{1,3},{2,0},{3,1},{4,6},{5,7},{6,4},{7,5},{8,10},{9,11},{10,... | collective-permute-start | bytes 786440 | tf_op jit(solution)/shard_map/ppermute | solution.py:175
  39.9 24.5 %copy-start.4 = (f32[256,256]{1,0:T(8,128)S(1)}, f32[256,256]{1,0:T(8,128)}, u32[]{:S(2)}) copy-start(f32[256,256]{1,0:T(8,128)} %get-tuple-element.37) | copy-start | bytes 786436
  39.9 16.6 %collective-permute-start.10 = (f32[256,256]{1,0:T(8,128)}, f32[256,256]{1,0:T(8,128)S(1)}, u32[]{:S(2)}, u32[]{:S(2)}) collective-permute-start(f32[256,256]{1,0:T(8,128)} %get-tuple-element.48), channel_id=1, source_target_pairs={{0,1},{1,0},{2,3},{3,2},{4,5},{5,4},{6,7},{7,6},{8,9},{9,8},{10,11... | collective-permute-start | bytes 786440 | tf_op jit(solution)/shard_map/ppermute | solution.py:171
  41.5 13.5 %collective-permute-start.18 = (f32[256,256]{1,0:T(8,128)}, f32[256,256]{1,0:T(8,128)S(1)}, u32[]{:S(2)}, u32[]{:S(2)}) collective-permute-start(f32[256,256]{1,0:T(8,128)} %get-tuple-element.54), channel_id=1, source_target_pairs={{0,1},{1,0},{2,3},{3,2},{4,5},{5,4},{6,7},{7,6},{8,9},{9,8},{10,11... | collective-permute-start | bytes 786440 | tf_op jit(solution)/shard_map/ppermute | solution.py:171
  42.0 15.0 %collective-permute-start.12 = (f32[256,256]{1,0:T(8,128)S(1)}, f32[256,256]{1,0:T(8,128)S(1)}, u32[]{:S(2)}, u32[]{:S(2)}) collective-permute-start(f32[256,256]{1,0:T(8,128)S(1)} %add.113), channel_id=1, source_target_pairs={{0,2},{1,3},{2,0},{3,1},{4,6},{5,7},{6,4},{7,5},{8,10},{9,11},{10,... | collective-permute-start | bytes 786440 | tf_op jit(solution)/shard_map/ppermute | solution.py:175
  42.2 14.8 %collective-permute-start.11 = (f32[256,256]{1,0:T(8,128)S(1)}, f32[256,256]{1,0:T(8,128)S(1)}, u32[]{:S(2)}, u32[]{:S(2)}) collective-permute-start(f32[256,256]{1,0:T(8,128)S(1)} %add_add_fusion.2), channel_id=1, source_target_pairs={{0,4},{1,5},{2,6},{3,7},{4,0},{5,1},{6,2},{7,3},{8,12},{9,13},{10,... | collective-permute-start | bytes 786440 | tf_op jit(solution)/shard_map/ppermute | solution.py:175
  45.3 15.7 %collective-permute-start.5 = (f32[256,256]{1,0:T(8,128)S(1)}, f32[256,256]{1,0:T(8,128)S(1)}, u32[]{:S(2)}, u32[]{:S(2)}) collective-permute-start(f32[256,256]{1,0:T(8,128)S(1)} %copy-done.9), channel_id=1, source_target_pairs={{0,1},{1,0},{2,3},{3,2},{4,5},{5,4},{6,7},{7,6},{8,9},{9,8},{10,11... | collective-permute-start | bytes 786440 | tf_op jit(solution)/shard_map/ppermute | solution.py:171
  54.9 37.6 %collective-permute-start.4 = (f32[256,256]{1,0:T(8,128)}, f32[256,256]{1,0:T(8,128)S(1)}, u32[]{:S(2)}, u32[]{:S(2)}) collective-permute-start(f32[256,256]{1,0:T(8,128)} %get-tuple-element.36), channel_id=1, source_target_pairs={{0,1},{1,0},{2,3},{3,2},{4,5},{5,4},{6,7},{7,6},{8,9},{9,8},{10,11... | collective-permute-start | bytes 786440 | tf_op jit(solution)/shard_map/ppermute | solution.py:171
  56.5 7.9 %collective-permute-start.9 = (f32[256,256]{1,0:T(8,128)S(1)}, f32[256,256]{1,0:T(8,128)S(1)}, u32[]{:S(2)}, u32[]{:S(2)}) collective-permute-start(f32[256,256]{1,0:T(8,128)S(1)} %copy-done.10), channel_id=1, source_target_pairs={{0,2},{1,3},{2,0},{3,1},{4,6},{5,7},{6,4},{7,5},{8,10},{9,11},{10,... | collective-permute-start | bytes 786440 | tf_op jit(solution)/shard_map/ppermute | solution.py:175
  58.9 11.2 %collective-permute-start.13 = (f32[128,256]{1,0:T(8,128)S(1)}, f32[128,256]{1,0:T(8,128)S(1)}, u32[]{:S(2)}, u32[]{:S(2)}) collective-permute-start(f32[128,256]{1,0:T(8,128)S(1)} %broadcast_select_fusion.4), channel_id=1, source_target_pairs={{0,2},{1,3},{2,0},{3,1},{4,6},{5,7},{6,4},{7,5},{8,10},{9,11},{10,... | collective-permute-start | bytes 393224 | tf_op jit(solution)/shard_map/ppermute | solution.py:175
  71.1 8.4 %collective-permute-start.15 = (f32[128,256]{1,0:T(8,128)S(1)}, f32[128,256]{1,0:T(8,128)S(1)}, u32[]{:S(2)}, u32[]{:S(2)}) collective-permute-start(f32[128,256]{1,0:T(8,128)S(1)} %broadcast_select_fusion.3), channel_id=1, source_target_pairs={{0,4},{1,5},{4,0},{5,1},{8,12},{9,13},{12,8},{13,9},{16,20},{17,21... | collective-permute-start | bytes 393224 | tf_op jit(solution)/shard_map/ppermute | solution.py:175
  73.7 18.8 %collective-permute-start.14 = (f32[256,256]{1,0:T(8,128)S(1)}, f32[256,256]{1,0:T(8,128)S(1)}, u32[]{:S(2)}, u32[]{:S(2)}) collective-permute-start(f32[256,256]{1,0:T(8,128)S(1)} %add_add_fusion.3), channel_id=1, source_target_pairs={{0,4},{1,5},{2,6},{3,7},{4,0},{5,1},{6,2},{7,3},{8,12},{9,13},{10,... | collective-permute-start | bytes 786440 | tf_op jit(solution)/shard_map/ppermute | solution.py:175
  76.0 16.5 %collective-permute-start.19 = (f32[256,256]{1,0:T(8,128)S(1)}, f32[256,256]{1,0:T(8,128)S(1)}, u32[]{:S(2)}, u32[]{:S(2)}) collective-permute-start(f32[256,256]{1,0:T(8,128)S(1)} %add.121), channel_id=1, source_target_pairs={{0,2},{1,3},{2,0},{3,1},{4,6},{5,7},{6,4},{7,5},{8,10},{9,11},{10,... | collective-permute-start | bytes 786440 | tf_op jit(solution)/shard_map/ppermute | solution.py:175
  79.6 13.0 %copy-start.1 = (f32[256,256]{1,0:T(8,128)S(1)}, f32[256,256]{1,0:T(8,128)}, u32[]{:S(2)}) copy-start(f32[256,256]{1,0:T(8,128)} %get-tuple-element.33) | copy-start | bytes 786436
  80.5 3.2 %collective-permute-start.16 = (f32[128,256]{1,0:T(8,128)S(1)}, f32[128,256]{1,0:T(8,128)S(1)}, u32[]{:S(2)}, u32[]{:S(2)}) collective-permute-start(f32[128,256]{1,0:T(8,128)S(1)} %broadcast_select_fusion.2), channel_id=1, source_target_pairs={{0,8},{1,9},{8,0},{9,1},{16,24},{17,25},{24,16},{25,17}} | collective-permute-start | bytes 393224 | tf_op jit(solution)/shard_map/ppermute | solution.py:321
  84.7 6.9 %collective-permute-start.17 = (f32[128,256]{1,0:T(8,128)S(1)}, f32[128,256]{1,0:T(8,128)S(1)}, u32[]{:S(2)}, u32[]{:S(2)}) collective-permute-start(f32[128,256]{1,0:T(8,128)S(1)} %broadcast_select_fusion.1), channel_id=1, source_target_pairs={{0,16},{1,17},{16,0},{17,1}} | collective-permute-start | bytes 393224 | tf_op jit(solution)/shard_map/ppermute | solution.py:321
  93.6 13.8 %collective-permute-start.20 = (f32[384,128]{1,0:T(8,128)S(1)}, f32[384,128]{1,0:T(8,128)S(1)}, u32[]{:S(2)}, u32[]{:S(2)}) collective-permute-start(f32[384,128]{1,0:T(8,128)S(1)} %pad_maximum_fusion.5), channel_id=1, source_target_pairs={{0,1},{1,0},{2,3},{3,2},{4,5},{5,4},{6,7},{7,6},{8,9},{9,8},{10,11... | collective-permute-start | bytes 589832 | tf_op jit(solution)/shard_map/ppermute | solution.py:171
  94.6 5.4 %collective-permute-start.21 = (f32[128,128]{1,0:T(8,128)S(1)}, f32[128,128]{1,0:T(8,128)S(1)}, u32[]{:S(2)}, u32[]{:S(2)}) collective-permute-start(f32[128,128]{1,0:T(8,128)S(1)} %get-tuple-element.79), channel_id=1, source_target_pairs={{0,1},{1,0},{2,3},{3,2},{4,5},{5,4},{6,7},{7,6},{8,9},{9,8},{10,11... | collective-permute-start | bytes 196616 | tf_op jit(solution)/shard_map/ppermute | solution.py:171
  107.4 0.7 copy-start.6
  (1 other events, 0.6 us)

commit v4 on v3

--- a/solution.py
+++ b/solution.py
@@ -110,17 +110,17 @@
     return dot(block, away, precision=None), dot(block, home, precision=None)
 
 
-def plain_kernel(n_leaf, n_grp, mask, place_ref, matrix_ref, probes_ref, send_ref, keep_ref):
-    spot = (place_ref[1] >> 1) ^ mask
-    hit = place_ref[0] * n_leaf + 2 * spot + pl.program_id(0) - place_ref[1] * n_grp
+def plain_kernel(n_leaf, n_grp, mask, matrix_ref, probes_ref, send_ref, keep_ref):
+    spot = (lax.axis_index("leaf") >> 1) ^ mask
+    hit = lax.axis_index("grp") * n_leaf + 2 * spot + pl.program_id(0) - lax.axis_index("leaf") * n_grp
     block = jnp.concatenate(unit_rows(matrix_ref, hit, n_grp), axis=1)
-    send_ref[...], keep_ref[...] = sides(block, probes_ref, place_ref[1] & 1, send_ref.shape[1])
-
-
-def ordered_kernel(n_leaf, n_grp, high, place_ref, matrix_ref, probes_ref, picked_ref, *outs):
+    send_ref[...], keep_ref[...] = sides(block, probes_ref, lax.axis_index("leaf") & 1, send_ref.shape[1])
+
+
+def ordered_kernel(n_leaf, n_grp, high, matrix_ref, probes_ref, picked_ref, *outs):
     step = pl.program_id(0)
-    spot = (place_ref[1] >> 1) ^ (high - step // 2)
-    hit = place_ref[0] * n_leaf + 2 * spot + step % 2 - place_ref[1] * n_grp
+    spot = (lax.axis_index("leaf") >> 1) ^ (high - step // 2)
+    hit = lax.axis_index("grp") * n_leaf + 2 * spot + step % 2 - lax.axis_index("leaf") * n_grp
     rank, half = picked_ref.shape[2], outs[0].shape[1]
     chosen, others = choices(picked_ref[0], matrix_ref.shape[0])
     order = jnp.concatenate([chosen, others], axis=1).astype(jnp.bfloat16)
@@ -131,7 +131,7 @@
         ],
         axis=1,
     )
-    away, home = sides(block, probes_ref, place_ref[1] & 1, half)
+    away, home = sides(block, probes_ref, lax.axis_index("leaf") & 1, half)
     for j in range(len(outs) // 4):
 
         @pl.when(step // 2 == j)
@@ -143,11 +143,18 @@
             outs[4 * j + 3][at, :] = home[rank:]
 
 
-def split_kernel(place_ref, keep_ref, received_ref, picked_ref, first_ref, second_ref):
+def split_kernel(keep_ref, received_ref, picked_ref, first_ref, second_ref):
     total = keep_ref[...] + received_ref[...]
-    chosen, others = choices(picked_ref[0], total.shape[0])
-    first_ref[...] = dot(chosen, total, ((0,), (0,)))
-    second_ref[...] = dot(others, total, ((0,), (0,)))
+    order = jnp.concatenate(choices(picked_ref[0], total.shape[0]), axis=1).astype(jnp.bfloat16)
+    moved = None
+    for _ in range(3):
+        part = total.astype(jnp.bfloat16)
+        total = total - part.astype(jnp.float32)
+        value = dot(order, part, ((0,), (0,)), None)
+        moved = value if moved is None else moved + value
+    rank = first_ref.shape[0]
+    first_ref[...] = moved[:rank]
+    second_ref[...] = moved[rank:]
 
 
 def on_device(matrix, probes, leaf_skeleton, node_skeleton):
@@ -174,39 +181,36 @@
         pairs = [(2 * a + s, 2 * b + s) for a, b in hops for s in range(2)]
         return lax.ppermute(value, "leaf", pairs)
 
-    place = jnp.stack([grp_pos, leaf_pos]).astype(jnp.int32)
     masks = list(range(spots - 1, -1, -1))
     top = masks[0]
     wide = jax.ShapeDtypeStruct((2 * leaf_rows, half), jnp.float32)
     slim = jax.ShapeDtypeStruct((2 * rank, half), jnp.float32)
 
     def leaf_row(high):
-        return lambda i, at: 2 * ((at[1] >> 1) ^ (high - i // 2)) + i % 2
+        return lambda i: 2 * ((lax.axis_index("leaf") >> 1) ^ (high - i // 2)) + i % 2
 
     def grid_spec(count, in_specs, out_specs):
-        return pltpu.PrefetchScalarGridSpec(
-            num_scalar_prefetch=1, grid=(count,), in_specs=in_specs, out_specs=out_specs
-        )
+        return pl.GridSpec(grid=(count,), in_specs=in_specs, out_specs=out_specs)
 
     def matrix_specs(high):
         row = leaf_row(high)
         return [
-            pl.BlockSpec((leaf_rows, col_count), lambda i, at: (row(i, at), 0)),
-            pl.BlockSpec(probes.shape, lambda i, at: (0, 0)),
+            pl.BlockSpec((leaf_rows, col_count), lambda i: (row(i), 0)),
+            pl.BlockSpec(memory_space=pltpu.VMEM),
         ]
 
     def picked_spec(high):
         row = leaf_row(high)
-        return pl.BlockSpec((1, 1, rank), lambda i, at: (row(i, at), 0, 0))
+        return pl.BlockSpec((1, 1, rank), lambda i: (row(i), 0, 0))
 
     send, keep = pl.pallas_call(
         lambda *refs: plain_kernel(n_leaf, n_grp, top, *refs),
         out_shape=(wide,) * 2,
         grid_spec=grid_spec(
-            2, matrix_specs(top), [pl.BlockSpec((leaf_rows, half), lambda i, at: (i, 0))] * 2
+            2, matrix_specs(top), [pl.BlockSpec((leaf_rows, half), lambda i: (i, 0))] * 2
         ),
         name="product",
-    )(place, matrix, probes)
+    )(matrix, probes)
 
     skeletons = leaf_skeleton
     for bit in range(leaf_bits):
@@ -229,19 +233,19 @@
             grid_spec=grid_spec(
                 2 * count,
                 [*matrix_specs(high), picked_spec(high)],
-                [pl.BlockSpec(slim.shape, lambda i, at: (0, 0))] * (4 * count),
+                [pl.BlockSpec(slim.shape, lambda i: (0, 0))] * (4 * count),
             ),
             name="ordered",
         )
-        outs = outs(place, matrix, probes, tables)
+        outs = outs(matrix, probes, tables)
         return {mask: outs[4 * j : 4 * j + 4] for j, mask in enumerate(group)}
 
     pieces = {}
     for at in range(1, spots, GROUP):
         pieces.update(ordered(masks[at : at + GROUP]))
 
-    piece = pl.BlockSpec((leaf_rows, half), lambda i, at: (i, 0))
-    part = pl.BlockSpec((rank, half), lambda i, at: (i, 0))
+    piece = pl.BlockSpec((leaf_rows, half), lambda i: (i, 0))
+    part = pl.BlockSpec((rank, half), lambda i: (i, 0))
     first, second = {}, {}
     split = pl.pallas_call(
         split_kernel,
@@ -249,7 +253,7 @@
         grid_spec=grid_spec(2, [piece, piece, picked_spec(top)], [part] * 2),
         name="split",
     )
-    first[top], second[top] = split(place, keep, top_received, tables)
+    first[top], second[top] = split(keep, top_received, tables)
 
     for mask in masks[1:]:
         received = across(pieces[mask][0])
@@ -298,10 +302,15 @@
         return lax.dynamic_slice_in_dim(node_skeleton, node, 1, 0)[0]
 
     gates = []
+
+    def taken(stacked, picked):
+        index = jnp.arange(stacked.shape[0], dtype=jnp.int32)
+        return dot((picked[:, None] == index[None, :]).astype(jnp.float32), stacked)
+
     low_stack = skeleton_rows
     low_picked = picked_of(1)
     node_own = device >> 1
-    current = jnp.take(low_stack, low_picked, axis=0)
+    current = taken(low_stack, low_picked)
     low_cross = high_cross = cross_of(low_stack, current)
     even = device - side
     for level in range(2, levels + 1):
@@ -329,7 +338,7 @@
             axis=0,
         )
         picked = picked_of(level)
-        current = jnp.take(stacked, picked, axis=0)
+        current = taken(stacked, picked)
         select = even % (1 << level) == 1 << level - 1
         if level == levels:
             select = select | (even == 0)

time: 116 us -> 108 us (0.931)
  Pallas kernels: 34.3 us -> 30.7 us
  local copies, waits for them, and re-layouts: 5.95 us -> 2.98 us
  other arithmetic: 4.88 us -> 2.65 us
  matrix products: 3.63 us -> 4.96 us
    gather x5 -> x0, local copies, waits for them, and re-layouts: 3.77 us -> none  [the longest x4 3.02 us: on_device(): current = jnp.take(stacked, picked, axis=0)]
    ppermute x9, waiting for transfers between devices: 11.5 us -> 8.54 us  [across(): return lax.ppermute(value, 'leaf', [(p, p ^ 1) for p in range(n_leaf)])]
    pallas_call x4, Pallas kernels: 17.2 us -> 14.2 us  [the longest x3 11.7 us: ordered(): outs = outs(matrix, probes, tables)]
    ppermute x8, waiting for transfers between devices: 12 us -> 14.2 us  [along(): return lax.ppermute(value, 'leaf', pairs)]
    dot_general x9 -> x14, matrix products: 3.63 us -> 4.96 us  [dot(): lax.dot_general(a, b, (dims, ((), ())), precision=precision, preferred_el...]
  transfers between devices with their start and end apart: 22 -> 22, of which waited for: 9 -> 10; matrix products, arithmetic and copies ran while one was open for 10% -> 7% of each run, Pallas kernels for 23% -> 22%
where the time goes in v4:
time: 108 us; the launch traced here: 107 us
  starting transfers between devices  34.5 us (32%)
  Pallas kernels  30.7 us (28%)
  waiting for transfers between devices  30.5 us (28%)
  matrix products  4.96 us (5%)
  local copies, waits for them, and re-layouts  2.98 us (3%)
  other arithmetic  2.65 us (2%)
    ppermute x8, waiting for transfers between devices, along(): return lax.ppermute(value, 'leaf', pairs)  14.2 us
    ppermute x8, starting transfers between devices, along(): return lax.ppermute(value, 'leaf', pairs)  11.9 us
    pallas_call x3, Pallas kernels, ordered(): outs = outs(matrix, probes, tables)  11.7 us
    ppermute x9, starting transfers between devices, across(): return lax.ppermute(value, 'leaf', [(p, p ^ 1) for p in range(n_leaf)])  9.81 us
    ppermute x9, waiting for transfers between devices, across(): return lax.ppermute(value, 'leaf', [(p, p ^ 1) for p in range(n_leaf)])  8.54 us
    pallas_call x1, Pallas kernels, on_device(): pl.pallas_call(finish_kernel, out_shape=tall, in_specs=[pl.BlockSpec(memo...  7.3 us
    ppermute x3, starting transfers between devices, on_device(): lax.ppermute(skeletons, 'leaf', [(p, p ^ 1 << bit) for p in range(n_leaf)])  7.29 us
    pallas_call x1, Pallas kernels, on_device(): pl.pallas_call(inverse_kernel, out_shape=square, name='inverse')  6.02 us
  transfers between devices with their start and end apart: 22, of which 10 were waited for; matrix products, arithmetic and copies ran while one was open for 7% of the time, Pallas kernels for 22%

profile of v4, /device:TPU:0, one launch (start us, length us, event | category | flops | bytes accessed | tf_op | source)
XLA Modules:
  0.0 107.2 jit_solution(15637751378907377983)
XLA Ops:
  0.6 3.1 %collective-permute-start = (s32[1,128]{1,0:T(1,128)}, s32[1,128]{1,0:T(1,128)S(1)}, u32[]{:S(2)}, u32[]{:S(2)}) collective-permute-start(s32[1,128]{1,0:T(1,128)} %picked_ref.1), channel_id=1, source_target_pairs={{0,1},{1,0},{2,3},{3,2},{4,5},{5,4},{6,7},{7,6},{8,9},{9,8},{10,11... | collective-permute-start | bytes 1544 | tf_op jit(solution)/shard_map/ppermute | solution.py:217
  3.7 3.1 %product.1 = (f32[512,256]{1,0:T(8,128)}, f32[512,256]{1,0:T(8,128)}) custom-call(bf16[2048,1024]{1,0:T(8,128)(2,1)} %refs_0_.7, bf16[1024,512]{1,0:T(8,128)(2,1)} %refs_1_.7), custom_call_target="tpu_custom_call" | custom-call | tf_op jit(solution)/shard_map/product/pallas_call | solution.py:206
  7.4 1.6 %collective-permute-start.1 = (s32[2,128]{1,0:T(2,128)S(1)}, s32[2,128]{1,0:T(2,128)S(1)}, u32[]{:S(2)}, u32[]{:S(2)}) collective-permute-start(s32[2,128]{1,0:T(2,128)S(1)} %add_select_fusion.1), channel_id=1, source_target_pairs={{0,2},{1,3},{2,0},{3,1},{4,6},{5,7},{6,4},{7,5},{8,10},{9,11},{10,... | collective-permute-start | bytes 3080 | tf_op jit(solution)/shard_map/ppermute | solution.py:217
  9.1 2.0 %collective-permute-done.1 = s32[2,128]{1,0:T(2,128)S(1)} collective-permute-done((s32[2,128]{1,0:T(2,128)S(1)}, s32[2,128]{1,0:T(2,128)S(1)}, u32[]{:S(2)}, u32[]{:S(2)}) %collective-permute-start.1) | collective-permute-done | bytes 1056 | tf_op jit(solution)/shard_map/ppermute | solution.py:217
  11.1 2.6 %collective-permute-start.2 = (s32[4,128]{1,0:T(4,128)S(1)}, s32[4,128]{1,0:T(4,128)S(1)}, u32[]{:S(2)}, u32[]{:S(2)}) collective-permute-start(s32[4,128]{1,0:T(4,128)S(1)} %add_select_fusion), channel_id=1, source_target_pairs={{0,4},{1,5},{2,6},{3,7},{4,0},{5,1},{6,2},{7,3},{8,12},{9,13},{10,... | collective-permute-start | bytes 6152 | tf_op jit(solution)/shard_map/ppermute | solution.py:217
  13.7 1.9 %collective-permute-done.2 = s32[4,128]{1,0:T(4,128)S(1)} collective-permute-done((s32[4,128]{1,0:T(4,128)S(1)}, s32[4,128]{1,0:T(4,128)S(1)}, u32[]{:S(2)}, u32[]{:S(2)}) %collective-permute-start.2) | collective-permute-done | bytes 2080 | tf_op jit(solution)/shard_map/ppermute | solution.py:217
  16.1 3.9 %ordered.4 = (f32[256,256]{1,0:T(8,128)}, f32[256,256]{1,0:T(8,128)}, f32[256,256]{1,0:T(8,128)}, f32[256,256]{1,0:T(8,128)}) custom-call(bf16[2048,1024]{1,0:T(8,128)(2,1)} %refs_0_.7, bf16[1024,512]{1,0:T(8,128)(2,1)} %refs_1_.7, s32[8,1,128]{2,1,0:T(1,128)} %broadcast_select_fusion.14.refs_2_.picked_ref), custom_call_target="tpu_custom_call" | custom-call | tf_op jit(solution)/shard_map/ordered/pallas_call | solution.py:240
  20.1 1.5 %collective-permute-start.3 = (f32[256,256]{1,0:T(8,128)}, f32[256,256]{1,0:T(8,128)S(1)}, u32[]{:S(2)}, u32[]{:S(2)}) collective-permute-start(f32[256,256]{1,0:T(8,128)} %get-tuple-element.34), channel_id=1, source_target_pairs={{0,1},{1,0},{2,3},{3,2},{4,5},{5,4},{6,7},{7,6},{8,9},{9,8},{10,11... | collective-permute-start | bytes 786440 | tf_op jit(solution)/shard_map/ppermute | solution.py:178
  21.5 3.9 %ordered.5 = (f32[256,256]{1,0:T(8,128)}, f32[256,256]{1,0:T(8,128)}, f32[256,256]{1,0:T(8,128)}, f32[256,256]{1,0:T(8,128)}) custom-call(bf16[2048,1024]{1,0:T(8,128)(2,1)} %refs_0_.7, bf16[1024,512]{1,0:T(8,128)(2,1)} %refs_1_.7, s32[8,1,128]{2,1,0:T(1,128)} %broadcast_select_fusion.14.refs_2_.picked_ref), custom_call_target="tpu_custom_call" | custom-call | tf_op jit(solution)/shard_map/ordered/pallas_call | solution.py:240
  26.9 2.5 %split.1 = (f32[256,256]{1,0:T(8,128)}, f32[256,256]{1,0:T(8,128)}) custom-call(f32[512,256]{1,0:T(8,128)} %get-tuple-element.39.keep_ref, f32[512,256]{1,0:T(8,128)} %copy-done, s32[8,1,128]{2,1,0:T(1,128)} %broadcast_select_fusion.14.refs_2_.picked_ref), custom_call_target="tpu_custom_call" | custom-call | tf_op jit(solution)/shard_map/split/pallas_call | solution.py:256
  29.4 1.6 %collective-permute-start.8 = (f32[256,256]{1,0:T(8,128)}, f32[256,256]{1,0:T(8,128)S(1)}, u32[]{:S(2)}, u32[]{:S(2)}) collective-permute-start(f32[256,256]{1,0:T(8,128)} %get-tuple-element.44), channel_id=1, source_target_pairs={{0,2},{1,3},{2,0},{3,1},{4,6},{5,7},{6,4},{7,5},{8,10},{9,11},{10,... | collective-permute-start | bytes 786440 | tf_op jit(solution)/shard_map/ppermute | solution.py:182
  31.1 3.9 %ordered.3 = (f32[256,256]{1,0:T(8,128)}, f32[256,256]{1,0:T(8,128)}, f32[256,256]{1,0:T(8,128)}, f32[256,256]{1,0:T(8,128)}) custom-call(bf16[2048,1024]{1,0:T(8,128)(2,1)} %refs_0_.7, bf16[1024,512]{1,0:T(8,128)(2,1)} %refs_1_.7, s32[8,1,128]{2,1,0:T(1,128)} %broadcast_select_fusion.14.refs_2_.picked_ref), custom_call_target="tpu_custom_call" | custom-call | tf_op jit(solution)/shard_map/ordered/pallas_call | solution.py:240
  35.0 1.5 %collective-permute-start.10 = (f32[256,256]{1,0:T(8,128)}, f32[256,256]{1,0:T(8,128)S(1)}, u32[]{:S(2)}, u32[]{:S(2)}) collective-permute-start(f32[256,256]{1,0:T(8,128)} %get-tuple-element.47), channel_id=1, source_target_pairs={{0,1},{1,0},{2,3},{3,2},{4,5},{5,4},{6,7},{7,6},{8,9},{9,8},{10,11... | collective-permute-start | bytes 786440 | tf_op jit(solution)/shard_map/ppermute | solution.py:178
  37.6 2.2 %collective-permute-done.8 = f32[256,256]{1,0:T(8,128)S(1)} collective-permute-done((f32[256,256]{1,0:T(8,128)}, f32[256,256]{1,0:T(8,128)S(1)}, u32[]{:S(2)}, u32[]{:S(2)}) %collective-permute-start.8) | collective-permute-done | bytes 262176 | tf_op jit(solution)/shard_map/ppermute | solution.py:182
  39.8 2.7 %collective-permute-start.11 = (f32[256,256]{1,0:T(8,128)S(1)}, f32[256,256]{1,0:T(8,128)S(1)}, u32[]{:S(2)}, u32[]{:S(2)}) collective-permute-start(f32[256,256]{1,0:T(8,128)S(1)} %add_add_fusion.2), channel_id=1, source_target_pairs={{0,4},{1,5},{2,6},{3,7},{4,0},{5,1},{6,2},{7,3},{8,12},{9,13},{10,... | collective-permute-start | bytes 786440 | tf_op jit(solution)/shard_map/ppermute | solution.py:182
  43.3 1.6 %collective-permute-start.5 = (f32[256,256]{1,0:T(8,128)S(1)}, f32[256,256]{1,0:T(8,128)S(1)}, u32[]{:S(2)}, u32[]{:S(2)}) collective-permute-start(f32[256,256]{1,0:T(8,128)S(1)} %copy-done.9), channel_id=1, source_target_pairs={{0,1},{1,0},{2,3},{3,2},{4,5},{5,4},{6,7},{7,6},{8,9},{9,8},{10,11... | collective-permute-start | bytes 786440 | tf_op jit(solution)/shard_map/ppermute | solution.py:178
  44.9 5.1 %collective-permute-done.18 = f32[256,256]{1,0:T(8,128)S(1)} collective-permute-done((f32[256,256]{1,0:T(8,128)}, f32[256,256]{1,0:T(8,128)S(1)}, u32[]{:S(2)}, u32[]{:S(2)}) %collective-permute-start.18) | collective-permute-done | bytes 262176 | tf_op jit(solution)/shard_map/ppermute | solution.py:178
  50.0 1.5 %collective-permute-start.4 = (f32[256,256]{1,0:T(8,128)}, f32[256,256]{1,0:T(8,128)S(1)}, u32[]{:S(2)}, u32[]{:S(2)}) collective-permute-start(f32[256,256]{1,0:T(8,128)} %get-tuple-element.35), channel_id=1, source_target_pairs={{0,1},{1,0},{2,3},{3,2},{4,5},{5,4},{6,7},{7,6},{8,9},{9,8},{10,11... | collective-permute-start | bytes 786440 | tf_op jit(solution)/shard_map/ppermute | solution.py:178
  52.0 1.0 add_add_fusion.1
  53.3 1.7 %collective-permute-start.13 = (f32[128,256]{1,0:T(8,128)S(1)}, f32[128,256]{1,0:T(8,128)S(1)}, u32[]{:S(2)}, u32[]{:S(2)}) collective-permute-start(f32[128,256]{1,0:T(8,128)S(1)} %fusion.8), channel_id=1, source_target_pairs={{0,2},{1,3},{2,0},{3,1},{4,6},{5,7},{6,4},{7,5},{8,10},{9,11},{10,... | collective-permute-start | bytes 393224 | tf_op jit(solution)/shard_map/ppermute | solution.py:182
  55.4 3.2 %collective-permute-done.9 = f32[256,256]{1,0:T(8,128)S(1)} collective-permute-done((f32[256,256]{1,0:T(8,128)S(1)}, f32[256,256]{1,0:T(8,128)S(1)}, u32[]{:S(2)}, u32[]{:S(2)}) %collective-permute-start.9) | collective-permute-done | bytes 262176 | tf_op jit(solution)/shard_map/ppermute | solution.py:182
  58.9 5.9 %collective-permute-done.13 = f32[128,256]{1,0:T(8,128)S(1)} collective-permute-done((f32[128,256]{1,0:T(8,128)S(1)}, f32[128,256]{1,0:T(8,128)S(1)}, u32[]{:S(2)}, u32[]{:S(2)}) %collective-permute-start.13) | collective-permute-done | bytes 131104 | tf_op jit(solution)/shard_map/ppermute | solution.py:182
  65.1 3.3 %collective-permute-start.15 = (f32[128,256]{1,0:T(8,128)S(1)}, f32[128,256]{1,0:T(8,128)S(1)}, u32[]{:S(2)}, u32[]{:S(2)}) collective-permute-start(f32[128,256]{1,0:T(8,128)S(1)} %fusion.3), channel_id=1, source_target_pairs={{0,4},{1,5},{4,0},{5,1},{8,12},{9,13},{12,8},{13,9},{16,20},{17,21... | collective-permute-start | bytes 393224 | tf_op jit(solution)/shard_map/ppermute | solution.py:182
  68.4 1.6 %collective-permute-start.14 = (f32[256,256]{1,0:T(8,128)S(1)}, f32[256,256]{1,0:T(8,128)S(1)}, u32[]{:S(2)}, u32[]{:S(2)}) collective-permute-start(f32[256,256]{1,0:T(8,128)S(1)} %add_add_fusion.3), channel_id=1, source_target_pairs={{0,4},{1,5},{2,6},{3,7},{4,0},{5,1},{6,2},{7,3},{8,12},{9,13},{10,... | collective-permute-start | bytes 786440 | tf_op jit(solution)/shard_map/ppermute | solution.py:182
  70.4 3.0 %collective-permute-done.15 = f32[128,256]{1,0:T(8,128)S(1)} collective-permute-done((f32[128,256]{1,0:T(8,128)S(1)}, f32[128,256]{1,0:T(8,128)S(1)}, u32[]{:S(2)}, u32[]{:S(2)}) %collective-permute-start.15) | collective-permute-done | bytes 131104 | tf_op jit(solution)/shard_map/ppermute | solution.py:182
  73.7 1.9 %collective-permute-start.16 = (f32[128,256]{1,0:T(8,128)S(1)}, f32[128,256]{1,0:T(8,128)S(1)}, u32[]{:S(2)}, u32[]{:S(2)}) collective-permute-start(f32[128,256]{1,0:T(8,128)S(1)} %fusion.2), channel_id=1, source_target_pairs={{0,8},{1,9},{8,0},{9,1},{16,24},{17,25},{24,16},{25,17}} | collective-permute-start | bytes 393224 | tf_op jit(solution)/shard_map/ppermute | solution.py:330
  77.2 3.5 %collective-permute-start.17 = (f32[128,256]{1,0:T(8,128)S(1)}, f32[128,256]{1,0:T(8,128)S(1)}, u32[]{:S(2)}, u32[]{:S(2)}) collective-permute-start(f32[128,256]{1,0:T(8,128)S(1)} %fusion.1), channel_id=1, source_target_pairs={{0,16},{1,17},{16,0},{17,1}} | collective-permute-start | bytes 393224 | tf_op jit(solution)/shard_map/ppermute | solution.py:330
  81.1 2.9 %collective-permute-done.17 = f32[128,256]{1,0:T(8,128)S(1)} collective-permute-done((f32[128,256]{1,0:T(8,128)S(1)}, f32[128,256]{1,0:T(8,128)S(1)}, u32[]{:S(2)}, u32[]{:S(2)}) %collective-permute-start.17) | collective-permute-done | bytes 131104 | tf_op jit(solution)/shard_map/ppermute | solution.py:330
  86.5 2.0 %collective-permute-start.21 = (f32[128,128]{1,0:T(8,128)S(1)}, f32[128,128]{1,0:T(8,128)S(1)}, u32[]{:S(2)}, u32[]{:S(2)}) collective-permute-start(f32[128,128]{1,0:T(8,128)S(1)} %get-tuple-element.68), channel_id=1, source_target_pairs={{0,1},{1,0},{2,3},{3,2},{4,5},{5,4},{6,7},{7,6},{8,9},{9,8},{10,11... | collective-permute-start | bytes 196616 | tf_op jit(solution)/shard_map/ppermute | solution.py:178
  88.5 3.4 %collective-permute-done.21.received_ref = f32[128,128]{1,0:T(8,128)S(1)} collective-permute-done((f32[128,128]{1,0:T(8,128)S(1)}, f32[128,128]{1,0:T(8,128)S(1)}, u32[]{:S(2)}, u32[]{:S(2)}) %collective-permute-start.21) | collective-permute-done | bytes 65568 | tf_op jit(solution)/shard_map/ppermute | solution.py:178
  92.5 6.0 %inverse.1.inverse_ref = f32[128,128]{1,0:T(8,128)} custom-call(f32[128,128]{1,0:T(8,128)} %get-tuple-element.69.own_ref, f32[128,128]{1,0:T(8,128)} %copy-done.7), custom_call_target="tpu_custom_call" | custom-call | tf_op jit(solution)/shard_map/inverse/pallas_call | solution.py:369
  99.9 7.3 %finish.1 = (f32[256,128]{1,0:T(8,128)}, f32[256,128]{1,0:T(8,128)}) custom-call(s32[1]{0:T(128)} %bitcast.node_at, f32[384,128]{1,0:T(8,128)} %pad_maximum_fusion.12.own_ref, f32[384,128]{1,0:T(8,128)} %copy-done.6, f32[128,128]{1,0:T(8,128)} %inverse.1.inverse_ref, s32[1,128]{1,0:T(1,128)} %picked_ref.1, s32[31,128]{1,0:T(8,128)} %table_ref.1), custom_call_target="tpu_custom_call" | custom-call | tf_op jit(solution)/shard_map/finish/pallas_call | solution.py:372
  (71 shorter events, 13.3 us)
Async XLA Ops:
  0.6 6.8 %copy-start.8 = (s32[1,128]{1,0:T(1,128)S(1)}, s32[1,128]{1,0:T(1,128)}, u32[]{:S(2)}) copy-start(s32[1,128]{1,0:T(1,128)} %picked_ref.1) | copy-start | bytes 1540
  0.6 6.2 %collective-permute-start = (s32[1,128]{1,0:T(1,128)}, s32[1,128]{1,0:T(1,128)S(1)}, u32[]{:S(2)}, u32[]{:S(2)}) collective-permute-start(s32[1,128]{1,0:T(1,128)} %picked_ref.1), channel_id=1, source_target_pairs={{0,1},{1,0},{2,3},{3,2},{4,5},{5,4},{6,7},{7,6},{8,9},{9,8},{10,11... | collective-permute-start | bytes 1544 | tf_op jit(solution)/shard_map/ppermute | solution.py:217
  6.8 19.2 %collective-permute-start.6 = (f32[512,256]{1,0:T(8,128)}, f32[512,256]{1,0:T(8,128)S(1)}, u32[]{:S(2)}, u32[]{:S(2)}) collective-permute-start(f32[512,256]{1,0:T(8,128)} %get-tuple-element.40), channel_id=1, source_target_pairs={{0,1},{1,0},{2,3},{3,2},{4,5},{5,4},{6,7},{7,6},{8,9},{9,8},{10,11... | collective-permute-start | bytes 1572872 | tf_op jit(solution)/shard_map/ppermute | solution.py:178
  7.4 3.6 %collective-permute-start.1 = (s32[2,128]{1,0:T(2,128)S(1)}, s32[2,128]{1,0:T(2,128)S(1)}, u32[]{:S(2)}, u32[]{:S(2)}) collective-permute-start(s32[2,128]{1,0:T(2,128)S(1)} %add_select_fusion.1), channel_id=1, source_target_pairs={{0,2},{1,3},{2,0},{3,1},{4,6},{5,7},{6,4},{7,5},{8,10},{9,11},{10,... | collective-permute-start | bytes 3080 | tf_op jit(solution)/shard_map/ppermute | solution.py:217
  11.1 4.5 %collective-permute-start.2 = (s32[4,128]{1,0:T(4,128)S(1)}, s32[4,128]{1,0:T(4,128)S(1)}, u32[]{:S(2)}, u32[]{:S(2)}) collective-permute-start(s32[4,128]{1,0:T(4,128)S(1)} %add_select_fusion), channel_id=1, source_target_pairs={{0,4},{1,5},{2,6},{3,7},{4,0},{5,1},{6,2},{7,3},{8,12},{9,13},{10,... | collective-permute-start | bytes 6152 | tf_op jit(solution)/shard_map/ppermute | solution.py:217
  20.1 16.4 %collective-permute-start.3 = (f32[256,256]{1,0:T(8,128)}, f32[256,256]{1,0:T(8,128)S(1)}, u32[]{:S(2)}, u32[]{:S(2)}) collective-permute-start(f32[256,256]{1,0:T(8,128)} %get-tuple-element.34), channel_id=1, source_target_pairs={{0,1},{1,0},{2,3},{3,2},{4,5},{5,4},{6,7},{7,6},{8,9},{9,8},{10,11... | collective-permute-start | bytes 786440 | tf_op jit(solution)/shard_map/ppermute | solution.py:178
  25.4 11.6 %copy-start.3 = (f32[256,256]{1,0:T(8,128)S(1)}, f32[256,256]{1,0:T(8,128)}, u32[]{:S(2)}) copy-start(f32[256,256]{1,0:T(8,128)} %get-tuple-element.48) | copy-start | bytes 786436
  25.4 14.3 %copy-start.5 = (f32[256,256]{1,0:T(8,128)S(1)}, f32[256,256]{1,0:T(8,128)}, u32[]{:S(2)}) copy-start(f32[256,256]{1,0:T(8,128)} %get-tuple-element.42) | copy-start | bytes 786436
  25.4 17.9 %copy-start.9 = (f32[256,256]{1,0:T(8,128)S(1)}, f32[256,256]{1,0:T(8,128)}, u32[]{:S(2)}) copy-start(f32[256,256]{1,0:T(8,128)} %get-tuple-element.38) | copy-start | bytes 786436
  25.4 26.0 %copy-start.2 = (f32[256,256]{1,0:T(8,128)S(1)}, f32[256,256]{1,0:T(8,128)}, u32[]{:S(2)}) copy-start(f32[256,256]{1,0:T(8,128)} %get-tuple-element.51) | copy-start | bytes 786436
  25.4 12.1 %collective-permute-start.7 = (f32[256,256]{1,0:T(8,128)}, f32[256,256]{1,0:T(8,128)S(1)}, u32[]{:S(2)}, u32[]{:S(2)}) collective-permute-start(f32[256,256]{1,0:T(8,128)} %get-tuple-element.43), channel_id=1, source_target_pairs={{0,1},{1,0},{2,3},{3,2},{4,5},{5,4},{6,7},{7,6},{8,9},{9,8},{10,11... | collective-permute-start | bytes 786440 | tf_op jit(solution)/shard_map/ppermute | solution.py:178
  26.1 0.8 copy-start
  29.4 22.1 %copy-start.10 = (f32[256,256]{1,0:T(8,128)S(1)}, f32[256,256]{1,0:T(8,128)}, u32[]{:S(2)}) copy-start(f32[256,256]{1,0:T(8,128)} %get-tuple-element.45) | copy-start | bytes 786436
  29.4 29.2 %copy-start.4 = (f32[256,256]{1,0:T(8,128)S(1)}, f32[256,256]{1,0:T(8,128)}, u32[]{:S(2)}) copy-start(f32[256,256]{1,0:T(8,128)} %get-tuple-element.36) | copy-start | bytes 786436
  29.4 10.3 %collective-permute-start.8 = (f32[256,256]{1,0:T(8,128)}, f32[256,256]{1,0:T(8,128)S(1)}, u32[]{:S(2)}, u32[]{:S(2)}) collective-permute-start(f32[256,256]{1,0:T(8,128)} %get-tuple-element.44), channel_id=1, source_target_pairs={{0,2},{1,3},{2,0},{3,1},{4,6},{5,7},{6,4},{7,5},{8,10},{9,11},{10,... | collective-permute-start | bytes 786440 | tf_op jit(solution)/shard_map/ppermute | solution.py:182
  35.0 16.5 %collective-permute-start.10 = (f32[256,256]{1,0:T(8,128)}, f32[256,256]{1,0:T(8,128)S(1)}, u32[]{:S(2)}, u32[]{:S(2)}) collective-permute-start(f32[256,256]{1,0:T(8,128)} %get-tuple-element.47), channel_id=1, source_target_pairs={{0,1},{1,0},{2,3},{3,2},{4,5},{5,4},{6,7},{7,6},{8,9},{9,8},{10,11... | collective-permute-start | bytes 786440 | tf_op jit(solution)/shard_map/ppermute | solution.py:178
  36.5 13.5 %collective-permute-start.18 = (f32[256,256]{1,0:T(8,128)}, f32[256,256]{1,0:T(8,128)S(1)}, u32[]{:S(2)}, u32[]{:S(2)}) collective-permute-start(f32[256,256]{1,0:T(8,128)} %get-tuple-element.53), channel_id=1, source_target_pairs={{0,1},{1,0},{2,3},{3,2},{4,5},{5,4},{6,7},{7,6},{8,9},{9,8},{10,11... | collective-permute-start | bytes 786440 | tf_op jit(solution)/shard_map/ppermute | solution.py:178
  37.0 15.0 %collective-permute-start.12 = (f32[256,256]{1,0:T(8,128)S(1)}, f32[256,256]{1,0:T(8,128)S(1)}, u32[]{:S(2)}, u32[]{:S(2)}) collective-permute-start(f32[256,256]{1,0:T(8,128)S(1)} %add.108), channel_id=1, source_target_pairs={{0,2},{1,3},{2,0},{3,1},{4,6},{5,7},{6,4},{7,5},{8,10},{9,11},{10,... | collective-permute-start | bytes 786440 | tf_op jit(solution)/shard_map/ppermute | solution.py:182
  39.8 12.2 %collective-permute-start.11 = (f32[256,256]{1,0:T(8,128)S(1)}, f32[256,256]{1,0:T(8,128)S(1)}, u32[]{:S(2)}, u32[]{:S(2)}) collective-permute-start(f32[256,256]{1,0:T(8,128)S(1)} %add_add_fusion.2), channel_id=1, source_target_pairs={{0,4},{1,5},{2,6},{3,7},{4,0},{5,1},{6,2},{7,3},{8,12},{9,13},{10,... | collective-permute-start | bytes 786440 | tf_op jit(solution)/shard_map/ppermute | solution.py:182
  43.3 12.0 %collective-permute-start.5 = (f32[256,256]{1,0:T(8,128)S(1)}, f32[256,256]{1,0:T(8,128)S(1)}, u32[]{:S(2)}, u32[]{:S(2)}) collective-permute-start(f32[256,256]{1,0:T(8,128)S(1)} %copy-done.9), channel_id=1, source_target_pairs={{0,1},{1,0},{2,3},{3,2},{4,5},{5,4},{6,7},{7,6},{8,9},{9,8},{10,11... | collective-permute-start | bytes 786440 | tf_op jit(solution)/shard_map/ppermute | solution.py:178
  50.0 34.4 %collective-permute-start.4 = (f32[256,256]{1,0:T(8,128)}, f32[256,256]{1,0:T(8,128)S(1)}, u32[]{:S(2)}, u32[]{:S(2)}) collective-permute-start(f32[256,256]{1,0:T(8,128)} %get-tuple-element.35), channel_id=1, source_target_pairs={{0,1},{1,0},{2,3},{3,2},{4,5},{5,4},{6,7},{7,6},{8,9},{9,8},{10,11... | collective-permute-start | bytes 786440 | tf_op jit(solution)/shard_map/ppermute | solution.py:178
  51.5 7.1 %collective-permute-start.9 = (f32[256,256]{1,0:T(8,128)S(1)}, f32[256,256]{1,0:T(8,128)S(1)}, u32[]{:S(2)}, u32[]{:S(2)}) collective-permute-start(f32[256,256]{1,0:T(8,128)S(1)} %copy-done.10), channel_id=1, source_target_pairs={{0,2},{1,3},{2,0},{3,1},{4,6},{5,7},{6,4},{7,5},{8,10},{9,11},{10,... | collective-permute-start | bytes 786440 | tf_op jit(solution)/shard_map/ppermute | solution.py:182
  53.0 31.4 %copy-start.1 = (f32[256,256]{1,0:T(8,128)S(1)}, f32[256,256]{1,0:T(8,128)}, u32[]{:S(2)}) copy-start(f32[256,256]{1,0:T(8,128)} %get-tuple-element.32) | copy-start | bytes 786436
  53.3 11.5 %collective-permute-start.13 = (f32[128,256]{1,0:T(8,128)S(1)}, f32[128,256]{1,0:T(8,128)S(1)}, u32[]{:S(2)}, u32[]{:S(2)}) collective-permute-start(f32[128,256]{1,0:T(8,128)S(1)} %fusion.8), channel_id=1, source_target_pairs={{0,2},{1,3},{2,0},{3,1},{4,6},{5,7},{6,4},{7,5},{8,10},{9,11},{10,... | collective-permute-start | bytes 393224 | tf_op jit(solution)/shard_map/ppermute | solution.py:182
  65.1 8.3 %collective-permute-start.15 = (f32[128,256]{1,0:T(8,128)S(1)}, f32[128,256]{1,0:T(8,128)S(1)}, u32[]{:S(2)}, u32[]{:S(2)}) collective-permute-start(f32[128,256]{1,0:T(8,128)S(1)} %fusion.3), channel_id=1, source_target_pairs={{0,4},{1,5},{4,0},{5,1},{8,12},{9,13},{12,8},{13,9},{16,20},{17,21... | collective-permute-start | bytes 393224 | tf_op jit(solution)/shard_map/ppermute | solution.py:182
  68.4 16.0 %collective-permute-start.14 = (f32[256,256]{1,0:T(8,128)S(1)}, f32[256,256]{1,0:T(8,128)S(1)}, u32[]{:S(2)}, u32[]{:S(2)}) collective-permute-start(f32[256,256]{1,0:T(8,128)S(1)} %add_add_fusion.3), channel_id=1, source_target_pairs={{0,4},{1,5},{2,6},{3,7},{4,0},{5,1},{6,2},{7,3},{8,12},{9,13},{10,... | collective-permute-start | bytes 786440 | tf_op jit(solution)/shard_map/ppermute | solution.py:182
  70.0 14.4 %collective-permute-start.19 = (f32[256,256]{1,0:T(8,128)S(1)}, f32[256,256]{1,0:T(8,128)S(1)}, u32[]{:S(2)}, u32[]{:S(2)}) collective-permute-start(f32[256,256]{1,0:T(8,128)S(1)} %add.115), channel_id=1, source_target_pairs={{0,2},{1,3},{2,0},{3,1},{4,6},{5,7},{6,4},{7,5},{8,10},{9,11},{10,... | collective-permute-start | bytes 786440 | tf_op jit(solution)/shard_map/ppermute | solution.py:182
  73.7 3.2 %collective-permute-start.16 = (f32[128,256]{1,0:T(8,128)S(1)}, f32[128,256]{1,0:T(8,128)S(1)}, u32[]{:S(2)}, u32[]{:S(2)}) collective-permute-start(f32[128,256]{1,0:T(8,128)S(1)} %fusion.2), channel_id=1, source_target_pairs={{0,8},{1,9},{8,0},{9,1},{16,24},{17,25},{24,16},{25,17}} | collective-permute-start | bytes 393224 | tf_op jit(solution)/shard_map/ppermute | solution.py:330
  77.2 6.9 %collective-permute-start.17 = (f32[128,256]{1,0:T(8,128)S(1)}, f32[128,256]{1,0:T(8,128)S(1)}, u32[]{:S(2)}, u32[]{:S(2)}) collective-permute-start(f32[128,256]{1,0:T(8,128)S(1)} %fusion.1), channel_id=1, source_target_pairs={{0,16},{1,17},{16,0},{17,1}} | collective-permute-start | bytes 393224 | tf_op jit(solution)/shard_map/ppermute | solution.py:330
  85.5 13.8 %collective-permute-start.20 = (f32[384,128]{1,0:T(8,128)S(1)}, f32[384,128]{1,0:T(8,128)S(1)}, u32[]{:S(2)}, u32[]{:S(2)}) collective-permute-start(f32[384,128]{1,0:T(8,128)S(1)} %pad_maximum_fusion.13), channel_id=1, source_target_pairs={{0,1},{1,0},{2,3},{3,2},{4,5},{5,4},{6,7},{7,6},{8,9},{9,8},{10,11... | collective-permute-start | bytes 589832 | tf_op jit(solution)/shard_map/ppermute | solution.py:178
  86.5 5.4 %collective-permute-start.21 = (f32[128,128]{1,0:T(8,128)S(1)}, f32[128,128]{1,0:T(8,128)S(1)}, u32[]{:S(2)}, u32[]{:S(2)}) collective-permute-start(f32[128,128]{1,0:T(8,128)S(1)} %get-tuple-element.68), channel_id=1, source_target_pairs={{0,1},{1,0},{2,3},{3,2},{4,5},{5,4},{6,7},{7,6},{8,9},{9,8},{10,11... | collective-permute-start | bytes 196616 | tf_op jit(solution)/shard_map/ppermute | solution.py:178
  99.3 0.7 copy-start.6
  (1 other events, 0.6 us)

commit v5 on v4

--- a/solution.py
+++ b/solution.py
@@ -77,21 +77,20 @@
     return chosen.astype(jnp.float32), others.astype(jnp.float32)
 
 
-def inverse_kernel(own_ref, received_ref, out_ref):
-    out_ref[...] = spd_inverse(own_ref[...] + received_ref[...])
+def inverse_kernel(gram_ref, out_ref):
+    out_ref[...] = spd_inverse(gram_ref[...])
 
 
 def finish_kernel(
-    node_at, own_ref, received_ref, inverse_ref, picked_ref, table_ref, leaf_ref, node_ref
+    node_at, total_ref, inverse_ref, picked_ref, table_ref, leaf_ref, node_ref
 ):
-    total = own_ref[...] + received_ref[...]
-    rank = total.shape[1]
-    cross = total[rank:]
+    rank = total_ref.shape[1]
+    cross = total_ref[rank:, :]
     index = lax.broadcasted_iota(jnp.int32, cross.shape, 0)
     choice = (index == table_ref[pl.ds(node_at[0], 1), :]).astype(jnp.float32)
     gram = dot(choice, cross, ((0,), (0,)))
     chosen, others = choices(picked_ref[...], leaf_ref.shape[0])
-    leaf_ref[...] = chosen + dot(others, dot(total[:rank], inverse_ref[...]))
+    leaf_ref[...] = chosen + dot(others, dot(total_ref[:rank, :], inverse_ref[...]))
     node_ref[...] = dot(cross, spd_inverse(gram))
 
 
@@ -330,6 +329,9 @@
             send = lambda value: lax.ppermute(value, ("grp", "leaf"), pairs)
             partner = send(current)
             upper = grp_pos >> bit & 1
+        before = current
+        if level == levels:
+            partner, gram = lax.optimization_barrier((partner, own_gram + received_gram))
         stacked = jnp.concatenate(
             [
                 jnp.where(upper == 1, partner, current),
@@ -346,10 +348,18 @@
         node = level_offset(level) + (device >> level)
         node_own = jnp.where(select & (side == 0), node, node_own)
 
-    other_rows = gathered(second, [early[0], gates[0], current])
+    other_rows = gathered(second, [early[0], gates[0], before])
     crosses = [
         cross_of(z, r) for z, r in zip((other_rows[:rank], other_rows[rank:]), halves)
     ]
+    sent = jnp.concatenate(
+        [
+            jnp.where(side == 0, crosses[1], crosses[0]),
+            jnp.where(side == 1, high_cross, low_cross),
+        ],
+        axis=0,
+    )
+    received = across(sent)
     own = jnp.concatenate(
         [
             jnp.where(side == 0, crosses[0], crosses[1]),
@@ -357,24 +367,19 @@
         ],
         axis=0,
     )
-    sent = jnp.concatenate(
-        [
-            jnp.where(side == 0, crosses[1], crosses[0]),
-            jnp.where(side == 1, high_cross, low_cross),
-        ],
-        axis=0,
-    )
-    received = across(sent)
+    total = own + received
     square = jax.ShapeDtypeStruct((rank, rank), jnp.float32)
-    inverse = pl.pallas_call(inverse_kernel, out_shape=square, name="inverse")(own_gram, received_gram)
+    inverse = pl.pallas_call(inverse_kernel, out_shape=square, name="inverse")(gram)
     tall = [jax.ShapeDtypeStruct((rows, rank), jnp.float32) for rows in (leaf_rows, 2 * rank)]
     whole = pl.BlockSpec(memory_space=pltpu.VMEM)
     leaf_basis, transfer = pl.pallas_call(
         finish_kernel,
         out_shape=tall,
-        in_specs=[pl.BlockSpec(memory_space=pltpu.SMEM)] + [whole] * 5,
+        in_specs=[pl.BlockSpec(memory_space=pltpu.SMEM)] + [whole] * 4,
         name="finish",
-    )(node_own[None], own, received, inverse, leaf_skeleton, node_skeleton)
+    )(
+        node_own[None], total, inverse, leaf_skeleton, node_skeleton
+    )
     return (leaf_basis, transfer[None])
 
 

time: 108 us -> 99.3 us (0.919)
  waiting for transfers between devices: 30.5 us -> 23.3 us
  local copies, waits for them, and re-layouts: 2.98 us -> 1.65 us
    ppermute x8, waiting for transfers between devices: 14.2 us -> 10.6 us  [along(): return lax.ppermute(value, 'leaf', pairs)]
    ppermute x9, waiting for transfers between devices: 8.54 us -> 5.2 us  [across(): return lax.ppermute(value, 'leaf', [(p, p ^ 1) for p in range(n_leaf)])]
    ppermute x8, starting transfers between devices: 11.9 us -> 13.9 us  [along(): return lax.ppermute(value, 'leaf', pairs)]
    ppermute x9, starting transfers between devices: 9.81 us -> 8.21 us  [across(): return lax.ppermute(value, 'leaf', [(p, p ^ 1) for p in range(n_leaf)])]
    add x0 -> x2, other arithmetic: none -> 1.35 us  [the longest x1 0.7 us: on_device(): total = own + received]
    unnamed x22 -> x18, local copies, waits for them, and re-layouts: 2.18 us -> 0.85 us
  transfers between devices with their start and end apart: 22 -> 22, of which waited for: 10 -> 9; matrix products, arithmetic and copies ran while one was open for 7% -> 7% of each run, Pallas kernels for 22% -> 24%
where the time goes in v5:
time: 99.3 us; the launch traced here: 98.9 us
  starting transfers between devices  34.8 us (35%)
  Pallas kernels  30.5 us (31%)
  waiting for transfers between devices  23.3 us (23%)
  matrix products  4.34 us (4%)
  other arithmetic  3.31 us (3%)
  local copies, waits for them, and re-layouts  1.65 us (2%)
    ppermute x8, starting transfers between devices, along(): return lax.ppermute(value, 'leaf', pairs)  13.9 us
    pallas_call x3, Pallas kernels, ordered(): outs = outs(matrix, probes, tables)  11.7 us
    ppermute x8, waiting for transfers between devices, along(): return lax.ppermute(value, 'leaf', pairs)  10.6 us
    ppermute x9, starting transfers between devices, across(): return lax.ppermute(value, 'leaf', [(p, p ^ 1) for p in range(n_leaf)])  8.21 us
    ppermute x3, starting transfers between devices, on_device(): lax.ppermute(skeletons, 'leaf', [(p, p ^ 1 << bit) for p in range(n_leaf)])  7.29 us
    pallas_call x1, Pallas kernels, on_device(): pl.pallas_call(finish_kernel, out_shape=tall, in_specs=[pl.BlockSpec(memo...  7.21 us
    pallas_call x1, Pallas kernels, on_device(): pl.pallas_call(inverse_kernel, out_shape=square, name='inverse')(gram)  6 us
    ppermute x2, starting transfers between devices, on_device(): send = lambda value: lax.ppermute(value, ('grp', 'leaf'), pairs)  5.42 us
  transfers between devices with their start and end apart: 22, of which 9 were waited for; matrix products, arithmetic and copies ran while one was open for 7% of the time, Pallas kernels for 24%

profile of v5, /device:TPU:0, one launch (start us, length us, event | category | flops | bytes accessed | tf_op | source)
XLA Modules:
  0.0 98.9 jit_solution(6979028228453413063)
XLA Ops:
  0.6 3.1 %collective-permute-start = (s32[1,128]{1,0:T(1,128)}, s32[1,128]{1,0:T(1,128)S(1)}, u32[]{:S(2)}, u32[]{:S(2)}) collective-permute-start(s32[1,128]{1,0:T(1,128)} %picked_ref.1), channel_id=1, source_target_pairs={{0,1},{1,0},{2,3},{3,2},{4,5},{5,4},{6,7},{7,6},{8,9},{9,8},{10,11... | collective-permute-start | bytes 1544 | tf_op jit(solution)/shard_map/ppermute | solution.py:216
  3.7 3.1 %product.1 = (f32[512,256]{1,0:T(8,128)}, f32[512,256]{1,0:T(8,128)}) custom-call(bf16[2048,1024]{1,0:T(8,128)(2,1)} %refs_0_.7, bf16[1024,512]{1,0:T(8,128)(2,1)} %refs_1_.7), custom_call_target="tpu_custom_call" | custom-call | tf_op jit(solution)/shard_map/product/pallas_call | solution.py:205
  7.4 1.6 %collective-permute-start.1 = (s32[2,128]{1,0:T(2,128)S(1)}, s32[2,128]{1,0:T(2,128)S(1)}, u32[]{:S(2)}, u32[]{:S(2)}) collective-permute-start(s32[2,128]{1,0:T(2,128)S(1)} %add_select_fusion.1), channel_id=1, source_target_pairs={{0,2},{1,3},{2,0},{3,1},{4,6},{5,7},{6,4},{7,5},{8,10},{9,11},{10,... | collective-permute-start | bytes 3080 | tf_op jit(solution)/shard_map/ppermute | solution.py:216
  9.1 2.0 %collective-permute-done.1 = s32[2,128]{1,0:T(2,128)S(1)} collective-permute-done((s32[2,128]{1,0:T(2,128)S(1)}, s32[2,128]{1,0:T(2,128)S(1)}, u32[]{:S(2)}, u32[]{:S(2)}) %collective-permute-start.1) | collective-permute-done | bytes 1056 | tf_op jit(solution)/shard_map/ppermute | solution.py:216
  11.1 2.6 %collective-permute-start.2 = (s32[4,128]{1,0:T(4,128)S(1)}, s32[4,128]{1,0:T(4,128)S(1)}, u32[]{:S(2)}, u32[]{:S(2)}) collective-permute-start(s32[4,128]{1,0:T(4,128)S(1)} %add_select_fusion), channel_id=1, source_target_pairs={{0,4},{1,5},{2,6},{3,7},{4,0},{5,1},{6,2},{7,3},{8,12},{9,13},{10,... | collective-permute-start | bytes 6152 | tf_op jit(solution)/shard_map/ppermute | solution.py:216
  13.7 1.9 %collective-permute-done.2 = s32[4,128]{1,0:T(4,128)S(1)} collective-permute-done((s32[4,128]{1,0:T(4,128)S(1)}, s32[4,128]{1,0:T(4,128)S(1)}, u32[]{:S(2)}, u32[]{:S(2)}) %collective-permute-start.2) | collective-permute-done | bytes 2080 | tf_op jit(solution)/shard_map/ppermute | solution.py:216
  16.1 3.9 %ordered.4 = (f32[256,256]{1,0:T(8,128)}, f32[256,256]{1,0:T(8,128)}, f32[256,256]{1,0:T(8,128)}, f32[256,256]{1,0:T(8,128)}) custom-call(bf16[2048,1024]{1,0:T(8,128)(2,1)} %refs_0_.7, bf16[1024,512]{1,0:T(8,128)(2,1)} %refs_1_.7, s32[8,1,128]{2,1,0:T(1,128)} %broadcast_select_fusion.13.refs_2_.picked_ref), custom_call_target="tpu_custom_call" | custom-call | tf_op jit(solution)/shard_map/ordered/pallas_call | solution.py:239
  20.1 1.4 %collective-permute-start.3 = (f32[256,256]{1,0:T(8,128)}, f32[256,256]{1,0:T(8,128)S(1)}, u32[]{:S(2)}, u32[]{:S(2)}) collective-permute-start(f32[256,256]{1,0:T(8,128)} %get-tuple-element.36), channel_id=1, source_target_pairs={{0,1},{1,0},{2,3},{3,2},{4,5},{5,4},{6,7},{7,6},{8,9},{9,8},{10,11... | collective-permute-start | bytes 786440 | tf_op jit(solution)/shard_map/ppermute | solution.py:177
  21.5 3.9 %ordered.5 = (f32[256,256]{1,0:T(8,128)}, f32[256,256]{1,0:T(8,128)}, f32[256,256]{1,0:T(8,128)}, f32[256,256]{1,0:T(8,128)}) custom-call(bf16[2048,1024]{1,0:T(8,128)(2,1)} %refs_0_.7, bf16[1024,512]{1,0:T(8,128)(2,1)} %refs_1_.7, s32[8,1,128]{2,1,0:T(1,128)} %broadcast_select_fusion.13.refs_2_.picked_ref), custom_call_target="tpu_custom_call" | custom-call | tf_op jit(solution)/shard_map/ordered/pallas_call | solution.py:239
  26.1 0.8 copy-done
  26.9 2.5 %split.1 = (f32[256,256]{1,0:T(8,128)}, f32[256,256]{1,0:T(8,128)}) custom-call(f32[512,256]{1,0:T(8,128)} %get-tuple-element.41.keep_ref, f32[512,256]{1,0:T(8,128)} %copy-done, s32[8,1,128]{2,1,0:T(1,128)} %broadcast_select_fusion.13.refs_2_.picked_ref), custom_call_target="tpu_custom_call" | custom-call | tf_op jit(solution)/shard_map/split/pallas_call | solution.py:255
  29.4 1.6 %collective-permute-start.8 = (f32[256,256]{1,0:T(8,128)}, f32[256,256]{1,0:T(8,128)S(1)}, u32[]{:S(2)}, u32[]{:S(2)}) collective-permute-start(f32[256,256]{1,0:T(8,128)} %get-tuple-element.46), channel_id=1, source_target_pairs={{0,2},{1,3},{2,0},{3,1},{4,6},{5,7},{6,4},{7,5},{8,10},{9,11},{10,... | collective-permute-start | bytes 786440 | tf_op jit(solution)/shard_map/ppermute | solution.py:181
  31.0 3.9 %ordered.3 = (f32[256,256]{1,0:T(8,128)}, f32[256,256]{1,0:T(8,128)}, f32[256,256]{1,0:T(8,128)}, f32[256,256]{1,0:T(8,128)}) custom-call(bf16[2048,1024]{1,0:T(8,128)(2,1)} %refs_0_.7, bf16[1024,512]{1,0:T(8,128)(2,1)} %refs_1_.7, s32[8,1,128]{2,1,0:T(1,128)} %broadcast_select_fusion.13.refs_2_.picked_ref), custom_call_target="tpu_custom_call" | custom-call | tf_op jit(solution)/shard_map/ordered/pallas_call | solution.py:239
  34.9 1.4 %collective-permute-start.10 = (f32[256,256]{1,0:T(8,128)}, f32[256,256]{1,0:T(8,128)S(1)}, u32[]{:S(2)}, u32[]{:S(2)}) collective-permute-start(f32[256,256]{1,0:T(8,128)} %get-tuple-element.49), channel_id=1, source_target_pairs={{0,1},{1,0},{2,3},{3,2},{4,5},{5,4},{6,7},{7,6},{8,9},{9,8},{10,11... | collective-permute-start | bytes 786440 | tf_op jit(solution)/shard_map/ppermute | solution.py:177
  37.5 2.3 %collective-permute-done.8 = f32[256,256]{1,0:T(8,128)S(1)} collective-permute-done((f32[256,256]{1,0:T(8,128)}, f32[256,256]{1,0:T(8,128)S(1)}, u32[]{:S(2)}, u32[]{:S(2)}) %collective-permute-start.8) | collective-permute-done | bytes 262176 | tf_op jit(solution)/shard_map/ppermute | solution.py:181
  39.8 2.8 %collective-permute-start.11 = (f32[256,256]{1,0:T(8,128)S(1)}, f32[256,256]{1,0:T(8,128)S(1)}, u32[]{:S(2)}, u32[]{:S(2)}) collective-permute-start(f32[256,256]{1,0:T(8,128)S(1)} %add_add_fusion.2), channel_id=1, source_target_pairs={{0,4},{1,5},{2,6},{3,7},{4,0},{5,1},{6,2},{7,3},{8,12},{9,13},{10,... | collective-permute-start | bytes 786440 | tf_op jit(solution)/shard_map/ppermute | solution.py:181
  42.7 0.8 fusion.26
  43.5 1.3 %collective-permute-start.5 = (f32[256,256]{1,0:T(8,128)S(1)}, f32[256,256]{1,0:T(8,128)S(1)}, u32[]{:S(2)}, u32[]{:S(2)}) collective-permute-start(f32[256,256]{1,0:T(8,128)S(1)} %copy-done.7), channel_id=1, source_target_pairs={{0,1},{1,0},{2,3},{3,2},{4,5},{5,4},{6,7},{7,6},{8,9},{9,8},{10,11... | collective-permute-start | bytes 786440 | tf_op jit(solution)/shard_map/ppermute | solution.py:177
  44.7 5.2 %collective-permute-done.17 = f32[256,256]{1,0:T(8,128)S(1)} collective-permute-done((f32[256,256]{1,0:T(8,128)}, f32[256,256]{1,0:T(8,128)S(1)}, u32[]{:S(2)}, u32[]{:S(2)}) %collective-permute-start.17) | collective-permute-done | bytes 262176 | tf_op jit(solution)/shard_map/ppermute | solution.py:177
  49.9 1.4 %collective-permute-start.4 = (f32[256,256]{1,0:T(8,128)}, f32[256,256]{1,0:T(8,128)S(1)}, u32[]{:S(2)}, u32[]{:S(2)}) collective-permute-start(f32[256,256]{1,0:T(8,128)} %get-tuple-element.37), channel_id=1, source_target_pairs={{0,1},{1,0},{2,3},{3,2},{4,5},{5,4},{6,7},{7,6},{8,9},{9,8},{10,11... | collective-permute-start | bytes 786440 | tf_op jit(solution)/shard_map/ppermute | solution.py:177
  52.0 1.0 %add_add_fusion.1 = f32[256,256]{1,0:T(8,128)S(1)} fusion(f32[256,256]{1,0:T(8,128)S(1)} %collective-permute-done.12, f32[256,256]{1,0:T(8,128)S(1)} %collective-permute-done.11, f32[256,256]{1,0:T(8,128)} %get-tuple-element.48, f32[256,256]{1,0:T(8,128)S(1)} %collective-permute-done.10), kind=kLoop, calls=%fused_computation.9 | loop fusion | flops 196608 | bytes 1310720 | tf_op jit(solution)/shard_map/add | solution.py:281
  54.5 2.9 %collective-permute-start.13 = (f32[128,256]{1,0:T(8,128)S(1)}, f32[128,256]{1,0:T(8,128)S(1)}, u32[]{:S(2)}, u32[]{:S(2)}) collective-permute-start(f32[128,256]{1,0:T(8,128)S(1)} %fusion.10), channel_id=1, source_target_pairs={{0,2},{1,3},{2,0},{3,1},{4,6},{5,7},{6,4},{7,5},{8,10},{9,11},{10,... | collective-permute-start | bytes 393224 | tf_op jit(solution)/shard_map/ppermute | solution.py:181
  59.0 3.0 %collective-permute-done.13 = f32[128,256]{1,0:T(8,128)S(1)} collective-permute-done((f32[128,256]{1,0:T(8,128)S(1)}, f32[128,256]{1,0:T(8,128)S(1)}, u32[]{:S(2)}, u32[]{:S(2)}) %collective-permute-start.13) | collective-permute-done | bytes 131104 | tf_op jit(solution)/shard_map/ppermute | solution.py:181
  62.2 5.3 %collective-permute-start.15 = (f32[128,256]{1,0:T(8,128)S(1)}, f32[128,256]{1,0:T(8,128)S(1)}, u32[]{:S(2)}, u32[]{:S(2)}) collective-permute-start(f32[128,256]{1,0:T(8,128)S(1)} %fusion.5), channel_id=1, source_target_pairs={{0,4},{1,5},{4,0},{5,1},{8,12},{9,13},{12,8},{13,9},{16,20},{17,21... | collective-permute-start | bytes 393224 | tf_op jit(solution)/shard_map/ppermute | solution.py:181
  68.1 4.9 %collective-permute-done.15 = f32[128,256]{1,0:T(8,128)S(1)} collective-permute-done((f32[128,256]{1,0:T(8,128)S(1)}, f32[128,256]{1,0:T(8,128)S(1)}, u32[]{:S(2)}, u32[]{:S(2)}) %collective-permute-start.15) | collective-permute-done | bytes 131104 | tf_op jit(solution)/shard_map/ppermute | solution.py:181
  73.3 1.9 %collective-permute-start.16 = (f32[128,256]{1,0:T(8,128)S(1)}, f32[128,256]{1,0:T(8,128)S(1)}, u32[]{:S(2)}, u32[]{:S(2)}) collective-permute-start(f32[128,256]{1,0:T(8,128)S(1)} %fusion.4), channel_id=1, source_target_pairs={{0,8},{1,9},{8,0},{9,1},{16,24},{17,25},{24,16},{25,17}} | collective-permute-start | bytes 393224 | tf_op jit(solution)/shard_map/ppermute | solution.py:329
  75.6 0.9 collective-permute-done.16
  76.8 3.5 %collective-permute-start.19 = (f32[128,256]{1,0:T(8,128)S(1)}, f32[128,256]{1,0:T(8,128)S(1)}, u32[]{:S(2)}, u32[]{:S(2)}) collective-permute-start(f32[128,256]{1,0:T(8,128)S(1)} %fusion.3), channel_id=1, source_target_pairs={{0,16},{1,17},{16,0},{17,1}} | collective-permute-start | bytes 393224 | tf_op jit(solution)/shard_map/ppermute | solution.py:329
  81.0 2.7 %collective-permute-done.19 = f32[128,256]{1,0:T(8,128)S(1)} collective-permute-done((f32[128,256]{1,0:T(8,128)S(1)}, f32[128,256]{1,0:T(8,128)S(1)}, u32[]{:S(2)}, u32[]{:S(2)}) %collective-permute-start.19) | collective-permute-done | bytes 131104 | tf_op jit(solution)/shard_map/ppermute | solution.py:329
  85.0 6.0 %inverse.1.inverse_ref = f32[128,128]{1,0:T(8,128)} custom-call(f32[128,128]{1,0:T(8,128)} %select_add_fusion.gram_ref), custom_call_target="tpu_custom_call" | custom-call | tf_op jit(solution)/shard_map/inverse/pallas_call | solution.py:372
  91.0 0.7 maximum_add_fusion.total_ref
  91.7 7.2 %finish.1 = (f32[256,128]{1,0:T(8,128)}, f32[256,128]{1,0:T(8,128)}) custom-call(s32[1]{0:T(128)} %bitcast.node_at, f32[384,128]{1,0:T(8,128)} %maximum_add_fusion.total_ref, f32[128,128]{1,0:T(8,128)} %inverse.1.inverse_ref, s32[1,128]{1,0:T(1,128)} %picked_ref.1, s32[31,128]{1,0:T(8,128)} %table_ref.1), custom_call_target="tpu_custom_call" | custom-call | tf_op jit(solution)/shard_map/finish/pallas_call | solution.py:375
  (68 shorter events, 10.3 us)
Async XLA Ops:
  0.6 6.8 %copy-start.6 = (s32[1,128]{1,0:T(1,128)S(1)}, s32[1,128]{1,0:T(1,128)}, u32[]{:S(2)}) copy-start(s32[1,128]{1,0:T(1,128)} %picked_ref.1) | copy-start | bytes 1540
  0.6 6.2 %collective-permute-start = (s32[1,128]{1,0:T(1,128)}, s32[1,128]{1,0:T(1,128)S(1)}, u32[]{:S(2)}, u32[]{:S(2)}) collective-permute-start(s32[1,128]{1,0:T(1,128)} %picked_ref.1), channel_id=1, source_target_pairs={{0,1},{1,0},{2,3},{3,2},{4,5},{5,4},{6,7},{7,6},{8,9},{9,8},{10,11... | collective-permute-start | bytes 1544 | tf_op jit(solution)/shard_map/ppermute | solution.py:216
  6.8 19.2 %collective-permute-start.6 = (f32[512,256]{1,0:T(8,128)}, f32[512,256]{1,0:T(8,128)S(1)}, u32[]{:S(2)}, u32[]{:S(2)}) collective-permute-start(f32[512,256]{1,0:T(8,128)} %get-tuple-element.42), channel_id=1, source_target_pairs={{0,1},{1,0},{2,3},{3,2},{4,5},{5,4},{6,7},{7,6},{8,9},{9,8},{10,11... | collective-permute-start | bytes 1572872 | tf_op jit(solution)/shard_map/ppermute | solution.py:177
  7.4 3.6 %collective-permute-start.1 = (s32[2,128]{1,0:T(2,128)S(1)}, s32[2,128]{1,0:T(2,128)S(1)}, u32[]{:S(2)}, u32[]{:S(2)}) collective-permute-start(s32[2,128]{1,0:T(2,128)S(1)} %add_select_fusion.1), channel_id=1, source_target_pairs={{0,2},{1,3},{2,0},{3,1},{4,6},{5,7},{6,4},{7,5},{8,10},{9,11},{10,... | collective-permute-start | bytes 3080 | tf_op jit(solution)/shard_map/ppermute | solution.py:216
  11.1 4.5 %collective-permute-start.2 = (s32[4,128]{1,0:T(4,128)S(1)}, s32[4,128]{1,0:T(4,128)S(1)}, u32[]{:S(2)}, u32[]{:S(2)}) collective-permute-start(s32[4,128]{1,0:T(4,128)S(1)} %add_select_fusion), channel_id=1, source_target_pairs={{0,4},{1,5},{2,6},{3,7},{4,0},{5,1},{6,2},{7,3},{8,12},{9,13},{10,... | collective-permute-start | bytes 6152 | tf_op jit(solution)/shard_map/ppermute | solution.py:216
  20.1 16.3 %collective-permute-start.3 = (f32[256,256]{1,0:T(8,128)}, f32[256,256]{1,0:T(8,128)S(1)}, u32[]{:S(2)}, u32[]{:S(2)}) collective-permute-start(f32[256,256]{1,0:T(8,128)} %get-tuple-element.36), channel_id=1, source_target_pairs={{0,1},{1,0},{2,3},{3,2},{4,5},{5,4},{6,7},{7,6},{8,9},{9,8},{10,11... | collective-permute-start | bytes 786440 | tf_op jit(solution)/shard_map/ppermute | solution.py:177
  25.4 11.6 %copy-start.3 = (f32[256,256]{1,0:T(8,128)S(1)}, f32[256,256]{1,0:T(8,128)}, u32[]{:S(2)}) copy-start(f32[256,256]{1,0:T(8,128)} %get-tuple-element.50) | copy-start | bytes 786436
  25.4 14.4 %copy-start.5 = (f32[256,256]{1,0:T(8,128)S(1)}, f32[256,256]{1,0:T(8,128)}, u32[]{:S(2)}) copy-start(f32[256,256]{1,0:T(8,128)} %get-tuple-element.44) | copy-start | bytes 786436
  25.4 18.1 %copy-start.7 = (f32[256,256]{1,0:T(8,128)S(1)}, f32[256,256]{1,0:T(8,128)}, u32[]{:S(2)}) copy-start(f32[256,256]{1,0:T(8,128)} %get-tuple-element.40) | copy-start | bytes 786436
  25.4 26.0 %copy-start.2 = (f32[256,256]{1,0:T(8,128)S(1)}, f32[256,256]{1,0:T(8,128)}, u32[]{:S(2)}) copy-start(f32[256,256]{1,0:T(8,128)} %get-tuple-element.53) | copy-start | bytes 786436
  25.4 12.1 %collective-permute-start.7 = (f32[256,256]{1,0:T(8,128)}, f32[256,256]{1,0:T(8,128)S(1)}, u32[]{:S(2)}, u32[]{:S(2)}) collective-permute-start(f32[256,256]{1,0:T(8,128)} %get-tuple-element.45), channel_id=1, source_target_pairs={{0,1},{1,0},{2,3},{3,2},{4,5},{5,4},{6,7},{7,6},{8,9},{9,8},{10,11... | collective-permute-start | bytes 786440 | tf_op jit(solution)/shard_map/ppermute | solution.py:177
  26.0 0.8 copy-start
  29.4 22.0 %copy-start.8 = (f32[256,256]{1,0:T(8,128)S(1)}, f32[256,256]{1,0:T(8,128)}, u32[]{:S(2)}) copy-start(f32[256,256]{1,0:T(8,128)} %get-tuple-element.47) | copy-start | bytes 786436
  29.4 28.5 %copy-start.4 = (f32[256,256]{1,0:T(8,128)S(1)}, f32[256,256]{1,0:T(8,128)}, u32[]{:S(2)}) copy-start(f32[256,256]{1,0:T(8,128)} %get-tuple-element.38) | copy-start | bytes 786436
  29.4 10.3 %collective-permute-start.8 = (f32[256,256]{1,0:T(8,128)}, f32[256,256]{1,0:T(8,128)S(1)}, u32[]{:S(2)}, u32[]{:S(2)}) collective-permute-start(f32[256,256]{1,0:T(8,128)} %get-tuple-element.46), channel_id=1, source_target_pairs={{0,2},{1,3},{2,0},{3,1},{4,6},{5,7},{6,4},{7,5},{8,10},{9,11},{10,... | collective-permute-start | bytes 786440 | tf_op jit(solution)/shard_map/ppermute | solution.py:181
  34.9 16.5 %collective-permute-start.10 = (f32[256,256]{1,0:T(8,128)}, f32[256,256]{1,0:T(8,128)S(1)}, u32[]{:S(2)}, u32[]{:S(2)}) collective-permute-start(f32[256,256]{1,0:T(8,128)} %get-tuple-element.49), channel_id=1, source_target_pairs={{0,1},{1,0},{2,3},{3,2},{4,5},{5,4},{6,7},{7,6},{8,9},{9,8},{10,11... | collective-permute-start | bytes 786440 | tf_op jit(solution)/shard_map/ppermute | solution.py:177
  36.4 13.6 %collective-permute-start.17 = (f32[256,256]{1,0:T(8,128)}, f32[256,256]{1,0:T(8,128)S(1)}, u32[]{:S(2)}, u32[]{:S(2)}) collective-permute-start(f32[256,256]{1,0:T(8,128)} %get-tuple-element.55), channel_id=1, source_target_pairs={{0,1},{1,0},{2,3},{3,2},{4,5},{5,4},{6,7},{7,6},{8,9},{9,8},{10,11... | collective-permute-start | bytes 786440 | tf_op jit(solution)/shard_map/ppermute | solution.py:177
  37.0 15.0 %collective-permute-start.12 = (f32[256,256]{1,0:T(8,128)S(1)}, f32[256,256]{1,0:T(8,128)S(1)}, u32[]{:S(2)}, u32[]{:S(2)}) collective-permute-start(f32[256,256]{1,0:T(8,128)S(1)} %add.114), channel_id=1, source_target_pairs={{0,2},{1,3},{2,0},{3,1},{4,6},{5,7},{6,4},{7,5},{8,10},{9,11},{10,... | collective-permute-start | bytes 786440 | tf_op jit(solution)/shard_map/ppermute | solution.py:181
  39.8 12.2 %collective-permute-start.11 = (f32[256,256]{1,0:T(8,128)S(1)}, f32[256,256]{1,0:T(8,128)S(1)}, u32[]{:S(2)}, u32[]{:S(2)}) collective-permute-start(f32[256,256]{1,0:T(8,128)S(1)} %add_add_fusion.2), channel_id=1, source_target_pairs={{0,4},{1,5},{2,6},{3,7},{4,0},{5,1},{6,2},{7,3},{8,12},{9,13},{10,... | collective-permute-start | bytes 786440 | tf_op jit(solution)/shard_map/ppermute | solution.py:181
  43.5 13.9 %collective-permute-start.5 = (f32[256,256]{1,0:T(8,128)S(1)}, f32[256,256]{1,0:T(8,128)S(1)}, u32[]{:S(2)}, u32[]{:S(2)}) collective-permute-start(f32[256,256]{1,0:T(8,128)S(1)} %copy-done.7), channel_id=1, source_target_pairs={{0,1},{1,0},{2,3},{3,2},{4,5},{5,4},{6,7},{7,6},{8,9},{9,8},{10,11... | collective-permute-start | bytes 786440 | tf_op jit(solution)/shard_map/ppermute | solution.py:177
  49.9 30.4 %collective-permute-start.4 = (f32[256,256]{1,0:T(8,128)}, f32[256,256]{1,0:T(8,128)S(1)}, u32[]{:S(2)}, u32[]{:S(2)}) collective-permute-start(f32[256,256]{1,0:T(8,128)} %get-tuple-element.37), channel_id=1, source_target_pairs={{0,1},{1,0},{2,3},{3,2},{4,5},{5,4},{6,7},{7,6},{8,9},{9,8},{10,11... | collective-permute-start | bytes 786440 | tf_op jit(solution)/shard_map/ppermute | solution.py:177
  51.4 29.0 %copy-start.1 = (f32[256,256]{1,0:T(8,128)S(1)}, f32[256,256]{1,0:T(8,128)}, u32[]{:S(2)}) copy-start(f32[256,256]{1,0:T(8,128)} %get-tuple-element.34) | copy-start | bytes 786436
  51.4 6.4 %collective-permute-start.9 = (f32[256,256]{1,0:T(8,128)S(1)}, f32[256,256]{1,0:T(8,128)S(1)}, u32[]{:S(2)}, u32[]{:S(2)}) collective-permute-start(f32[256,256]{1,0:T(8,128)S(1)} %copy-done.8), channel_id=1, source_target_pairs={{0,2},{1,3},{2,0},{3,1},{4,6},{5,7},{6,4},{7,5},{8,10},{9,11},{10,... | collective-permute-start | bytes 786440 | tf_op jit(solution)/shard_map/ppermute | solution.py:181
  53.6 4.7 %collective-permute-start.20 = (f32[128,128]{1,0:T(8,128)S(1)}, f32[128,128]{1,0:T(8,128)S(1)}, u32[]{:S(2)}, u32[]{:S(2)}) collective-permute-start(f32[128,128]{1,0:T(8,128)S(1)} %get-tuple-element.79), channel_id=1, source_target_pairs={{0,1},{1,0},{2,3},{3,2},{4,5},{5,4},{6,7},{7,6},{8,9},{9,8},{10,11... | collective-permute-start | bytes 196616 | tf_op jit(solution)/shard_map/ppermute | solution.py:177
  54.5 7.5 %collective-permute-start.13 = (f32[128,256]{1,0:T(8,128)S(1)}, f32[128,256]{1,0:T(8,128)S(1)}, u32[]{:S(2)}, u32[]{:S(2)}) collective-permute-start(f32[128,256]{1,0:T(8,128)S(1)} %fusion.10), channel_id=1, source_target_pairs={{0,2},{1,3},{2,0},{3,1},{4,6},{5,7},{6,4},{7,5},{8,10},{9,11},{10,... | collective-permute-start | bytes 393224 | tf_op jit(solution)/shard_map/ppermute | solution.py:181
  62.2 10.7 %collective-permute-start.15 = (f32[128,256]{1,0:T(8,128)S(1)}, f32[128,256]{1,0:T(8,128)S(1)}, u32[]{:S(2)}, u32[]{:S(2)}) collective-permute-start(f32[128,256]{1,0:T(8,128)S(1)} %fusion.5), channel_id=1, source_target_pairs={{0,4},{1,5},{4,0},{5,1},{8,12},{9,13},{12,8},{13,9},{16,20},{17,21... | collective-permute-start | bytes 393224 | tf_op jit(solution)/shard_map/ppermute | solution.py:181
  67.5 12.8 %collective-permute-start.14 = (f32[256,256]{1,0:T(8,128)S(1)}, f32[256,256]{1,0:T(8,128)S(1)}, u32[]{:S(2)}, u32[]{:S(2)}) collective-permute-start(f32[256,256]{1,0:T(8,128)S(1)} %add_add_fusion.3), channel_id=1, source_target_pairs={{0,4},{1,5},{2,6},{3,7},{4,0},{5,1},{6,2},{7,3},{8,12},{9,13},{10,... | collective-permute-start | bytes 786440 | tf_op jit(solution)/shard_map/ppermute | solution.py:181
  67.6 12.7 %collective-permute-start.18 = (f32[256,256]{1,0:T(8,128)S(1)}, f32[256,256]{1,0:T(8,128)S(1)}, u32[]{:S(2)}, u32[]{:S(2)}) collective-permute-start(f32[256,256]{1,0:T(8,128)S(1)} %add.120), channel_id=1, source_target_pairs={{0,2},{1,3},{2,0},{3,1},{4,6},{5,7},{6,4},{7,5},{8,10},{9,11},{10,... | collective-permute-start | bytes 786440 | tf_op jit(solution)/shard_map/ppermute | solution.py:181
  73.3 3.2 %collective-permute-start.16 = (f32[128,256]{1,0:T(8,128)S(1)}, f32[128,256]{1,0:T(8,128)S(1)}, u32[]{:S(2)}, u32[]{:S(2)}) collective-permute-start(f32[128,256]{1,0:T(8,128)S(1)} %fusion.4), channel_id=1, source_target_pairs={{0,8},{1,9},{8,0},{9,1},{16,24},{17,25},{24,16},{25,17}} | collective-permute-start | bytes 393224 | tf_op jit(solution)/shard_map/ppermute | solution.py:329
  76.8 6.9 %collective-permute-start.19 = (f32[128,256]{1,0:T(8,128)S(1)}, f32[128,256]{1,0:T(8,128)S(1)}, u32[]{:S(2)}, u32[]{:S(2)}) collective-permute-start(f32[128,256]{1,0:T(8,128)S(1)} %fusion.3), channel_id=1, source_target_pairs={{0,16},{1,17},{16,0},{17,1}} | collective-permute-start | bytes 393224 | tf_op jit(solution)/shard_map/ppermute | solution.py:329
  84.8 6.2 %collective-permute-start.21 = (f32[384,128]{1,0:T(8,128)S(1)}, f32[384,128]{1,0:T(8,128)S(1)}, u32[]{:S(2)}, u32[]{:S(2)}) collective-permute-start(f32[384,128]{1,0:T(8,128)S(1)} %pad_maximum_fusion.12), channel_id=1, source_target_pairs={{0,1},{1,0},{2,3},{3,2},{4,5},{5,4},{6,7},{7,6},{8,9},{9,8},{10,11... | collective-permute-start | bytes 589832 | tf_op jit(solution)/shard_map/ppermute | solution.py:177

commit v6 on v5

--- a/solution.py
+++ b/solution.py
@@ -22,33 +22,23 @@
     for kb in range(n // 8):
         k = 8 * kb
         edge = [jnp.broadcast_to(tiles[kb][:, k + j : k + j + 1], (8, n)) for j in range(8)]
-        d = {
-            (i, j): jnp.broadcast_to(edge[j][i : i + 1, :], (8, n))
-            for i in range(8)
-            for j in range(i + 1)
-        }
         inside = (lane >= k) & (lane < k + 8)
-        base = jnp.where(inside, jnp.where(lane - k == sub, 1.0, 0.0), tiles[kb])
-        p = [jnp.broadcast_to(base[j : j + 1, :], (8, n)) for j in range(8)]
-        inv, low = [None] * 8, {}
+        w = jnp.where(inside, jnp.where(lane - k == sub, 1.0, 0.0), tiles[kb])
         for j in range(8):
-            inv[j] = 1.0 / d[j, j]
+            pivot = 1.0 / jnp.broadcast_to(edge[j][j : j + 1, :], (8, n))
+            mine = sub == j
+            factor = jnp.where(mine, 0.0, edge[j])
+            scaled = jnp.broadcast_to(w[j : j + 1, :], (8, n)) * pivot
+            w = jnp.where(mine, scaled, w - factor * scaled)
             for i in range(j + 1, 8):
-                low[i, j] = d[i, j] * inv[j]
-            for i in range(j + 1, 8):
-                for m in range(j + 1, i + 1):
-                    d[i, m] = d[i, m] - low[i, j] * d[m, j]
-                p[i] = p[i] - low[i, j] * p[j]
-        w = [p[j] * inv[j] for j in range(8)]
-        for j in range(7, 0, -1):
-            for i in range(j):
-                w[i] = w[i] - low[j, i] * w[j]
+                scaled = jnp.broadcast_to(edge[i][j : j + 1, :], (8, n)) * pivot
+                edge[i] = jnp.where(mine, scaled, edge[i] - factor * scaled)
+        solved = w
+        w = [jnp.broadcast_to(solved[j : j + 1, :], (8, n)) for j in range(8)]
         fresh = []
         for r, t in enumerate(tiles):
             if r == kb:
-                x = w[0]
-                for j in range(1, 8):
-                    x = jnp.where(sub == j, w[j], x)
+                x = solved
             else:
                 x = jnp.where(inside, 0.0, t)
                 col = [jnp.broadcast_to(t[:, k + j : k + j + 1], (8, n)) for j in range(8)]

time: 99.3 us -> 98.1 us (0.988)
  Pallas kernels: 30.5 us -> 29.3 us
where the time goes in v6:
time: 98.1 us; the launch traced here: 97.7 us
  starting transfers between devices  34.8 us (35%)
  Pallas kernels  29.3 us (30%)
  waiting for transfers between devices  23.3 us (24%)
  matrix products  4.34 us (4%)
  other arithmetic  3.31 us (3%)
  local copies, waits for them, and re-layouts  1.65 us (2%)
    ppermute x8, starting transfers between devices, along(): return lax.ppermute(value, 'leaf', pairs)  13.9 us
    pallas_call x3, Pallas kernels, ordered(): outs = outs(matrix, probes, tables)  11.7 us
    ppermute x8, waiting for transfers between devices, along(): return lax.ppermute(value, 'leaf', pairs)  10.6 us
    ppermute x9, starting transfers between devices, across(): return lax.ppermute(value, 'leaf', [(p, p ^ 1) for p in range(n_leaf)])  8.21 us
    ppermute x3, starting transfers between devices, on_device(): lax.ppermute(skeletons, 'leaf', [(p, p ^ 1 << bit) for p in range(n_leaf)])  7.29 us
    pallas_call x1, Pallas kernels, on_device(): pl.pallas_call(finish_kernel, out_shape=tall, in_specs=[pl.BlockSpec(memo...  6.34 us
    pallas_call x1, Pallas kernels, on_device(): pl.pallas_call(inverse_kernel, out_shape=square, name='inverse')(gram)  5.62 us
    ppermute x2, starting transfers between devices, on_device(): send = lambda value: lax.ppermute(value, ('grp', 'leaf'), pairs)  5.42 us
  transfers between devices with their start and end apart: 22, of which 9 were waited for; matrix products, arithmetic and copies ran while one was open for 7% of the time, Pallas kernels for 24%

profile of v6, /device:TPU:0, one launch (start us, length us, event | category | flops | bytes accessed | tf_op | source)
XLA Modules:
  0.0 97.7 jit_solution(8449276757781804223)
XLA Ops:
  0.6 3.1 %collective-permute-start = (s32[1,128]{1,0:T(1,128)}, s32[1,128]{1,0:T(1,128)S(1)}, u32[]{:S(2)}, u32[]{:S(2)}) collective-permute-start(s32[1,128]{1,0:T(1,128)} %picked_ref.1), channel_id=1, source_target_pairs={{0,1},{1,0},{2,3},{3,2},{4,5},{5,4},{6,7},{7,6},{8,9},{9,8},{10,11... | collective-permute-start | bytes 1544 | tf_op jit(solution)/shard_map/ppermute | solution.py:206
  3.7 3.1 %product.1 = (f32[512,256]{1,0:T(8,128)}, f32[512,256]{1,0:T(8,128)}) custom-call(bf16[2048,1024]{1,0:T(8,128)(2,1)} %refs_0_.7, bf16[1024,512]{1,0:T(8,128)(2,1)} %refs_1_.7), custom_call_target="tpu_custom_call" | custom-call | tf_op jit(solution)/shard_map/product/pallas_call | solution.py:195
  7.4 1.6 %collective-permute-start.1 = (s32[2,128]{1,0:T(2,128)S(1)}, s32[2,128]{1,0:T(2,128)S(1)}, u32[]{:S(2)}, u32[]{:S(2)}) collective-permute-start(s32[2,128]{1,0:T(2,128)S(1)} %add_select_fusion.1), channel_id=1, source_target_pairs={{0,2},{1,3},{2,0},{3,1},{4,6},{5,7},{6,4},{7,5},{8,10},{9,11},{10,... | collective-permute-start | bytes 3080 | tf_op jit(solution)/shard_map/ppermute | solution.py:206
  9.1 2.0 %collective-permute-done.1 = s32[2,128]{1,0:T(2,128)S(1)} collective-permute-done((s32[2,128]{1,0:T(2,128)S(1)}, s32[2,128]{1,0:T(2,128)S(1)}, u32[]{:S(2)}, u32[]{:S(2)}) %collective-permute-start.1) | collective-permute-done | bytes 1056 | tf_op jit(solution)/shard_map/ppermute | solution.py:206
  11.1 2.6 %collective-permute-start.2 = (s32[4,128]{1,0:T(4,128)S(1)}, s32[4,128]{1,0:T(4,128)S(1)}, u32[]{:S(2)}, u32[]{:S(2)}) collective-permute-start(s32[4,128]{1,0:T(4,128)S(1)} %add_select_fusion), channel_id=1, source_target_pairs={{0,4},{1,5},{2,6},{3,7},{4,0},{5,1},{6,2},{7,3},{8,12},{9,13},{10,... | collective-permute-start | bytes 6152 | tf_op jit(solution)/shard_map/ppermute | solution.py:206
  13.7 1.9 %collective-permute-done.2 = s32[4,128]{1,0:T(4,128)S(1)} collective-permute-done((s32[4,128]{1,0:T(4,128)S(1)}, s32[4,128]{1,0:T(4,128)S(1)}, u32[]{:S(2)}, u32[]{:S(2)}) %collective-permute-start.2) | collective-permute-done | bytes 2080 | tf_op jit(solution)/shard_map/ppermute | solution.py:206
  16.1 3.9 %ordered.4 = (f32[256,256]{1,0:T(8,128)}, f32[256,256]{1,0:T(8,128)}, f32[256,256]{1,0:T(8,128)}, f32[256,256]{1,0:T(8,128)}) custom-call(bf16[2048,1024]{1,0:T(8,128)(2,1)} %refs_0_.7, bf16[1024,512]{1,0:T(8,128)(2,1)} %refs_1_.7, s32[8,1,128]{2,1,0:T(1,128)} %broadcast_select_fusion.13.refs_2_.picked_ref), custom_call_target="tpu_custom_call" | custom-call | tf_op jit(solution)/shard_map/ordered/pallas_call | solution.py:229
  20.1 1.4 %collective-permute-start.3 = (f32[256,256]{1,0:T(8,128)}, f32[256,256]{1,0:T(8,128)S(1)}, u32[]{:S(2)}, u32[]{:S(2)}) collective-permute-start(f32[256,256]{1,0:T(8,128)} %get-tuple-element.36), channel_id=1, source_target_pairs={{0,1},{1,0},{2,3},{3,2},{4,5},{5,4},{6,7},{7,6},{8,9},{9,8},{10,11... | collective-permute-start | bytes 786440 | tf_op jit(solution)/shard_map/ppermute | solution.py:167
  21.5 3.9 %ordered.5 = (f32[256,256]{1,0:T(8,128)}, f32[256,256]{1,0:T(8,128)}, f32[256,256]{1,0:T(8,128)}, f32[256,256]{1,0:T(8,128)}) custom-call(bf16[2048,1024]{1,0:T(8,128)(2,1)} %refs_0_.7, bf16[1024,512]{1,0:T(8,128)(2,1)} %refs_1_.7, s32[8,1,128]{2,1,0:T(1,128)} %broadcast_select_fusion.13.refs_2_.picked_ref), custom_call_target="tpu_custom_call" | custom-call | tf_op jit(solution)/shard_map/ordered/pallas_call | solution.py:229
  26.1 0.8 copy-done
  26.9 2.5 %split.1 = (f32[256,256]{1,0:T(8,128)}, f32[256,256]{1,0:T(8,128)}) custom-call(f32[512,256]{1,0:T(8,128)} %get-tuple-element.41.keep_ref, f32[512,256]{1,0:T(8,128)} %copy-done, s32[8,1,128]{2,1,0:T(1,128)} %broadcast_select_fusion.13.refs_2_.picked_ref), custom_call_target="tpu_custom_call" | custom-call | tf_op jit(solution)/shard_map/split/pallas_call | solution.py:245
  29.4 1.6 %collective-permute-start.8 = (f32[256,256]{1,0:T(8,128)}, f32[256,256]{1,0:T(8,128)S(1)}, u32[]{:S(2)}, u32[]{:S(2)}) collective-permute-start(f32[256,256]{1,0:T(8,128)} %get-tuple-element.46), channel_id=1, source_target_pairs={{0,2},{1,3},{2,0},{3,1},{4,6},{5,7},{6,4},{7,5},{8,10},{9,11},{10,... | collective-permute-start | bytes 786440 | tf_op jit(solution)/shard_map/ppermute | solution.py:171
  31.0 3.9 %ordered.3 = (f32[256,256]{1,0:T(8,128)}, f32[256,256]{1,0:T(8,128)}, f32[256,256]{1,0:T(8,128)}, f32[256,256]{1,0:T(8,128)}) custom-call(bf16[2048,1024]{1,0:T(8,128)(2,1)} %refs_0_.7, bf16[1024,512]{1,0:T(8,128)(2,1)} %refs_1_.7, s32[8,1,128]{2,1,0:T(1,128)} %broadcast_select_fusion.13.refs_2_.picked_ref), custom_call_target="tpu_custom_call" | custom-call | tf_op jit(solution)/shard_map/ordered/pallas_call | solution.py:229
  34.9 1.4 %collective-permute-start.10 = (f32[256,256]{1,0:T(8,128)}, f32[256,256]{1,0:T(8,128)S(1)}, u32[]{:S(2)}, u32[]{:S(2)}) collective-permute-start(f32[256,256]{1,0:T(8,128)} %get-tuple-element.49), channel_id=1, source_target_pairs={{0,1},{1,0},{2,3},{3,2},{4,5},{5,4},{6,7},{7,6},{8,9},{9,8},{10,11... | collective-permute-start | bytes 786440 | tf_op jit(solution)/shard_map/ppermute | solution.py:167
  37.5 2.3 %collective-permute-done.8 = f32[256,256]{1,0:T(8,128)S(1)} collective-permute-done((f32[256,256]{1,0:T(8,128)}, f32[256,256]{1,0:T(8,128)S(1)}, u32[]{:S(2)}, u32[]{:S(2)}) %collective-permute-start.8) | collective-permute-done | bytes 262176 | tf_op jit(solution)/shard_map/ppermute | solution.py:171
  39.8 2.8 %collective-permute-start.11 = (f32[256,256]{1,0:T(8,128)S(1)}, f32[256,256]{1,0:T(8,128)S(1)}, u32[]{:S(2)}, u32[]{:S(2)}) collective-permute-start(f32[256,256]{1,0:T(8,128)S(1)} %add_add_fusion.2), channel_id=1, source_target_pairs={{0,4},{1,5},{2,6},{3,7},{4,0},{5,1},{6,2},{7,3},{8,12},{9,13},{10,... | collective-permute-start | bytes 786440 | tf_op jit(solution)/shard_map/ppermute | solution.py:171
  42.7 0.8 fusion.26
  43.5 1.3 %collective-permute-start.5 = (f32[256,256]{1,0:T(8,128)S(1)}, f32[256,256]{1,0:T(8,128)S(1)}, u32[]{:S(2)}, u32[]{:S(2)}) collective-permute-start(f32[256,256]{1,0:T(8,128)S(1)} %copy-done.7), channel_id=1, source_target_pairs={{0,1},{1,0},{2,3},{3,2},{4,5},{5,4},{6,7},{7,6},{8,9},{9,8},{10,11... | collective-permute-start | bytes 786440 | tf_op jit(solution)/shard_map/ppermute | solution.py:167
  44.7 5.2 %collective-permute-done.17 = f32[256,256]{1,0:T(8,128)S(1)} collective-permute-done((f32[256,256]{1,0:T(8,128)}, f32[256,256]{1,0:T(8,128)S(1)}, u32[]{:S(2)}, u32[]{:S(2)}) %collective-permute-start.17) | collective-permute-done | bytes 262176 | tf_op jit(solution)/shard_map/ppermute | solution.py:167
  49.9 1.4 %collective-permute-start.4 = (f32[256,256]{1,0:T(8,128)}, f32[256,256]{1,0:T(8,128)S(1)}, u32[]{:S(2)}, u32[]{:S(2)}) collective-permute-start(f32[256,256]{1,0:T(8,128)} %get-tuple-element.37), channel_id=1, source_target_pairs={{0,1},{1,0},{2,3},{3,2},{4,5},{5,4},{6,7},{7,6},{8,9},{9,8},{10,11... | collective-permute-start | bytes 786440 | tf_op jit(solution)/shard_map/ppermute | solution.py:167
  52.0 1.0 %add_add_fusion.1 = f32[256,256]{1,0:T(8,128)S(1)} fusion(f32[256,256]{1,0:T(8,128)S(1)} %collective-permute-done.12, f32[256,256]{1,0:T(8,128)S(1)} %collective-permute-done.11, f32[256,256]{1,0:T(8,128)} %get-tuple-element.48, f32[256,256]{1,0:T(8,128)S(1)} %collective-permute-done.10), kind=kLoop, calls=%fused_computation.9 | loop fusion | flops 196608 | bytes 1310720 | tf_op jit(solution)/shard_map/add | solution.py:271
  54.5 2.9 %collective-permute-start.13 = (f32[128,256]{1,0:T(8,128)S(1)}, f32[128,256]{1,0:T(8,128)S(1)}, u32[]{:S(2)}, u32[]{:S(2)}) collective-permute-start(f32[128,256]{1,0:T(8,128)S(1)} %fusion.10), channel_id=1, source_target_pairs={{0,2},{1,3},{2,0},{3,1},{4,6},{5,7},{6,4},{7,5},{8,10},{9,11},{10,... | collective-permute-start | bytes 393224 | tf_op jit(solution)/shard_map/ppermute | solution.py:171
  59.0 3.0 %collective-permute-done.13 = f32[128,256]{1,0:T(8,128)S(1)} collective-permute-done((f32[128,256]{1,0:T(8,128)S(1)}, f32[128,256]{1,0:T(8,128)S(1)}, u32[]{:S(2)}, u32[]{:S(2)}) %collective-permute-start.13) | collective-permute-done | bytes 131104 | tf_op jit(solution)/shard_map/ppermute | solution.py:171
  62.2 5.3 %collective-permute-start.15 = (f32[128,256]{1,0:T(8,128)S(1)}, f32[128,256]{1,0:T(8,128)S(1)}, u32[]{:S(2)}, u32[]{:S(2)}) collective-permute-start(f32[128,256]{1,0:T(8,128)S(1)} %fusion.5), channel_id=1, source_target_pairs={{0,4},{1,5},{4,0},{5,1},{8,12},{9,13},{12,8},{13,9},{16,20},{17,21... | collective-permute-start | bytes 393224 | tf_op jit(solution)/shard_map/ppermute | solution.py:171
  68.1 4.9 %collective-permute-done.15 = f32[128,256]{1,0:T(8,128)S(1)} collective-permute-done((f32[128,256]{1,0:T(8,128)S(1)}, f32[128,256]{1,0:T(8,128)S(1)}, u32[]{:S(2)}, u32[]{:S(2)}) %collective-permute-start.15) | collective-permute-done | bytes 131104 | tf_op jit(solution)/shard_map/ppermute | solution.py:171
  73.3 1.9 %collective-permute-start.16 = (f32[128,256]{1,0:T(8,128)S(1)}, f32[128,256]{1,0:T(8,128)S(1)}, u32[]{:S(2)}, u32[]{:S(2)}) collective-permute-start(f32[128,256]{1,0:T(8,128)S(1)} %fusion.4), channel_id=1, source_target_pairs={{0,8},{1,9},{8,0},{9,1},{16,24},{17,25},{24,16},{25,17}} | collective-permute-start | bytes 393224 | tf_op jit(solution)/shard_map/ppermute | solution.py:319
  75.6 0.9 collective-permute-done.16
  76.8 3.5 %collective-permute-start.19 = (f32[128,256]{1,0:T(8,128)S(1)}, f32[128,256]{1,0:T(8,128)S(1)}, u32[]{:S(2)}, u32[]{:S(2)}) collective-permute-start(f32[128,256]{1,0:T(8,128)S(1)} %fusion.3), channel_id=1, source_target_pairs={{0,16},{1,17},{16,0},{17,1}} | collective-permute-start | bytes 393224 | tf_op jit(solution)/shard_map/ppermute | solution.py:319
  81.0 2.7 %collective-permute-done.19 = f32[128,256]{1,0:T(8,128)S(1)} collective-permute-done((f32[128,256]{1,0:T(8,128)S(1)}, f32[128,256]{1,0:T(8,128)S(1)}, u32[]{:S(2)}, u32[]{:S(2)}) %collective-permute-start.19) | collective-permute-done | bytes 131104 | tf_op jit(solution)/shard_map/ppermute | solution.py:319
  85.0 5.6 %inverse.1.inverse_ref = f32[128,128]{1,0:T(8,128)} custom-call(f32[128,128]{1,0:T(8,128)} %select_add_fusion.gram_ref), custom_call_target="tpu_custom_call" | custom-call | tf_op jit(solution)/shard_map/inverse/pallas_call | solution.py:362
  90.6 0.7 maximum_add_fusion.total_ref
  91.3 6.3 %finish.1 = (f32[256,128]{1,0:T(8,128)}, f32[256,128]{1,0:T(8,128)}) custom-call(s32[1]{0:T(128)} %bitcast.node_at, f32[384,128]{1,0:T(8,128)} %maximum_add_fusion.total_ref, f32[128,128]{1,0:T(8,128)} %inverse.1.inverse_ref, s32[1,128]{1,0:T(1,128)} %picked_ref.1, s32[31,128]{1,0:T(8,128)} %table_ref.1), custom_call_target="tpu_custom_call" | custom-call | tf_op jit(solution)/shard_map/finish/pallas_call | solution.py:365
  (68 shorter events, 10.3 us)
Async XLA Ops:
  0.6 6.8 %copy-start.6 = (s32[1,128]{1,0:T(1,128)S(1)}, s32[1,128]{1,0:T(1,128)}, u32[]{:S(2)}) copy-start(s32[1,128]{1,0:T(1,128)} %picked_ref.1) | copy-start | bytes 1540
  0.6 6.2 %collective-permute-start = (s32[1,128]{1,0:T(1,128)}, s32[1,128]{1,0:T(1,128)S(1)}, u32[]{:S(2)}, u32[]{:S(2)}) collective-permute-start(s32[1,128]{1,0:T(1,128)} %picked_ref.1), channel_id=1, source_target_pairs={{0,1},{1,0},{2,3},{3,2},{4,5},{5,4},{6,7},{7,6},{8,9},{9,8},{10,11... | collective-permute-start | bytes 1544 | tf_op jit(solution)/shard_map/ppermute | solution.py:206
  6.8 19.2 %collective-permute-start.6 = (f32[512,256]{1,0:T(8,128)}, f32[512,256]{1,0:T(8,128)S(1)}, u32[]{:S(2)}, u32[]{:S(2)}) collective-permute-start(f32[512,256]{1,0:T(8,128)} %get-tuple-element.42), channel_id=1, source_target_pairs={{0,1},{1,0},{2,3},{3,2},{4,5},{5,4},{6,7},{7,6},{8,9},{9,8},{10,11... | collective-permute-start | bytes 1572872 | tf_op jit(solution)/shard_map/ppermute | solution.py:167
  7.4 3.6 %collective-permute-start.1 = (s32[2,128]{1,0:T(2,128)S(1)}, s32[2,128]{1,0:T(2,128)S(1)}, u32[]{:S(2)}, u32[]{:S(2)}) collective-permute-start(s32[2,128]{1,0:T(2,128)S(1)} %add_select_fusion.1), channel_id=1, source_target_pairs={{0,2},{1,3},{2,0},{3,1},{4,6},{5,7},{6,4},{7,5},{8,10},{9,11},{10,... | collective-permute-start | bytes 3080 | tf_op jit(solution)/shard_map/ppermute | solution.py:206
  11.1 4.5 %collective-permute-start.2 = (s32[4,128]{1,0:T(4,128)S(1)}, s32[4,128]{1,0:T(4,128)S(1)}, u32[]{:S(2)}, u32[]{:S(2)}) collective-permute-start(s32[4,128]{1,0:T(4,128)S(1)} %add_select_fusion), channel_id=1, source_target_pairs={{0,4},{1,5},{2,6},{3,7},{4,0},{5,1},{6,2},{7,3},{8,12},{9,13},{10,... | collective-permute-start | bytes 6152 | tf_op jit(solution)/shard_map/ppermute | solution.py:206
  20.1 16.3 %collective-permute-start.3 = (f32[256,256]{1,0:T(8,128)}, f32[256,256]{1,0:T(8,128)S(1)}, u32[]{:S(2)}, u32[]{:S(2)}) collective-permute-start(f32[256,256]{1,0:T(8,128)} %get-tuple-element.36), channel_id=1, source_target_pairs={{0,1},{1,0},{2,3},{3,2},{4,5},{5,4},{6,7},{7,6},{8,9},{9,8},{10,11... | collective-permute-start | bytes 786440 | tf_op jit(solution)/shard_map/ppermute | solution.py:167
  25.4 11.6 %copy-start.3 = (f32[256,256]{1,0:T(8,128)S(1)}, f32[256,256]{1,0:T(8,128)}, u32[]{:S(2)}) copy-start(f32[256,256]{1,0:T(8,128)} %get-tuple-element.50) | copy-start | bytes 786436
  25.4 14.4 %copy-start.5 = (f32[256,256]{1,0:T(8,128)S(1)}, f32[256,256]{1,0:T(8,128)}, u32[]{:S(2)}) copy-start(f32[256,256]{1,0:T(8,128)} %get-tuple-element.44) | copy-start | bytes 786436
  25.4 18.1 %copy-start.7 = (f32[256,256]{1,0:T(8,128)S(1)}, f32[256,256]{1,0:T(8,128)}, u32[]{:S(2)}) copy-start(f32[256,256]{1,0:T(8,128)} %get-tuple-element.40) | copy-start | bytes 786436
  25.4 26.0 %copy-start.2 = (f32[256,256]{1,0:T(8,128)S(1)}, f32[256,256]{1,0:T(8,128)}, u32[]{:S(2)}) copy-start(f32[256,256]{1,0:T(8,128)} %get-tuple-element.53) | copy-start | bytes 786436
  25.4 12.1 %collective-permute-start.7 = (f32[256,256]{1,0:T(8,128)}, f32[256,256]{1,0:T(8,128)S(1)}, u32[]{:S(2)}, u32[]{:S(2)}) collective-permute-start(f32[256,256]{1,0:T(8,128)} %get-tuple-element.45), channel_id=1, source_target_pairs={{0,1},{1,0},{2,3},{3,2},{4,5},{5,4},{6,7},{7,6},{8,9},{9,8},{10,11... | collective-permute-start | bytes 786440 | tf_op jit(solution)/shard_map/ppermute | solution.py:167
  26.0 0.8 copy-start
  29.4 22.0 %copy-start.8 = (f32[256,256]{1,0:T(8,128)S(1)}, f32[256,256]{1,0:T(8,128)}, u32[]{:S(2)}) copy-start(f32[256,256]{1,0:T(8,128)} %get-tuple-element.47) | copy-start | bytes 786436
  29.4 28.5 %copy-start.4 = (f32[256,256]{1,0:T(8,128)S(1)}, f32[256,256]{1,0:T(8,128)}, u32[]{:S(2)}) copy-start(f32[256,256]{1,0:T(8,128)} %get-tuple-element.38) | copy-start | bytes 786436
  29.4 10.3 %collective-permute-start.8 = (f32[256,256]{1,0:T(8,128)}, f32[256,256]{1,0:T(8,128)S(1)}, u32[]{:S(2)}, u32[]{:S(2)}) collective-permute-start(f32[256,256]{1,0:T(8,128)} %get-tuple-element.46), channel_id=1, source_target_pairs={{0,2},{1,3},{2,0},{3,1},{4,6},{5,7},{6,4},{7,5},{8,10},{9,11},{10,... | collective-permute-start | bytes 786440 | tf_op jit(solution)/shard_map/ppermute | solution.py:171
  34.9 16.5 %collective-permute-start.10 = (f32[256,256]{1,0:T(8,128)}, f32[256,256]{1,0:T(8,128)S(1)}, u32[]{:S(2)}, u32[]{:S(2)}) collective-permute-start(f32[256,256]{1,0:T(8,128)} %get-tuple-element.49), channel_id=1, source_target_pairs={{0,1},{1,0},{2,3},{3,2},{4,5},{5,4},{6,7},{7,6},{8,9},{9,8},{10,11... | collective-permute-start | bytes 786440 | tf_op jit(solution)/shard_map/ppermute | solution.py:167
  36.4 13.6 %collective-permute-start.17 = (f32[256,256]{1,0:T(8,128)}, f32[256,256]{1,0:T(8,128)S(1)}, u32[]{:S(2)}, u32[]{:S(2)}) collective-permute-start(f32[256,256]{1,0:T(8,128)} %get-tuple-element.55), channel_id=1, source_target_pairs={{0,1},{1,0},{2,3},{3,2},{4,5},{5,4},{6,7},{7,6},{8,9},{9,8},{10,11... | collective-permute-start | bytes 786440 | tf_op jit(solution)/shard_map/ppermute | solution.py:167
  37.0 15.0 %collective-permute-start.12 = (f32[256,256]{1,0:T(8,128)S(1)}, f32[256,256]{1,0:T(8,128)S(1)}, u32[]{:S(2)}, u32[]{:S(2)}) collective-permute-start(f32[256,256]{1,0:T(8,128)S(1)} %add.114), channel_id=1, source_target_pairs={{0,2},{1,3},{2,0},{3,1},{4,6},{5,7},{6,4},{7,5},{8,10},{9,11},{10,... | collective-permute-start | bytes 786440 | tf_op jit(solution)/shard_map/ppermute | solution.py:171
  39.8 12.2 %collective-permute-start.11 = (f32[256,256]{1,0:T(8,128)S(1)}, f32[256,256]{1,0:T(8,128)S(1)}, u32[]{:S(2)}, u32[]{:S(2)}) collective-permute-start(f32[256,256]{1,0:T(8,128)S(1)} %add_add_fusion.2), channel_id=1, source_target_pairs={{0,4},{1,5},{2,6},{3,7},{4,0},{5,1},{6,2},{7,3},{8,12},{9,13},{10,... | collective-permute-start | bytes 786440 | tf_op jit(solution)/shard_map/ppermute | solution.py:171
  43.5 13.9 %collective-permute-start.5 = (f32[256,256]{1,0:T(8,128)S(1)}, f32[256,256]{1,0:T(8,128)S(1)}, u32[]{:S(2)}, u32[]{:S(2)}) collective-permute-start(f32[256,256]{1,0:T(8,128)S(1)} %copy-done.7), channel_id=1, source_target_pairs={{0,1},{1,0},{2,3},{3,2},{4,5},{5,4},{6,7},{7,6},{8,9},{9,8},{10,11... | collective-permute-start | bytes 786440 | tf_op jit(solution)/shard_map/ppermute | solution.py:167
  49.9 30.4 %collective-permute-start.4 = (f32[256,256]{1,0:T(8,128)}, f32[256,256]{1,0:T(8,128)S(1)}, u32[]{:S(2)}, u32[]{:S(2)}) collective-permute-start(f32[256,256]{1,0:T(8,128)} %get-tuple-element.37), channel_id=1, source_target_pairs={{0,1},{1,0},{2,3},{3,2},{4,5},{5,4},{6,7},{7,6},{8,9},{9,8},{10,11... | collective-permute-start | bytes 786440 | tf_op jit(solution)/shard_map/ppermute | solution.py:167
  51.4 29.0 %copy-start.1 = (f32[256,256]{1,0:T(8,128)S(1)}, f32[256,256]{1,0:T(8,128)}, u32[]{:S(2)}) copy-start(f32[256,256]{1,0:T(8,128)} %get-tuple-element.34) | copy-start | bytes 786436
  51.4 6.4 %collective-permute-start.9 = (f32[256,256]{1,0:T(8,128)S(1)}, f32[256,256]{1,0:T(8,128)S(1)}, u32[]{:S(2)}, u32[]{:S(2)}) collective-permute-start(f32[256,256]{1,0:T(8,128)S(1)} %copy-done.8), channel_id=1, source_target_pairs={{0,2},{1,3},{2,0},{3,1},{4,6},{5,7},{6,4},{7,5},{8,10},{9,11},{10,... | collective-permute-start | bytes 786440 | tf_op jit(solution)/shard_map/ppermute | solution.py:171
  53.6 4.7 %collective-permute-start.20 = (f32[128,128]{1,0:T(8,128)S(1)}, f32[128,128]{1,0:T(8,128)S(1)}, u32[]{:S(2)}, u32[]{:S(2)}) collective-permute-start(f32[128,128]{1,0:T(8,128)S(1)} %get-tuple-element.79), channel_id=1, source_target_pairs={{0,1},{1,0},{2,3},{3,2},{4,5},{5,4},{6,7},{7,6},{8,9},{9,8},{10,11... | collective-permute-start | bytes 196616 | tf_op jit(solution)/shard_map/ppermute | solution.py:167
  54.5 7.5 %collective-permute-start.13 = (f32[128,256]{1,0:T(8,128)S(1)}, f32[128,256]{1,0:T(8,128)S(1)}, u32[]{:S(2)}, u32[]{:S(2)}) collective-permute-start(f32[128,256]{1,0:T(8,128)S(1)} %fusion.10), channel_id=1, source_target_pairs={{0,2},{1,3},{2,0},{3,1},{4,6},{5,7},{6,4},{7,5},{8,10},{9,11},{10,... | collective-permute-start | bytes 393224 | tf_op jit(solution)/shard_map/ppermute | solution.py:171
  62.2 10.7 %collective-permute-start.15 = (f32[128,256]{1,0:T(8,128)S(1)}, f32[128,256]{1,0:T(8,128)S(1)}, u32[]{:S(2)}, u32[]{:S(2)}) collective-permute-start(f32[128,256]{1,0:T(8,128)S(1)} %fusion.5), channel_id=1, source_target_pairs={{0,4},{1,5},{4,0},{5,1},{8,12},{9,13},{12,8},{13,9},{16,20},{17,21... | collective-permute-start | bytes 393224 | tf_op jit(solution)/shard_map/ppermute | solution.py:171
  67.5 12.8 %collective-permute-start.14 = (f32[256,256]{1,0:T(8,128)S(1)}, f32[256,256]{1,0:T(8,128)S(1)}, u32[]{:S(2)}, u32[]{:S(2)}) collective-permute-start(f32[256,256]{1,0:T(8,128)S(1)} %add_add_fusion.3), channel_id=1, source_target_pairs={{0,4},{1,5},{2,6},{3,7},{4,0},{5,1},{6,2},{7,3},{8,12},{9,13},{10,... | collective-permute-start | bytes 786440 | tf_op jit(solution)/shard_map/ppermute | solution.py:171
  67.6 12.7 %collective-permute-start.18 = (f32[256,256]{1,0:T(8,128)S(1)}, f32[256,256]{1,0:T(8,128)S(1)}, u32[]{:S(2)}, u32[]{:S(2)}) collective-permute-start(f32[256,256]{1,0:T(8,128)S(1)} %add.120), channel_id=1, source_target_pairs={{0,2},{1,3},{2,0},{3,1},{4,6},{5,7},{6,4},{7,5},{8,10},{9,11},{10,... | collective-permute-start | bytes 786440 | tf_op jit(solution)/shard_map/ppermute | solution.py:171
  73.3 3.2 %collective-permute-start.16 = (f32[128,256]{1,0:T(8,128)S(1)}, f32[128,256]{1,0:T(8,128)S(1)}, u32[]{:S(2)}, u32[]{:S(2)}) collective-permute-start(f32[128,256]{1,0:T(8,128)S(1)} %fusion.4), channel_id=1, source_target_pairs={{0,8},{1,9},{8,0},{9,1},{16,24},{17,25},{24,16},{25,17}} | collective-permute-start | bytes 393224 | tf_op jit(solution)/shard_map/ppermute | solution.py:319
  76.8 6.9 %collective-permute-start.19 = (f32[128,256]{1,0:T(8,128)S(1)}, f32[128,256]{1,0:T(8,128)S(1)}, u32[]{:S(2)}, u32[]{:S(2)}) collective-permute-start(f32[128,256]{1,0:T(8,128)S(1)} %fusion.3), channel_id=1, source_target_pairs={{0,16},{1,17},{16,0},{17,1}} | collective-permute-start | bytes 393224 | tf_op jit(solution)/shard_map/ppermute | solution.py:319
  84.8 5.8 %collective-permute-start.21 = (f32[384,128]{1,0:T(8,128)S(1)}, f32[384,128]{1,0:T(8,128)S(1)}, u32[]{:S(2)}, u32[]{:S(2)}) collective-permute-start(f32[384,128]{1,0:T(8,128)S(1)} %pad_maximum_fusion.12), channel_id=1, source_target_pairs={{0,1},{1,0},{2,3},{3,2},{4,5},{5,4},{6,7},{7,6},{8,9},{9,8},{10,11... | collective-permute-start | bytes 589832 | tf_op jit(solution)/shard_map/ppermute | solution.py:167

commit v7 on v6

--- a/solution.py
+++ b/solution.py
@@ -94,9 +94,9 @@
 
 
 def sides(block, probes_ref, side, half):
-    away = probes_ref[:, pl.ds(pl.multiple_of((1 - side) * half, half), half)]
-    home = probes_ref[:, pl.ds(pl.multiple_of(side * half, half), half)]
-    return dot(block, away, precision=None), dot(block, home, precision=None)
+    both = dot(block, probes_ref[...], precision=None)
+    low, high = both[:, :half], both[:, half:]
+    return jnp.where(side == 0, high, low), jnp.where(side == 0, low, high)
 
 
 def plain_kernel(n_leaf, n_grp, mask, matrix_ref, probes_ref, send_ref, keep_ref):

time: 98.1 us -> 98.2 us (level)
  transfers between devices with their start and end apart: 22 -> 22, of which waited for: 9 -> 9; matrix products, arithmetic and copies ran while one was open for 7% -> 7% of each run, Pallas kernels for 24% -> 23%
where the time goes in v7:
time: 98.2 us; the launch traced here: 97.8 us
  starting transfers between devices  34.9 us (36%)
  Pallas kernels  29.3 us (30%)
  waiting for transfers between devices  23.3 us (24%)
  matrix products  4.34 us (4%)
  other arithmetic  3.31 us (3%)
  local copies, waits for them, and re-layouts  1.65 us (2%)
    ppermute x8, starting transfers between devices, along(): return lax.ppermute(value, 'leaf', pairs)  13.7 us
    pallas_call x3, Pallas kernels, ordered(): outs = outs(matrix, probes, tables)  11.7 us
    ppermute x8, waiting for transfers between devices, along(): return lax.ppermute(value, 'leaf', pairs)  10.7 us
    ppermute x9, starting transfers between devices, across(): return lax.ppermute(value, 'leaf', [(p, p ^ 1) for p in range(n_leaf)])  8.39 us
    ppermute x3, starting transfers between devices, on_device(): lax.ppermute(skeletons, 'leaf', [(p, p ^ 1 << bit) for p in range(n_leaf)])  7.29 us
    pallas_call x1, Pallas kernels, on_device(): pl.pallas_call(finish_kernel, out_shape=tall, in_specs=[pl.BlockSpec(memo...  6.34 us
    pallas_call x1, Pallas kernels, on_device(): pl.pallas_call(inverse_kernel, out_shape=square, name='inverse')(gram)  5.62 us
    ppermute x2, starting transfers between devices, on_device(): send = lambda value: lax.ppermute(value, ('grp', 'leaf'), pairs)  5.47 us
  transfers between devices with their start and end apart: 22, of which 9 were waited for; matrix products, arithmetic and copies ran while one was open for 7% of the time, Pallas kernels for 23%

profile of v7, /device:TPU:0, one launch (start us, length us, event | category | flops | bytes accessed | tf_op | source)
XLA Modules:
  0.0 97.8 jit_solution(16505551764013456838)
XLA Ops:
  0.6 3.1 %collective-permute-start = (s32[1,128]{1,0:T(1,128)}, s32[1,128]{1,0:T(1,128)S(1)}, u32[]{:S(2)}, u32[]{:S(2)}) collective-permute-start(s32[1,128]{1,0:T(1,128)} %picked_ref.1), channel_id=1, source_target_pairs={{0,1},{1,0},{2,3},{3,2},{4,5},{5,4},{6,7},{7,6},{8,9},{9,8},{10,11... | collective-permute-start | bytes 1544 | tf_op jit(solution)/shard_map/ppermute | solution.py:206
  3.7 3.1 %product.1 = (f32[512,256]{1,0:T(8,128)}, f32[512,256]{1,0:T(8,128)}) custom-call(bf16[2048,1024]{1,0:T(8,128)(2,1)} %refs_0_.7, bf16[1024,512]{1,0:T(8,128)(2,1)} %refs_1_.7), custom_call_target="tpu_custom_call" | custom-call | tf_op jit(solution)/shard_map/product/pallas_call | solution.py:195
  7.4 1.6 %collective-permute-start.1 = (s32[2,128]{1,0:T(2,128)S(1)}, s32[2,128]{1,0:T(2,128)S(1)}, u32[]{:S(2)}, u32[]{:S(2)}) collective-permute-start(s32[2,128]{1,0:T(2,128)S(1)} %add_select_fusion.1), channel_id=1, source_target_pairs={{0,2},{1,3},{2,0},{3,1},{4,6},{5,7},{6,4},{7,5},{8,10},{9,11},{10,... | collective-permute-start | bytes 3080 | tf_op jit(solution)/shard_map/ppermute | solution.py:206
  9.1 2.0 %collective-permute-done.1 = s32[2,128]{1,0:T(2,128)S(1)} collective-permute-done((s32[2,128]{1,0:T(2,128)S(1)}, s32[2,128]{1,0:T(2,128)S(1)}, u32[]{:S(2)}, u32[]{:S(2)}) %collective-permute-start.1) | collective-permute-done | bytes 1056 | tf_op jit(solution)/shard_map/ppermute | solution.py:206
  11.1 2.6 %collective-permute-start.2 = (s32[4,128]{1,0:T(4,128)S(1)}, s32[4,128]{1,0:T(4,128)S(1)}, u32[]{:S(2)}, u32[]{:S(2)}) collective-permute-start(s32[4,128]{1,0:T(4,128)S(1)} %add_select_fusion), channel_id=1, source_target_pairs={{0,4},{1,5},{2,6},{3,7},{4,0},{5,1},{6,2},{7,3},{8,12},{9,13},{10,... | collective-permute-start | bytes 6152 | tf_op jit(solution)/shard_map/ppermute | solution.py:206
  13.7 1.9 %collective-permute-done.2 = s32[4,128]{1,0:T(4,128)S(1)} collective-permute-done((s32[4,128]{1,0:T(4,128)S(1)}, s32[4,128]{1,0:T(4,128)S(1)}, u32[]{:S(2)}, u32[]{:S(2)}) %collective-permute-start.2) | collective-permute-done | bytes 2080 | tf_op jit(solution)/shard_map/ppermute | solution.py:206
  16.1 3.9 %ordered.4 = (f32[256,256]{1,0:T(8,128)}, f32[256,256]{1,0:T(8,128)}, f32[256,256]{1,0:T(8,128)}, f32[256,256]{1,0:T(8,128)}) custom-call(bf16[2048,1024]{1,0:T(8,128)(2,1)} %refs_0_.7, bf16[1024,512]{1,0:T(8,128)(2,1)} %refs_1_.7, s32[8,1,128]{2,1,0:T(1,128)} %broadcast_select_fusion.13.refs_2_.picked_ref), custom_call_target="tpu_custom_call" | custom-call | tf_op jit(solution)/shard_map/ordered/pallas_call | solution.py:229
  20.1 1.4 %collective-permute-start.3 = (f32[256,256]{1,0:T(8,128)}, f32[256,256]{1,0:T(8,128)S(1)}, u32[]{:S(2)}, u32[]{:S(2)}) collective-permute-start(f32[256,256]{1,0:T(8,128)} %get-tuple-element.36), channel_id=1, source_target_pairs={{0,1},{1,0},{2,3},{3,2},{4,5},{5,4},{6,7},{7,6},{8,9},{9,8},{10,11... | collective-permute-start | bytes 786440 | tf_op jit(solution)/shard_map/ppermute | solution.py:167
  21.5 3.9 %ordered.5 = (f32[256,256]{1,0:T(8,128)}, f32[256,256]{1,0:T(8,128)}, f32[256,256]{1,0:T(8,128)}, f32[256,256]{1,0:T(8,128)}) custom-call(bf16[2048,1024]{1,0:T(8,128)(2,1)} %refs_0_.7, bf16[1024,512]{1,0:T(8,128)(2,1)} %refs_1_.7, s32[8,1,128]{2,1,0:T(1,128)} %broadcast_select_fusion.13.refs_2_.picked_ref), custom_call_target="tpu_custom_call" | custom-call | tf_op jit(solution)/shard_map/ordered/pallas_call | solution.py:229
  26.1 0.8 copy-done
  26.9 2.5 %split.1 = (f32[256,256]{1,0:T(8,128)}, f32[256,256]{1,0:T(8,128)}) custom-call(f32[512,256]{1,0:T(8,128)} %get-tuple-element.41.keep_ref, f32[512,256]{1,0:T(8,128)} %copy-done, s32[8,1,128]{2,1,0:T(1,128)} %broadcast_select_fusion.13.refs_2_.picked_ref), custom_call_target="tpu_custom_call" | custom-call | tf_op jit(solution)/shard_map/split/pallas_call | solution.py:245
  29.4 1.6 %collective-permute-start.8 = (f32[256,256]{1,0:T(8,128)}, f32[256,256]{1,0:T(8,128)S(1)}, u32[]{:S(2)}, u32[]{:S(2)}) collective-permute-start(f32[256,256]{1,0:T(8,128)} %get-tuple-element.46), channel_id=1, source_target_pairs={{0,2},{1,3},{2,0},{3,1},{4,6},{5,7},{6,4},{7,5},{8,10},{9,11},{10,... | collective-permute-start | bytes 786440 | tf_op jit(solution)/shard_map/ppermute | solution.py:171
  31.1 3.9 %ordered.3 = (f32[256,256]{1,0:T(8,128)}, f32[256,256]{1,0:T(8,128)}, f32[256,256]{1,0:T(8,128)}, f32[256,256]{1,0:T(8,128)}) custom-call(bf16[2048,1024]{1,0:T(8,128)(2,1)} %refs_0_.7, bf16[1024,512]{1,0:T(8,128)(2,1)} %refs_1_.7, s32[8,1,128]{2,1,0:T(1,128)} %broadcast_select_fusion.13.refs_2_.picked_ref), custom_call_target="tpu_custom_call" | custom-call | tf_op jit(solution)/shard_map/ordered/pallas_call | solution.py:229
  35.0 1.4 %collective-permute-start.10 = (f32[256,256]{1,0:T(8,128)}, f32[256,256]{1,0:T(8,128)S(1)}, u32[]{:S(2)}, u32[]{:S(2)}) collective-permute-start(f32[256,256]{1,0:T(8,128)} %get-tuple-element.49), channel_id=1, source_target_pairs={{0,1},{1,0},{2,3},{3,2},{4,5},{5,4},{6,7},{7,6},{8,9},{9,8},{10,11... | collective-permute-start | bytes 786440 | tf_op jit(solution)/shard_map/ppermute | solution.py:167
  37.5 2.2 %collective-permute-done.8 = f32[256,256]{1,0:T(8,128)S(1)} collective-permute-done((f32[256,256]{1,0:T(8,128)}, f32[256,256]{1,0:T(8,128)S(1)}, u32[]{:S(2)}, u32[]{:S(2)}) %collective-permute-start.8) | collective-permute-done | bytes 262176 | tf_op jit(solution)/shard_map/ppermute | solution.py:171
  39.8 2.8 %collective-permute-start.11 = (f32[256,256]{1,0:T(8,128)S(1)}, f32[256,256]{1,0:T(8,128)S(1)}, u32[]{:S(2)}, u32[]{:S(2)}) collective-permute-start(f32[256,256]{1,0:T(8,128)S(1)} %add_add_fusion.2), channel_id=1, source_target_pairs={{0,4},{1,5},{2,6},{3,7},{4,0},{5,1},{6,2},{7,3},{8,12},{9,13},{10,... | collective-permute-start | bytes 786440 | tf_op jit(solution)/shard_map/ppermute | solution.py:171
  42.7 0.8 fusion.26
  43.5 1.3 %collective-permute-start.5 = (f32[256,256]{1,0:T(8,128)S(1)}, f32[256,256]{1,0:T(8,128)S(1)}, u32[]{:S(2)}, u32[]{:S(2)}) collective-permute-start(f32[256,256]{1,0:T(8,128)S(1)} %copy-done.7), channel_id=1, source_target_pairs={{0,1},{1,0},{2,3},{3,2},{4,5},{5,4},{6,7},{7,6},{8,9},{9,8},{10,11... | collective-permute-start | bytes 786440 | tf_op jit(solution)/shard_map/ppermute | solution.py:167
  44.8 5.2 %collective-permute-done.17 = f32[256,256]{1,0:T(8,128)S(1)} collective-permute-done((f32[256,256]{1,0:T(8,128)}, f32[256,256]{1,0:T(8,128)S(1)}, u32[]{:S(2)}, u32[]{:S(2)}) %collective-permute-start.17) | collective-permute-done | bytes 262176 | tf_op jit(solution)/shard_map/ppermute | solution.py:167
  50.0 1.4 %collective-permute-start.4 = (f32[256,256]{1,0:T(8,128)}, f32[256,256]{1,0:T(8,128)S(1)}, u32[]{:S(2)}, u32[]{:S(2)}) collective-permute-start(f32[256,256]{1,0:T(8,128)} %get-tuple-element.37), channel_id=1, source_target_pairs={{0,1},{1,0},{2,3},{3,2},{4,5},{5,4},{6,7},{7,6},{8,9},{9,8},{10,11... | collective-permute-start | bytes 786440 | tf_op jit(solution)/shard_map/ppermute | solution.py:167
  52.0 1.0 %add_add_fusion.1 = f32[256,256]{1,0:T(8,128)S(1)} fusion(f32[256,256]{1,0:T(8,128)S(1)} %collective-permute-done.12, f32[256,256]{1,0:T(8,128)S(1)} %collective-permute-done.11, f32[256,256]{1,0:T(8,128)} %get-tuple-element.48, f32[256,256]{1,0:T(8,128)S(1)} %collective-permute-done.10), kind=kLoop, calls=%fused_computation.9 | loop fusion | flops 196608 | bytes 1310720 | tf_op jit(solution)/shard_map/add | solution.py:271
  54.5 2.9 %collective-permute-start.13 = (f32[128,256]{1,0:T(8,128)S(1)}, f32[128,256]{1,0:T(8,128)S(1)}, u32[]{:S(2)}, u32[]{:S(2)}) collective-permute-start(f32[128,256]{1,0:T(8,128)S(1)} %fusion.10), channel_id=1, source_target_pairs={{0,2},{1,3},{2,0},{3,1},{4,6},{5,7},{6,4},{7,5},{8,10},{9,11},{10,... | collective-permute-start | bytes 393224 | tf_op jit(solution)/shard_map/ppermute | solution.py:171
  59.0 3.0 %collective-permute-done.13 = f32[128,256]{1,0:T(8,128)S(1)} collective-permute-done((f32[128,256]{1,0:T(8,128)S(1)}, f32[128,256]{1,0:T(8,128)S(1)}, u32[]{:S(2)}, u32[]{:S(2)}) %collective-permute-start.13) | collective-permute-done | bytes 131104 | tf_op jit(solution)/shard_map/ppermute | solution.py:171
  62.4 5.2 %collective-permute-start.15 = (f32[128,256]{1,0:T(8,128)S(1)}, f32[128,256]{1,0:T(8,128)S(1)}, u32[]{:S(2)}, u32[]{:S(2)}) collective-permute-start(f32[128,256]{1,0:T(8,128)S(1)} %fusion.5), channel_id=1, source_target_pairs={{0,4},{1,5},{4,0},{5,1},{8,12},{9,13},{12,8},{13,9},{16,20},{17,21... | collective-permute-start | bytes 393224 | tf_op jit(solution)/shard_map/ppermute | solution.py:171
  68.1 4.9 %collective-permute-done.15 = f32[128,256]{1,0:T(8,128)S(1)} collective-permute-done((f32[128,256]{1,0:T(8,128)S(1)}, f32[128,256]{1,0:T(8,128)S(1)}, u32[]{:S(2)}, u32[]{:S(2)}) %collective-permute-start.15) | collective-permute-done | bytes 131104 | tf_op jit(solution)/shard_map/ppermute | solution.py:171
  73.3 1.9 %collective-permute-start.16 = (f32[128,256]{1,0:T(8,128)S(1)}, f32[128,256]{1,0:T(8,128)S(1)}, u32[]{:S(2)}, u32[]{:S(2)}) collective-permute-start(f32[128,256]{1,0:T(8,128)S(1)} %fusion.4), channel_id=1, source_target_pairs={{0,8},{1,9},{8,0},{9,1},{16,24},{17,25},{24,16},{25,17}} | collective-permute-start | bytes 393224 | tf_op jit(solution)/shard_map/ppermute | solution.py:319
  75.6 0.9 collective-permute-done.16
  76.8 3.6 %collective-permute-start.19 = (f32[128,256]{1,0:T(8,128)S(1)}, f32[128,256]{1,0:T(8,128)S(1)}, u32[]{:S(2)}, u32[]{:S(2)}) collective-permute-start(f32[128,256]{1,0:T(8,128)S(1)} %fusion.3), channel_id=1, source_target_pairs={{0,16},{1,17},{16,0},{17,1}} | collective-permute-start | bytes 393224 | tf_op jit(solution)/shard_map/ppermute | solution.py:319
  81.1 2.6 %collective-permute-done.19 = f32[128,256]{1,0:T(8,128)S(1)} collective-permute-done((f32[128,256]{1,0:T(8,128)S(1)}, f32[128,256]{1,0:T(8,128)S(1)}, u32[]{:S(2)}, u32[]{:S(2)}) %collective-permute-start.19) | collective-permute-done | bytes 131104 | tf_op jit(solution)/shard_map/ppermute | solution.py:319
  85.1 5.6 %inverse.1.inverse_ref = f32[128,128]{1,0:T(8,128)} custom-call(f32[128,128]{1,0:T(8,128)} %select_add_fusion.gram_ref), custom_call_target="tpu_custom_call" | custom-call | tf_op jit(solution)/shard_map/inverse/pallas_call | solution.py:362
  90.7 0.7 maximum_add_fusion.total_ref
  91.4 6.3 %finish.1 = (f32[256,128]{1,0:T(8,128)}, f32[256,128]{1,0:T(8,128)}) custom-call(s32[1]{0:T(128)} %bitcast.node_at, f32[384,128]{1,0:T(8,128)} %maximum_add_fusion.total_ref, f32[128,128]{1,0:T(8,128)} %inverse.1.inverse_ref, s32[1,128]{1,0:T(1,128)} %picked_ref.1, s32[31,128]{1,0:T(8,128)} %table_ref.1), custom_call_target="tpu_custom_call" | custom-call | tf_op jit(solution)/shard_map/finish/pallas_call | solution.py:365
  (68 shorter events, 10.5 us)
Async XLA Ops:
  0.6 6.8 %copy-start.6 = (s32[1,128]{1,0:T(1,128)S(1)}, s32[1,128]{1,0:T(1,128)}, u32[]{:S(2)}) copy-start(s32[1,128]{1,0:T(1,128)} %picked_ref.1) | copy-start | bytes 1540
  0.6 6.2 %collective-permute-start = (s32[1,128]{1,0:T(1,128)}, s32[1,128]{1,0:T(1,128)S(1)}, u32[]{:S(2)}, u32[]{:S(2)}) collective-permute-start(s32[1,128]{1,0:T(1,128)} %picked_ref.1), channel_id=1, source_target_pairs={{0,1},{1,0},{2,3},{3,2},{4,5},{5,4},{6,7},{7,6},{8,9},{9,8},{10,11... | collective-permute-start | bytes 1544 | tf_op jit(solution)/shard_map/ppermute | solution.py:206
  6.8 19.3 %collective-permute-start.6 = (f32[512,256]{1,0:T(8,128)}, f32[512,256]{1,0:T(8,128)S(1)}, u32[]{:S(2)}, u32[]{:S(2)}) collective-permute-start(f32[512,256]{1,0:T(8,128)} %get-tuple-element.42), channel_id=1, source_target_pairs={{0,1},{1,0},{2,3},{3,2},{4,5},{5,4},{6,7},{7,6},{8,9},{9,8},{10,11... | collective-permute-start | bytes 1572872 | tf_op jit(solution)/shard_map/ppermute | solution.py:167
  7.4 3.6 %collective-permute-start.1 = (s32[2,128]{1,0:T(2,128)S(1)}, s32[2,128]{1,0:T(2,128)S(1)}, u32[]{:S(2)}, u32[]{:S(2)}) collective-permute-start(s32[2,128]{1,0:T(2,128)S(1)} %add_select_fusion.1), channel_id=1, source_target_pairs={{0,2},{1,3},{2,0},{3,1},{4,6},{5,7},{6,4},{7,5},{8,10},{9,11},{10,... | collective-permute-start | bytes 3080 | tf_op jit(solution)/shard_map/ppermute | solution.py:206
  11.1 4.5 %collective-permute-start.2 = (s32[4,128]{1,0:T(4,128)S(1)}, s32[4,128]{1,0:T(4,128)S(1)}, u32[]{:S(2)}, u32[]{:S(2)}) collective-permute-start(s32[4,128]{1,0:T(4,128)S(1)} %add_select_fusion), channel_id=1, source_target_pairs={{0,4},{1,5},{2,6},{3,7},{4,0},{5,1},{6,2},{7,3},{8,12},{9,13},{10,... | collective-permute-start | bytes 6152 | tf_op jit(solution)/shard_map/ppermute | solution.py:206
  20.1 16.3 %collective-permute-start.3 = (f32[256,256]{1,0:T(8,128)}, f32[256,256]{1,0:T(8,128)S(1)}, u32[]{:S(2)}, u32[]{:S(2)}) collective-permute-start(f32[256,256]{1,0:T(8,128)} %get-tuple-element.36), channel_id=1, source_target_pairs={{0,1},{1,0},{2,3},{3,2},{4,5},{5,4},{6,7},{7,6},{8,9},{9,8},{10,11... | collective-permute-start | bytes 786440 | tf_op jit(solution)/shard_map/ppermute | solution.py:167
  25.4 11.6 %copy-start.3 = (f32[256,256]{1,0:T(8,128)S(1)}, f32[256,256]{1,0:T(8,128)}, u32[]{:S(2)}) copy-start(f32[256,256]{1,0:T(8,128)} %get-tuple-element.50) | copy-start | bytes 786436
  25.4 14.4 %copy-start.5 = (f32[256,256]{1,0:T(8,128)S(1)}, f32[256,256]{1,0:T(8,128)}, u32[]{:S(2)}) copy-start(f32[256,256]{1,0:T(8,128)} %get-tuple-element.44) | copy-start | bytes 786436
  25.4 18.1 %copy-start.7 = (f32[256,256]{1,0:T(8,128)S(1)}, f32[256,256]{1,0:T(8,128)}, u32[]{:S(2)}) copy-start(f32[256,256]{1,0:T(8,128)} %get-tuple-element.40) | copy-start | bytes 786436
  25.4 26.0 %copy-start.2 = (f32[256,256]{1,0:T(8,128)S(1)}, f32[256,256]{1,0:T(8,128)}, u32[]{:S(2)}) copy-start(f32[256,256]{1,0:T(8,128)} %get-tuple-element.53) | copy-start | bytes 786436
  25.4 12.1 %collective-permute-start.7 = (f32[256,256]{1,0:T(8,128)}, f32[256,256]{1,0:T(8,128)S(1)}, u32[]{:S(2)}, u32[]{:S(2)}) collective-permute-start(f32[256,256]{1,0:T(8,128)} %get-tuple-element.45), channel_id=1, source_target_pairs={{0,1},{1,0},{2,3},{3,2},{4,5},{5,4},{6,7},{7,6},{8,9},{9,8},{10,11... | collective-permute-start | bytes 786440 | tf_op jit(solution)/shard_map/ppermute | solution.py:167
  26.1 0.8 copy-start
  29.4 22.1 %copy-start.8 = (f32[256,256]{1,0:T(8,128)S(1)}, f32[256,256]{1,0:T(8,128)}, u32[]{:S(2)}) copy-start(f32[256,256]{1,0:T(8,128)} %get-tuple-element.47) | copy-start | bytes 786436
  29.4 28.5 %copy-start.4 = (f32[256,256]{1,0:T(8,128)S(1)}, f32[256,256]{1,0:T(8,128)}, u32[]{:S(2)}) copy-start(f32[256,256]{1,0:T(8,128)} %get-tuple-element.38) | copy-start | bytes 786436
  29.4 10.3 %collective-permute-start.8 = (f32[256,256]{1,0:T(8,128)}, f32[256,256]{1,0:T(8,128)S(1)}, u32[]{:S(2)}, u32[]{:S(2)}) collective-permute-start(f32[256,256]{1,0:T(8,128)} %get-tuple-element.46), channel_id=1, source_target_pairs={{0,2},{1,3},{2,0},{3,1},{4,6},{5,7},{6,4},{7,5},{8,10},{9,11},{10,... | collective-permute-start | bytes 786440 | tf_op jit(solution)/shard_map/ppermute | solution.py:171
  35.0 16.5 %collective-permute-start.10 = (f32[256,256]{1,0:T(8,128)}, f32[256,256]{1,0:T(8,128)S(1)}, u32[]{:S(2)}, u32[]{:S(2)}) collective-permute-start(f32[256,256]{1,0:T(8,128)} %get-tuple-element.49), channel_id=1, source_target_pairs={{0,1},{1,0},{2,3},{3,2},{4,5},{5,4},{6,7},{7,6},{8,9},{9,8},{10,11... | collective-permute-start | bytes 786440 | tf_op jit(solution)/shard_map/ppermute | solution.py:167
  36.4 13.6 %collective-permute-start.17 = (f32[256,256]{1,0:T(8,128)}, f32[256,256]{1,0:T(8,128)S(1)}, u32[]{:S(2)}, u32[]{:S(2)}) collective-permute-start(f32[256,256]{1,0:T(8,128)} %get-tuple-element.55), channel_id=1, source_target_pairs={{0,1},{1,0},{2,3},{3,2},{4,5},{5,4},{6,7},{7,6},{8,9},{9,8},{10,11... | collective-permute-start | bytes 786440 | tf_op jit(solution)/shard_map/ppermute | solution.py:167
  37.0 14.9 %collective-permute-start.12 = (f32[256,256]{1,0:T(8,128)S(1)}, f32[256,256]{1,0:T(8,128)S(1)}, u32[]{:S(2)}, u32[]{:S(2)}) collective-permute-start(f32[256,256]{1,0:T(8,128)S(1)} %add.114), channel_id=1, source_target_pairs={{0,2},{1,3},{2,0},{3,1},{4,6},{5,7},{6,4},{7,5},{8,10},{9,11},{10,... | collective-permute-start | bytes 786440 | tf_op jit(solution)/shard_map/ppermute | solution.py:171
  39.8 12.2 %collective-permute-start.11 = (f32[256,256]{1,0:T(8,128)S(1)}, f32[256,256]{1,0:T(8,128)S(1)}, u32[]{:S(2)}, u32[]{:S(2)}) collective-permute-start(f32[256,256]{1,0:T(8,128)S(1)} %add_add_fusion.2), channel_id=1, source_target_pairs={{0,4},{1,5},{2,6},{3,7},{4,0},{5,1},{6,2},{7,3},{8,12},{9,13},{10,... | collective-permute-start | bytes 786440 | tf_op jit(solution)/shard_map/ppermute | solution.py:171
  43.5 13.9 %collective-permute-start.5 = (f32[256,256]{1,0:T(8,128)S(1)}, f32[256,256]{1,0:T(8,128)S(1)}, u32[]{:S(2)}, u32[]{:S(2)}) collective-permute-start(f32[256,256]{1,0:T(8,128)S(1)} %copy-done.7), channel_id=1, source_target_pairs={{0,1},{1,0},{2,3},{3,2},{4,5},{5,4},{6,7},{7,6},{8,9},{9,8},{10,11... | collective-permute-start | bytes 786440 | tf_op jit(solution)/shard_map/ppermute | solution.py:167
  50.0 30.4 %collective-permute-start.4 = (f32[256,256]{1,0:T(8,128)}, f32[256,256]{1,0:T(8,128)S(1)}, u32[]{:S(2)}, u32[]{:S(2)}) collective-permute-start(f32[256,256]{1,0:T(8,128)} %get-tuple-element.37), channel_id=1, source_target_pairs={{0,1},{1,0},{2,3},{3,2},{4,5},{5,4},{6,7},{7,6},{8,9},{9,8},{10,11... | collective-permute-start | bytes 786440 | tf_op jit(solution)/shard_map/ppermute | solution.py:167
  51.5 29.0 %copy-start.1 = (f32[256,256]{1,0:T(8,128)S(1)}, f32[256,256]{1,0:T(8,128)}, u32[]{:S(2)}) copy-start(f32[256,256]{1,0:T(8,128)} %get-tuple-element.34) | copy-start | bytes 786436
  51.5 6.4 %collective-permute-start.9 = (f32[256,256]{1,0:T(8,128)S(1)}, f32[256,256]{1,0:T(8,128)S(1)}, u32[]{:S(2)}, u32[]{:S(2)}) collective-permute-start(f32[256,256]{1,0:T(8,128)S(1)} %copy-done.8), channel_id=1, source_target_pairs={{0,2},{1,3},{2,0},{3,1},{4,6},{5,7},{6,4},{7,5},{8,10},{9,11},{10,... | collective-permute-start | bytes 786440 | tf_op jit(solution)/shard_map/ppermute | solution.py:171
  53.6 4.8 %collective-permute-start.20 = (f32[128,128]{1,0:T(8,128)S(1)}, f32[128,128]{1,0:T(8,128)S(1)}, u32[]{:S(2)}, u32[]{:S(2)}) collective-permute-start(f32[128,128]{1,0:T(8,128)S(1)} %get-tuple-element.79), channel_id=1, source_target_pairs={{0,1},{1,0},{2,3},{3,2},{4,5},{5,4},{6,7},{7,6},{8,9},{9,8},{10,11... | collective-permute-start | bytes 196616 | tf_op jit(solution)/shard_map/ppermute | solution.py:167
  54.5 7.6 %collective-permute-start.13 = (f32[128,256]{1,0:T(8,128)S(1)}, f32[128,256]{1,0:T(8,128)S(1)}, u32[]{:S(2)}, u32[]{:S(2)}) collective-permute-start(f32[128,256]{1,0:T(8,128)S(1)} %fusion.10), channel_id=1, source_target_pairs={{0,2},{1,3},{2,0},{3,1},{4,6},{5,7},{6,4},{7,5},{8,10},{9,11},{10,... | collective-permute-start | bytes 393224 | tf_op jit(solution)/shard_map/ppermute | solution.py:171
  62.4 10.6 %collective-permute-start.15 = (f32[128,256]{1,0:T(8,128)S(1)}, f32[128,256]{1,0:T(8,128)S(1)}, u32[]{:S(2)}, u32[]{:S(2)}) collective-permute-start(f32[128,256]{1,0:T(8,128)S(1)} %fusion.5), channel_id=1, source_target_pairs={{0,4},{1,5},{4,0},{5,1},{8,12},{9,13},{12,8},{13,9},{16,20},{17,21... | collective-permute-start | bytes 393224 | tf_op jit(solution)/shard_map/ppermute | solution.py:171
  67.6 12.8 %collective-permute-start.14 = (f32[256,256]{1,0:T(8,128)S(1)}, f32[256,256]{1,0:T(8,128)S(1)}, u32[]{:S(2)}, u32[]{:S(2)}) collective-permute-start(f32[256,256]{1,0:T(8,128)S(1)} %add_add_fusion.3), channel_id=1, source_target_pairs={{0,4},{1,5},{2,6},{3,7},{4,0},{5,1},{6,2},{7,3},{8,12},{9,13},{10,... | collective-permute-start | bytes 786440 | tf_op jit(solution)/shard_map/ppermute | solution.py:171
  67.7 12.7 %collective-permute-start.18 = (f32[256,256]{1,0:T(8,128)S(1)}, f32[256,256]{1,0:T(8,128)S(1)}, u32[]{:S(2)}, u32[]{:S(2)}) collective-permute-start(f32[256,256]{1,0:T(8,128)S(1)} %add.120), channel_id=1, source_target_pairs={{0,2},{1,3},{2,0},{3,1},{4,6},{5,7},{6,4},{7,5},{8,10},{9,11},{10,... | collective-permute-start | bytes 786440 | tf_op jit(solution)/shard_map/ppermute | solution.py:171
  73.3 3.2 %collective-permute-start.16 = (f32[128,256]{1,0:T(8,128)S(1)}, f32[128,256]{1,0:T(8,128)S(1)}, u32[]{:S(2)}, u32[]{:S(2)}) collective-permute-start(f32[128,256]{1,0:T(8,128)S(1)} %fusion.4), channel_id=1, source_target_pairs={{0,8},{1,9},{8,0},{9,1},{16,24},{17,25},{24,16},{25,17}} | collective-permute-start | bytes 393224 | tf_op jit(solution)/shard_map/ppermute | solution.py:319
  76.8 6.9 %collective-permute-start.19 = (f32[128,256]{1,0:T(8,128)S(1)}, f32[128,256]{1,0:T(8,128)S(1)}, u32[]{:S(2)}, u32[]{:S(2)}) collective-permute-start(f32[128,256]{1,0:T(8,128)S(1)} %fusion.3), channel_id=1, source_target_pairs={{0,16},{1,17},{16,0},{17,1}} | collective-permute-start | bytes 393224 | tf_op jit(solution)/shard_map/ppermute | solution.py:319
  84.8 5.9 %collective-permute-start.21 = (f32[384,128]{1,0:T(8,128)S(1)}, f32[384,128]{1,0:T(8,128)S(1)}, u32[]{:S(2)}, u32[]{:S(2)}) collective-permute-start(f32[384,128]{1,0:T(8,128)S(1)} %pad_maximum_fusion.12), channel_id=1, source_target_pairs={{0,1},{1,0},{2,3},{3,2},{4,5},{5,4},{6,7},{7,6},{8,9},{9,8},{10,11... | collective-permute-start | bytes 589832 | tf_op jit(solution)/shard_map/ppermute | solution.py:167
